TPU v7x, 512 devices: a whole 4x8x8 slice. The times are simulated.
512 devices in a mesh: ch: 64 (over z_hi, y, x), ta: 8 (over z_lo, core).
Axes of the slice: x: 4, y: 8, z: 8 (z_hi: 2, z_lo: 4; z = z_hi * 4 + z_lo), core: 2. Of those that a mesh axis runs over, the one named last changes fastest.
Arguments:
- raw_strain: float32 [8192, 12288], P('ch', 'ta'), may hold values from -6 to 6
- band_index: int32 [8192], P('ch'), may hold values from 0 to 3
- filter_taps: float32 [4, 33], replicated, may hold values from -1 to 1
Outputs:
- correlation: float32 [2, 65, 8192, 128], P(None, None, ('ch', 'ta'))
All inputs are finite; a program needn't handle non-finite values.
Results may differ from a plain program's by a relative error of at most 0.0037.
Values may be sent and summed in bfloat16 or wider, within the bound.
No kernel may reach another device: no remote copies, remote signals or barrier semaphores. Data moves between devices by JAX's collectives and lax.ppermute only.
A program may use at most 64 MiB of HBM per device.

v0:
```python
import math

import jax
import jax.numpy as jnp
from jax import lax
from jax.sharding import PartitionSpec as P

HF = 16
TAPS = 33
NBANDS = 4
LAGH = 32
LAGS = 65
ROUNDS = 2


def padded_2(block, sides, width):
    for axis, dim in sides:
        count = lax.axis_size(axis)
        forward = [(i, i + 1) for i in range(count - 1)]
        backward = [(target, source) for source, target in forward]
        low = lax.ppermute(
            lax.slice_in_dim(block, block.shape[dim] - width, None, axis=dim), axis, forward
        )
        high = lax.ppermute(lax.slice_in_dim(block, 0, width, axis=dim), axis, backward)
        block = jnp.concatenate([low, block, high], axis=dim)
    return block


def passed_along(block, axis, distance):
    devices = range(lax.axis_size(axis))
    route = [((i - distance) % len(devices), i) for i in devices]
    return lax.ppermute(block, axis, route)


def correlate(own_rows, partner, scale):
    row_count = own_rows.shape[0]
    length = own_rows.shape[1]
    padded = jnp.pad(own_rows, ((0, 0), (LAGH, LAGH)))

    def lag_block(carry, block_id):
        pieces = []
        for inner in range(5):
            start = 2 * LAGH - (block_id * 5 + inner)
            pieces.append(lax.dynamic_slice_in_dim(padded, start, length, 1))
        stacked = jnp.concatenate(pieces, axis=0)
        result = lax.dot_general(
            stacked, partner, (((1,), (1,)), ((), ())), preferred_element_type=jnp.float32
        )
        return (carry, result.reshape(5, row_count, partner.shape[0]) * scale)

    unused, lagged = lax.scan(lag_block, 0, jnp.arange(LAGS // 5, dtype=jnp.int32))
    return lagged.reshape(LAGS, row_count, partner.shape[0])


def on_device(raw_strain, band_index, filter_taps):
    block_size = raw_strain.shape[0]
    local_len = raw_strain.shape[1]
    time_groups = lax.axis_size("ta")
    channel_groups = lax.axis_size("ch")
    whole_len = local_len * time_groups
    onehot = (band_index[:, None] == jnp.arange(NBANDS, dtype=jnp.int32)[None, :]).astype(
        jnp.float32
    )
    coeffs = jnp.dot(
        onehot, filter_taps, precision=lax.Precision.HIGHEST, preferred_element_type=jnp.float32
    )
    extended = padded_2(raw_strain, (("ta", 1),), HF)
    filtered = jnp.zeros_like(raw_strain)
    for step in range(TAPS):
        filtered = filtered + coeffs[:, step : step + 1] * extended[:, step : step + local_len]
    magnitude = padded_2(jnp.abs(filtered), (("ta", 1),), local_len)
    cumulative = jnp.concatenate(
        [jnp.zeros((block_size, 1), jnp.float32), jnp.cumsum(magnitude, axis=1)], axis=1
    )
    window_sum = cumulative[:, 2 * local_len + 1 : 3 * local_len + 1] - cumulative[:, 0:local_len]
    global_time = lax.axis_index("ta") * local_len + jnp.arange(local_len, dtype=jnp.int32)
    upper = jnp.minimum(global_time + local_len, whole_len - 1) + 1
    lower = jnp.maximum(global_time - local_len, 0)
    counted = (upper - lower).astype(jnp.float32)
    level = window_sum / counted[None, :]
    normalized = (filtered / (level + 1e-06)).astype(jnp.bfloat16)
    row_count = block_size // time_groups
    scale = 1.0 / math.sqrt(whole_len)
    results = []
    own_whole = lax.all_gather(normalized, "ta", axis=1, tiled=True)
    own_part = lax.dynamic_slice_in_dim(own_whole, lax.axis_index("ta") * row_count, row_count, 0)
    for round_id in range(ROUNDS):
        offset = (round_id + 1) * (channel_groups // 4)
        partner = passed_along(own_whole, "ch", offset)
        results.append(correlate(own_part, partner, scale))
    return jnp.stack(results)


def solution(mesh):
    placed = (P("ch", "ta"), P("ch"), P())
    return jax.shard_map(
        on_device,
        mesh=mesh,
        in_specs=placed,
        out_specs=P(None, None, ("ch", "ta"), None),
        check_vma=False,
    )
```

profile of v0, /device:TPU:18, one launch (start us, length us, event | category | flops | bytes accessed | tf_op | source)
XLA Modules:
  0.0 584.2 jit_solution(14284387562218362970)
XLA Ops:
  12.0 2.9 collective-permute-done.1
  14.9 5.4 fusion.103
  20.3 4.3 collective-permute-start.2
  32.8 60.4 %all-gather.2.cloned.1.call-done = bf16[128,12288]{0,1:T(8,128)(2,1)} async-done(((bf16[128,1536]{0,1:T(8,128)(2,1)}), bf16[128,12288]{0,1:T(8,128)(2,1)}) %all-gather.2.cloned.1.call-update) | async-done | bytes 3145744 | tf_op jit(solution)/shard_map/all_gather | solution.py:85
  93.2 5.6 collective-permute-start.4
  104.5 5.4 collective-permute-start.5
  109.9 215.6 %collective-permute-done.4 = bf16[128,12288]{0,1:T(8,128)(2,1)} collective-permute-done((bf16[128,12288]{0,1:T(8,128)(2,1)}, bf16[128,12288]{0,1:T(8,128)(2,1)}, u32[]{:S(2)}, u32[]{:S(2)}) %collective-permute-start.4) | collective-permute-done | bytes 3145760 | tf_op jit(solution)/shard_map/ppermute | solution.py:32
  325.5 3.2 copy.13
  329.6 121.2 %while.26 = (s32[]{:T(128)}, f32[13,5,16,128]{3,2,1,0:T(8,128)}, s32[13]{0:T(128)S(1)}, bf16[16,12352]{1,0:T(8,128)(2,1)S(1)}, bf16[128,12288]{1,0:T(8,128)(2,1)...) while((s32[]{:T(128)}, f32[13,5,16,128]{3,2,1,0:T(8,128)}, ...), condition=%wide.region_3.4_spmd, body=%wide.region_2.3_spmd.sunk | while | flops 251668512 | bytes 9167815 | solution.py:51
  363.5 2.7 convolution_multiply_fusion.4
  372.8 2.7 convolution_multiply_fusion.4
  400.8 2.7 convolution_multiply_fusion.4
  410.1 2.7 convolution_multiply_fusion.4
  419.4 2.7 convolution_multiply_fusion.4
  428.7 2.7 convolution_multiply_fusion.4
  450.8 3.2 copy.15
  454.8 120.3 %while.27 = (s32[]{:T(128)}, f32[13,5,16,128]{3,2,1,0:T(8,128)}, s32[13]{0:T(128)S(1)}, bf16[16,12352]{1,0:T(8,128)(2,1)S(1)}, bf16[128,12288]{1,0:T(8,128)(2,1)...) while((s32[]{:T(128)}, f32[13,5,16,128]{3,2,1,0:T(8,128)}, ...), condition=%wide.region_5.6_spmd, body=%wide.region_4.5_spmd.sunk | while | flops 251668512 | bytes 9167815 | solution.py:51
  469.9 2.7 convolution_multiply_fusion.5
  479.2 2.7 convolution_multiply_fusion.5
  488.4 2.7 convolution_multiply_fusion.5
  497.7 2.7 convolution_multiply_fusion.5
  534.7 2.7 convolution_multiply_fusion.5
  543.9 2.7 convolution_multiply_fusion.5
  553.2 2.7 convolution_multiply_fusion.5
  (229 shorter events, 211.5 us)
Async XLA Ops:
  6.5 4.5 copy-start
  6.5 86.7 %all-gather.2.cloned.1.call-start = ((), (), s32[]{:S(2)}) async-start(), calls=%async_computation | async-start | bytes 3538944 | tf_op jit(solution)/shard_map/all_gather | solution.py:85
  8.0 4.0 collective-permute-start
  9.7 5.2 collective-permute-start.1
  20.3 6.2 %collective-permute-start.2 = (f32[128,1536]{0,1:T(8,128)S(1)}, f32[128,1536]{0,1:T(8,128)S(1)}, u32[]{:S(2)}, u32[]{:S(2)}) collective-permute-start(f32[128,1536]{0,1:T(8,128)S(1)} %get-tuple-element.205), channel_id=1, source_target_pairs={{0,1},{1,2},{2,3},{3,4},{4,5},{5,6},{6,7},{8,9},{9,10},{10,11},{11... | collective-permute-start | bytes 2359304 | tf_op jit(solution)/shard_map/ppermute | solution.py:21
  24.6 4.2 collective-permute-start.3
  30.6 1.1 copy-start.1
  93.2 232.3 %collective-permute-start.4 = (bf16[128,12288]{0,1:T(8,128)(2,1)}, bf16[128,12288]{0,1:T(8,128)(2,1)}, u32[]{:S(2)}, u32[]{:S(2)}) collective-permute-start(bf16[128,12288]{0,1:T(8,128)(2,1)} %all-gather.2.cloned.1.call-done), channel_id=1, source_target_pairs={{384,0},{392,8},{400,16},{408,24},{416,32},{424,40},{432,48},{440,... | collective-permute-start | bytes 9437192 | tf_op jit(solution)/shard_map/ppermute | solution.py:32
  104.5 346.2 %collective-permute-start.5 = (bf16[128,12288]{0,1:T(8,128)(2,1)}, bf16[128,12288]{0,1:T(8,128)(2,1)}, u32[]{:S(2)}, u32[]{:S(2)}) collective-permute-start(bf16[128,12288]{0,1:T(8,128)(2,1)} %all-gather.2.cloned.1.call-done), channel_id=1, source_target_pairs={{256,0},{264,8},{272,16},{280,24},{288,32},{296,40},{304,48},{312,... | collective-permute-start | bytes 9437192 | tf_op jit(solution)/shard_map/ppermute | solution.py:32
Sparse Core Ops, SparseCore 0:
  32.9 60.2 all-gather.1
where the time goes:
time: 586 us; the launch traced here: 584 us
  waiting for transfers between devices  282 us (48%)
  local copies, waits for them, and re-layouts  169 us (29%)
  matrix products  72.2 us (12%)
  starting transfers between devices  19.6 us (3%)
  loops' own time  17.5 us (3%)
  between operations  13.6 us (2%)
  other arithmetic  10.4 us (2%)
    ppermute x2, waiting for transfers between devices, passed_along(): return lax.ppermute(block, axis, route)  216 us
    while x104, local copies, waits for them, and re-layouts  96.8 us
    dot_general x26, matrix products, lag_block(): lax.dot_general(stacked, partner, (((1,), (1,)), ((), ())), preferred_ele...  71.3 us
    all_gather x1, waiting for transfers between devices, on_device(): own_whole = lax.all_gather(normalized, 'ta', axis=1, tiled=True)  60.4 us
    concatenate x26, local copies, waits for them, and re-layouts, lag_block(): stacked = jnp.concatenate(pieces, axis=0)  24.6 us
    another operation x2, loops' own time, correlate(): lax.scan(lag_block, 0, jnp.arange(LAGS // 5, dtype=jnp.int32))  17.5 us
    dynamic_update_slice x26, local copies, waits for them, and re-layouts, correlate(): lax.scan(lag_block, 0, jnp.arange(LAGS // 5, dtype=jnp.int32))  16.2 us
    dynamic_slice x26, local copies, waits for them, and re-layouts, correlate(): lax.scan(lag_block, 0, jnp.arange(LAGS // 5, dtype=jnp.int32))  15.1 us
  transfers between devices with their start and end apart: 7, of which 5 were waited for; matrix products, arithmetic and copies ran while one was open for 21% of the time, Pallas kernels for 0%

commit v1 on v0

v1 whole, which is shorter than its diff:
```python
import functools
import math

import jax
import jax.numpy as jnp
from jax import lax
from jax.experimental import pallas as pl
from jax.experimental.pallas import tpu as pltpu
from jax.sharding import PartitionSpec as P

HF = 16
TAPS = 33
NBANDS = 4
LAGH = 32
LAGS = 65
ROUNDS = 2
EDGE = 128
GROUP = 13
AXES = ("ch", "ta")


class Layout:
    def __init__(self):
        self.blocks = lax.axis_size("ch")
        self.slices = lax.axis_size("ta")
        self.cols = self.blocks // 2
        self.depth = self.slices // 2
        self.ring = 2 * self.depth

    def index(self, pos, col, core):
        zh, zl = divmod(pos % self.ring, self.depth)
        return (zh * self.cols + col) * self.slices + zl * 2 + core

    def every(self):
        for pos in range(self.ring):
            for col in range(self.cols):
                for core in range(2):
                    yield pos, col, core

    def from_ring(self, step):
        return [(self.index(p + step, c, k), self.index(p, c, k)) for p, c, k in self.every()]

    def swap_columns(self):
        return [
            (self.index(p, (c + self.cols // 2) % self.cols, k), self.index(p, c, k))
            for p, c, k in self.every()
        ]

    def swap_cores(self):
        return [(self.index(p, c, 1 - k), self.index(p, c, k)) for p, c, k in self.every()]


def to_neighbours(low_part, high_part):
    count = lax.axis_size("ta")
    forward = [(i, i + 1) for i in range(count - 1)]
    backward = [(i + 1, i) for i in range(count - 1)]
    from_low = lax.ppermute(high_part, "ta", forward)
    from_high = lax.ppermute(low_part, "ta", backward)
    return from_low, from_high


def normalize(raw, band_index, filter_taps):
    length = raw.shape[1]
    time_groups = lax.axis_size("ta")
    whole_len = length * time_groups
    onehot = (band_index[:, None] == jnp.arange(NBANDS, dtype=jnp.int32)[None, :]).astype(
        jnp.float32
    )
    coeffs = jnp.dot(
        onehot, filter_taps, precision=lax.Precision.HIGHEST, preferred_element_type=jnp.float32
    )
    low, high = to_neighbours(raw[:, :HF], raw[:, length - HF :])
    extended = jnp.concatenate([low, raw, high], axis=1)
    filtered = jnp.zeros_like(raw)
    for step in range(TAPS):
        filtered = filtered + coeffs[:, step : step + 1] * extended[:, step : step + length]
    magnitude = jnp.abs(filtered)
    prefix = jnp.cumsum(magnitude, axis=1)
    total = prefix[:, length - 1 :]
    suffix = total - prefix + magnitude
    before, after = to_neighbours(prefix, suffix)
    window_sum = before + total + after
    global_time = lax.axis_index("ta") * length + jnp.arange(length, dtype=jnp.int32)
    upper = jnp.minimum(global_time + length, whole_len - 1) + 1
    lower = jnp.maximum(global_time - length, 0)
    counted = (upper - lower).astype(jnp.float32)
    level = window_sum / counted[None, :]
    return (filtered / (level + 1e-06)).astype(jnp.bfloat16)


def gather_ring(layout, piece):
    ring = layout.ring
    slots = {0: (piece,)}
    up = down = piece
    for step in range(1, ring // 2):
        up = lax.ppermute(up, AXES, layout.from_ring(1))
        down = lax.ppermute(down, AXES, layout.from_ring(-1))
        slots[step] = (up,)
        slots[ring - step] = (down,)
    half = piece.shape[0] // 2
    slots[ring // 2] = (
        lax.ppermute(up[:half], AXES, layout.from_ring(1)),
        lax.ppermute(down[half:], AXES, layout.from_ring(-1)),
    )
    return slots


def lagged_kernel(layout, rows, length, scale, *refs):
    place_ref, edge_ref = refs[:2]
    ring, depth = layout.ring, layout.depth
    flat = list(refs[2 : 2 + 2 * (ring + 1)])
    own_slots, swap_slots = {}, {}
    for slots in (own_slots, swap_slots):
        for d in range(ring):
            count = 2 if d == ring // 2 else 1
            slots[d] = [flat.pop(0) for _ in range(count)]
    mine_ref, other_ref, own_buf, part_buf, acc, own_sem, near_sem, far_sem = refs[
        2 + 2 * (ring + 1) :
    ]
    zl, core, same = place_ref[0], place_ref[1], place_ref[2]
    channels = part_buf.shape[1] // 2

    def copies(slots, wanted, first, dst, sem):
        out = []
        for d in range(ring):
            todo, row = [], first
            for ref in slots[d]:
                n = ref.shape[0]
                todo.append(pltpu.make_async_copy(ref, dst.at[pl.ds(row, n)], sem))
                row += n
            out.append((d, todo))
        return out

    def slice_at(j):
        return lax.rem(zl + 1 + j, depth)

    for j in range(depth):
        k = slice_at(j)
        own_d = lax.rem(k - zl + ring, ring)
        far_d = lax.rem(k - zl + ring // 2 + ring, ring)
        near_d = lax.rem(k - zl + ring + (1 - same) * (ring // 2), ring)
        first = pl.multiple_of(zl * rows, rows)
        for d in range(ring):
            if d == ring // 2:
                continue

            @pl.when(own_d == d)
            def _():
                pltpu.make_async_copy(
                    own_slots[d][0].at[pl.ds(first, rows)],
                    own_buf.at[j, :, pl.ds(EDGE, length)],
                    own_sem.at[j],
                ).start()

        for slots, wanted, row, sem in (
            (swap_slots, near_d, 0, near_sem),
            (own_slots, far_d, channels, far_sem),
        ):
            for d, todo in copies(slots, wanted, row, part_buf.at[j], sem.at[j]):

                @pl.when(wanted == d)
                def _():
                    for copy in todo:
                        copy.start()

    def body(j, carry):
        k = slice_at(j)
        left, right = k - 1 + core, k + core
        left_ok = (left >= 0).astype(jnp.bfloat16)
        right_ok = (right < depth).astype(jnp.bfloat16)
        left_at = jnp.clip(left - zl + depth - 1, 0, 2 * depth - 2)
        right_at = jnp.clip(right - zl + depth - 1, 0, 2 * depth - 2)
        own_buf[j, :, :EDGE] = edge_ref[left_at, 1] * left_ok
        own_buf[j, :, EDGE + length :] = edge_ref[right_at, 0] * right_ok
        pltpu.make_async_copy(
            own_buf.at[j, :, pl.ds(EDGE, length)],
            own_buf.at[j, :, pl.ds(EDGE, length)],
            own_sem.at[j],
        ).wait()
        half = part_buf.at[j, pl.ds(0, channels)]
        pltpu.make_async_copy(half, half, near_sem.at[j]).wait()
        pltpu.make_async_copy(half, half, far_sem.at[j]).wait()
        partner = part_buf[j]
        for group in range(LAGS // GROUP):
            stacked = jnp.concatenate(
                [
                    own_buf[j, :, EDGE + LAGH - lag : EDGE + LAGH - lag + length]
                    for lag in range(group * GROUP, (group + 1) * GROUP)
                ],
                axis=0,
            )
            block = pl.ds(group * GROUP * rows, GROUP * rows)
            product = lax.dot_general(
                stacked, partner, (((1,), (1,)), ((), ())), preferred_element_type=jnp.float32
            )
            acc[block] = jnp.where(j == 0, product, acc[block] + product)
        return carry

    acc[...] = jnp.zeros_like(acc)
    lax.fori_loop(0, depth, body, 0)
    half_rows = rows // 2

    def spread(lag, carry):
        base = lag * rows
        for ref, which in ((mine_ref, core), (other_ref, 1 - core)):
            start = pl.multiple_of(base + which * half_rows, half_rows)
            for r in range(ROUNDS):
                ref[r, lag] = (
                    acc[pl.ds(start, half_rows), r * channels : (r + 1) * channels] * scale
                )
        return carry

    lax.fori_loop(0, LAGS, spread, 0)


def lagged(layout, own, swapped, edges, place, channels, length, scale):
    rows = channels // layout.depth
    depth = layout.depth
    operands = [ref for slots in (own, swapped) for d in range(layout.ring) for ref in slots[d]]
    shape = jax.ShapeDtypeStruct((ROUNDS, LAGS, rows // 2, channels), jnp.float32)
    return pl.pallas_call(
        functools.partial(lagged_kernel, layout, rows, length, scale),
        out_shape=(shape, shape),
        in_specs=[
            pl.BlockSpec(memory_space=pltpu.SMEM),
            pl.BlockSpec(memory_space=pltpu.VMEM),
        ]
        + [pl.BlockSpec(memory_space=pl.ANY)] * len(operands),
        out_specs=(pl.BlockSpec(memory_space=pltpu.VMEM),) * 2,
        scratch_shapes=[
            pltpu.VMEM((depth, rows, length + 2 * EDGE), jnp.bfloat16),
            pltpu.VMEM((depth, 2 * channels, length), jnp.bfloat16),
            pltpu.VMEM((LAGS * rows, 2 * channels), jnp.float32),
            pltpu.SemaphoreType.DMA((depth,)),
            pltpu.SemaphoreType.DMA((depth,)),
            pltpu.SemaphoreType.DMA((depth,)),
        ],
        compiler_params=pltpu.CompilerParams(vmem_limit_bytes=40 * 1024 * 1024),
        name="lagged",
    )(place, edges, *operands)


def on_device(raw_strain, band_index, filter_taps):
    layout = Layout()
    channels, length = raw_strain.shape
    rows = channels // layout.depth
    scale = 1.0 / math.sqrt(length * layout.slices)
    block = lax.axis_index("ch")
    piece = lax.axis_index("ta")
    zl, core = piece // 2, piece % 2
    same = ((block % layout.cols) >= layout.cols // 2).astype(jnp.int32)
    place = jnp.stack([zl, core, same]).astype(jnp.int32)

    normalized = normalize(raw_strain, band_index, filter_taps)
    swapped_piece = lax.ppermute(normalized, AXES, layout.swap_columns())
    own = gather_ring(layout, normalized)
    swapped = gather_ring(layout, swapped_piece)

    mine = []
    for d in range(1 - layout.depth, layout.depth):
        slot = own[d % layout.ring][0]
        part = lax.dynamic_slice_in_dim(slot, zl * rows, rows, 0)
        mine.append(jnp.stack([part[:, :EDGE], part[:, length - EDGE :]]))
    edges = lax.ppermute(jnp.stack(mine), AXES, layout.swap_cores())

    kept, sent = lagged(layout, own, swapped, edges, place, channels, length, scale)
    return kept + lax.ppermute(sent, AXES, layout.swap_cores())


def solution(mesh):
    placed = (P("ch", "ta"), P("ch"), P())
    return jax.shard_map(
        on_device,
        mesh=mesh,
        in_specs=placed,
        out_specs=P(None, None, ("ch", "ta"), None),
        check_vma=False,
    )
```

time: 586 us -> 164 us (0.28)
  the two profiles are of different devices: /device:TPU:18 before, /device:TPU:21 now
where the time goes in v1:
time: 164 us; the launch traced here: 163 us
  starting transfers between devices  82.5 us (50%)
  waiting for transfers between devices  33.8 us (21%)
  Pallas kernels  20.1 us (12%)
  other arithmetic  15.5 us (9%)
  local copies, waits for them, and re-layouts  9.9 us (6%)
    ppermute x6, starting transfers between devices, gather_ring(): up = lax.ppermute(up, AXES, layout.from_ring(1))  28.8 us
    pallas_call x1, Pallas kernels, lagged(): pl.pallas_call(functools.partial(lagged_kernel, layout, rows, length, sca...  20.1 us
    ppermute x6, starting transfers between devices, gather_ring(): down = lax.ppermute(down, AXES, layout.from_ring(-1))  14.8 us
    ppermute x2, starting transfers between devices, gather_ring(): lax.ppermute(up[:half], AXES, layout.from_ring(1))  9.87 us
    ppermute x1, waiting for transfers between devices, on_device(): swapped_piece = lax.ppermute(normalized, AXES, layout.swap_columns())  9.17 us
    abs x1, other arithmetic, normalize(): magnitude = jnp.abs(filtered)  8 us
    ppermute x2, waiting for transfers between devices, to_neighbours(): from_high = lax.ppermute(low_part, 'ta', backward)  7.37 us
    ppermute x2, starting transfers between devices, to_neighbours(): from_low = lax.ppermute(high_part, 'ta', forward)  6.48 us
  transfers between devices with their start and end apart: 23, of which 9 were waited for; matrix products, arithmetic and copies ran while one was open for 5% of the time, Pallas kernels for 0%

profile of v1, /device:TPU:21, one launch (start us, length us, event | category | flops | bytes accessed | tf_op | source)
XLA Modules:
  0.0 162.6 jit_solution(1638927031176479044)
XLA Ops:
  1.0 4.6 %collective-permute-start = (f32[128,16]{1,0:T(8,128)S(1)}, f32[128,16]{1,0:T(8,128)S(1)}, u32[]{:S(2)}, u32[]{:S(2)}) collective-permute-start(f32[128,16]{1,0:T(8,128)S(1)} %get-tuple-element.11), channel_id=1, source_target_pairs={{0,1},{1,2},{2,3},{3,4},{4,5},{5,6},{6,7},{8,9},{9,10},{10,11},{11... | collective-permute-start | bytes 24584 | tf_op jit(solution)/shard_map/ppermute | solution.py:57
  9.1 2.1 %collective-permute-done.1 = f32[128,16]{1,0:T(8,128)S(1)} collective-permute-done((f32[128,16]{1,0:T(8,128)S(1)}, f32[128,16]{1,0:T(8,128)S(1)}, u32[]{:S(2)}, u32[]{:S(2)}) %collective-permute-start.1) | collective-permute-done | bytes 8224 | tf_op jit(solution)/shard_map/ppermute | solution.py:58
  11.2 8.0 %fusion.67 = (f32[128,1536]{1,0:T(8,128)S(1)}, f32[128,1536]{1,0:T(8,128)S(1)}) fusion(f32[128,1552]{1,0:T(8,128)S(1)} %constant_dynamic-update-slice_fusion, f32[128]{0:T(128)S(1)} %get-tuple-element.28, f32[128]{0:T(128)S(1)} %get-tuple-element.29, f32[128]{0:T(128)S(1)} %get-tuple-element.30, f32[128]{0:T(128)S(1)} %get-tuple-element.31, ...), kind=kLoop, calls=%fused_computation.183 | loop fusion | flops 16121856 | bytes 14967296 | tf_op jit(solution)/shard_map/abs | solution.py:77
  20.8 1.9 %collective-permute-start.2 = (f32[128,1536]{1,0:T(8,128)S(1)}, f32[128,1536]{1,0:T(8,128)S(1)}, u32[]{:S(2)}, u32[]{:S(2)}) collective-permute-start(f32[128,1536]{1,0:T(8,128)S(1)} %subtract_add_fusion), channel_id=1, source_target_pairs={{0,1},{1,2},{2,3},{3,4},{4,5},{5,6},{6,7},{8,9},{9,10},{10,11},{11... | collective-permute-start | bytes 2359304 | tf_op jit(solution)/shard_map/ppermute | solution.py:57
  22.7 2.5 %collective-permute-start.3 = (f32[128,1536]{1,0:T(8,128)S(1)}, f32[128,1536]{1,0:T(8,128)}, u32[]{:S(2)}, u32[]{:S(2)}) collective-permute-start(f32[128,1536]{1,0:T(8,128)S(1)} %copy.9), channel_id=1, source_target_pairs={{1,0},{2,1},{3,2},{4,3},{5,4},{6,5},{7,6},{9,8},{10,9},{11,10},{12... | collective-permute-start | bytes 2359304 | tf_op jit(solution)/shard_map/ppermute | solution.py:58
  25.2 6.4 %collective-permute-done.2 = f32[128,1536]{1,0:T(8,128)S(1)} collective-permute-done((f32[128,1536]{1,0:T(8,128)S(1)}, f32[128,1536]{1,0:T(8,128)S(1)}, u32[]{:S(2)}, u32[]{:S(2)}) %collective-permute-start.2) | collective-permute-done | bytes 786464 | tf_op jit(solution)/shard_map/ppermute | solution.py:57
  31.6 5.2 %collective-permute-done.3 = f32[128,1536]{1,0:T(8,128)} collective-permute-done((f32[128,1536]{1,0:T(8,128)S(1)}, f32[128,1536]{1,0:T(8,128)}, u32[]{:S(2)}, u32[]{:S(2)}) %collective-permute-start.3) | collective-permute-done | bytes 786464 | tf_op jit(solution)/shard_map/ppermute | solution.py:58
  40.2 4.0 %collective-permute-start.4 = (bf16[128,1536]{1,0:T(8,128)(2,1)S(1)}, bf16[128,1536]{1,0:T(8,128)(2,1)S(1)}, u32[]{:S(2)}, u32[]{:S(2)}) collective-permute-start(bf16[128,1536]{1,0:T(8,128)(2,1)S(1)} %divide_convert_fusion.refs_2_), channel_id=1, source_target_pairs={{262,0},{263,1},{270,8},{271,9},{278,16},{279,17},{286,24},{287,25... | collective-permute-start | bytes 1179656 | tf_op jit(solution)/shard_map/ppermute | solution.py:97
  44.2 5.7 %collective-permute-start.13 = (bf16[128,1536]{1,0:T(8,128)(2,1)S(1)}, bf16[128,1536]{1,0:T(8,128)(2,1)S(1)}, u32[]{:S(2)}, u32[]{:S(2)}) collective-permute-start(bf16[128,1536]{1,0:T(8,128)(2,1)S(1)} %divide_convert_fusion.refs_2_), channel_id=1, source_target_pairs={{128,0},{129,1},{136,8},{137,9},{144,16},{145,17},{152,24},{153,25... | collective-permute-start | bytes 1179656 | tf_op jit(solution)/shard_map/ppermute | solution.py:255
  49.9 7.6 %collective-permute-start.8 = (bf16[128,1536]{1,0:T(8,128)(2,1)S(1)}, bf16[128,1536]{1,0:T(8,128)(2,1)S(1)}, u32[]{:S(2)}, u32[]{:S(2)}) collective-permute-start(bf16[128,1536]{1,0:T(8,128)(2,1)S(1)} %collective-permute-done.7.refs_3_), channel_id=1, source_target_pairs={{2,0},{3,1},{10,8},{11,9},{18,16},{19,17},{26,24},{27,25},{34,32},... | collective-permute-start | bytes 1179656 | tf_op jit(solution)/shard_map/ppermute | solution.py:96
  59.5 9.2 %collective-permute-done.13.refs_11_ = bf16[128,1536]{1,0:T(8,128)(2,1)S(1)} collective-permute-done((bf16[128,1536]{1,0:T(8,128)(2,1)S(1)}, bf16[128,1536]{1,0:T(8,128)(2,1)S(1)}, u32[]{:S(2)}, u32[]{:S(2)}) %collective-permute-start.13) | collective-permute-done | bytes 393248 | tf_op jit(solution)/shard_map/ppermute | solution.py:255
  68.6 3.1 %collective-permute-start.18 = (bf16[128,1536]{1,0:T(8,128)(2,1)S(1)}, bf16[128,1536]{1,0:T(8,128)(2,1)S(1)}, u32[]{:S(2)}, u32[]{:S(2)}) collective-permute-start(bf16[128,1536]{1,0:T(8,128)(2,1)S(1)} %collective-permute-done.13.refs_11_), channel_id=1, source_target_pairs={{262,0},{263,1},{270,8},{271,9},{278,16},{279,17},{286,24},{287,25... | collective-permute-start | bytes 1179656 | tf_op jit(solution)/shard_map/ppermute | solution.py:97
  71.8 6.8 %collective-permute-start.14 = (bf16[128,1536]{1,0:T(8,128)(2,1)S(1)}, bf16[128,1536]{1,0:T(8,128)(2,1)}, u32[]{:S(2)}, u32[]{:S(2)}) collective-permute-start(bf16[128,1536]{1,0:T(8,128)(2,1)S(1)} %collective-permute-done.13.refs_11_), channel_id=1, source_target_pairs={{2,0},{3,1},{10,8},{11,9},{18,16},{19,17},{26,24},{27,25},{34,32},... | collective-permute-start | bytes 1179656 | tf_op jit(solution)/shard_map/ppermute | solution.py:96
  78.7 3.4 %collective-permute-start.9 = (bf16[128,1536]{1,0:T(8,128)(2,1)S(1)}, bf16[128,1536]{1,0:T(8,128)(2,1)S(1)}, u32[]{:S(2)}, u32[]{:S(2)}) collective-permute-start(bf16[128,1536]{1,0:T(8,128)(2,1)S(1)} %collective-permute-done.8.refs_4_), channel_id=1, source_target_pairs={{2,0},{3,1},{10,8},{11,9},{18,16},{19,17},{26,24},{27,25},{34,32},... | collective-permute-start | bytes 1179656 | tf_op jit(solution)/shard_map/ppermute | solution.py:96
  87.5 4.6 %collective-permute-start.15 = (bf16[128,1536]{1,0:T(8,128)(2,1)}, bf16[128,1536]{1,0:T(8,128)(2,1)S(1)}, u32[]{:S(2)}, u32[]{:S(2)}) collective-permute-start(bf16[128,1536]{1,0:T(8,128)(2,1)} %collective-permute-done.14.refs_12_), channel_id=1, source_target_pairs={{2,0},{3,1},{10,8},{11,9},{18,16},{19,17},{26,24},{27,25},{34,32},... | collective-permute-start | bytes 1179656 | tf_op jit(solution)/shard_map/ppermute | solution.py:96
  92.1 2.7 %collective-permute-done.9.refs_5_ = bf16[128,1536]{1,0:T(8,128)(2,1)S(1)} collective-permute-done((bf16[128,1536]{1,0:T(8,128)(2,1)S(1)}, bf16[128,1536]{1,0:T(8,128)(2,1)S(1)}, u32[]{:S(2)}, u32[]{:S(2)}) %collective-permute-start.9) | collective-permute-done | bytes 393248 | tf_op jit(solution)/shard_map/ppermute | solution.py:96
  95.5 5.3 %collective-permute-start.11 = (bf16[64,1536]{1,0:T(8,128)(2,1)}, bf16[64,1536]{1,0:T(8,128)(2,1)}, u32[]{:S(2)}, u32[]{:S(2)}) collective-permute-start(bf16[64,1536]{1,0:T(8,128)(2,1)} %slice.466), channel_id=1, source_target_pairs={{2,0},{3,1},{10,8},{11,9},{18,16},{19,17},{26,24},{27,25},{34,32},... | collective-permute-start | bytes 589832 | tf_op jit(solution)/shard_map/ppermute | solution.py:102
  107.2 4.6 %collective-permute-start.16 = (bf16[128,1536]{1,0:T(8,128)(2,1)S(1)}, bf16[128,1536]{1,0:T(8,128)(2,1)S(1)}, u32[]{:S(2)}, u32[]{:S(2)}) collective-permute-start(bf16[128,1536]{1,0:T(8,128)(2,1)S(1)} %collective-permute-done.15.refs_13_), channel_id=1, source_target_pairs={{2,0},{3,1},{10,8},{11,9},{18,16},{19,17},{26,24},{27,25},{34,32},... | collective-permute-start | bytes 1179656 | tf_op jit(solution)/shard_map/ppermute | solution.py:96
  113.6 3.1 %collective-permute-done.20.refs_17_ = bf16[128,1536]{1,0:T(8,128)(2,1)S(1)} collective-permute-done((bf16[128,1536]{1,0:T(8,128)(2,1)S(1)}, bf16[128,1536]{1,0:T(8,128)(2,1)S(1)}, u32[]{:S(2)}, u32[]{:S(2)}) %collective-permute-start.20) | collective-permute-done | bytes 393248 | tf_op jit(solution)/shard_map/ppermute | solution.py:97
  120.0 4.6 %collective-permute-start.17 = (bf16[64,1536]{1,0:T(8,128)(2,1)}, bf16[64,1536]{1,0:T(8,128)(2,1)}, u32[]{:S(2)}, u32[]{:S(2)}) collective-permute-start(bf16[64,1536]{1,0:T(8,128)(2,1)} %slice.468), channel_id=1, source_target_pairs={{2,0},{3,1},{10,8},{11,9},{18,16},{19,17},{26,24},{27,25},{34,32},... | collective-permute-start | bytes 589832 | tf_op jit(solution)/shard_map/ppermute | solution.py:102
  125.2 6.3 %collective-permute-start.10 = (bf16[7,2,32,128]{3,2,1,0:T(8,128)(2,1)}, bf16[7,2,32,128]{3,2,1,0:T(8,128)(2,1)}, u32[]{:S(2)}, u32[]{:S(2)}) collective-permute-start(bf16[7,2,32,128]{3,2,1,0:T(8,128)(2,1)} %constant_dynamic-update-slice_fusion.2), channel_id=1, source_target_pairs={{1,0},{0,1},{9,8},{8,9},{17,16},{16,17},{25,24},{24,25},{33,32},{3... | collective-permute-start | bytes 344072 | tf_op jit(solution)/shard_map/ppermute | solution.py:264
  136.8 20.1 %lagged.1 = (f32[2,65,16,128]{3,2,1,0:T(8,128)S(1)}, f32[2,65,16,128]{3,2,1,0:T(8,128)S(1)}) custom-call(s32[3]{0:T(128)S(1)} %pad_add_fusion.refs_0_, bf16[7,2,32,128]{3,2,1,0:T(8,128)(2,1)} %collective-permute-done.10.refs_1_, bf16[128,1536]{1,0:T(8,128)(2,1)S(1)} %divide_convert_fusion.refs_2_, bf16[128,1536]{1,0:T(8,128)(2,1)S(1)} %collective-permute-done.7.refs_3_, ...), custom_call_target="tpu_custom_call" | custom-call | tf_op jit(solution)/shard_map/lagged/pallas_call | solution.py:221
  156.9 2.3 %collective-permute-start.22 = (f32[2,65,16,128]{3,2,1,0:T(8,128)S(1)}, f32[2,65,16,128]{3,2,1,0:T(8,128)S(1)}, u32[]{:S(2)}, u32[]{:S(2)}) collective-permute-start(f32[2,65,16,128]{3,2,1,0:T(8,128)S(1)} %get-tuple-element.8), channel_id=1, source_target_pairs={{1,0},{0,1},{9,8},{8,9},{17,16},{16,17},{25,24},{24,25},{33,32},{3... | collective-permute-start | bytes 3194888 | tf_op jit(solution)/shard_map/ppermute | solution.py:267
  159.2 2.3 %collective-permute-done.22 = f32[2,65,16,128]{3,2,1,0:T(8,128)S(1)} collective-permute-done((f32[2,65,16,128]{3,2,1,0:T(8,128)S(1)}, f32[2,65,16,128]{3,2,1,0:T(8,128)S(1)}, u32[]{:S(2)}, u32[]{:S(2)}) %collective-permute-start.22) | collective-permute-done | bytes 1064992 | tf_op jit(solution)/shard_map/ppermute | solution.py:267
  (83 shorter events, 35.8 us)
Async XLA Ops:
  1.0 10.2 %collective-permute-start = (f32[128,16]{1,0:T(8,128)S(1)}, f32[128,16]{1,0:T(8,128)S(1)}, u32[]{:S(2)}, u32[]{:S(2)}) collective-permute-start(f32[128,16]{1,0:T(8,128)S(1)} %get-tuple-element.11), channel_id=1, source_target_pairs={{0,1},{1,2},{2,3},{3,4},{4,5},{5,6},{6,7},{8,9},{9,10},{10,11},{11... | collective-permute-start | bytes 24584 | tf_op jit(solution)/shard_map/ppermute | solution.py:57
  5.6 5.6 %collective-permute-start.1 = (f32[128,16]{1,0:T(8,128)S(1)}, f32[128,16]{1,0:T(8,128)S(1)}, u32[]{:S(2)}, u32[]{:S(2)}) collective-permute-start(f32[128,16]{1,0:T(8,128)S(1)} %get-tuple-element.12), channel_id=1, source_target_pairs={{1,0},{2,1},{3,2},{4,3},{5,4},{6,5},{7,6},{9,8},{10,9},{11,10},{12... | collective-permute-start | bytes 24584 | tf_op jit(solution)/shard_map/ppermute | solution.py:58
  20.8 10.8 %collective-permute-start.2 = (f32[128,1536]{1,0:T(8,128)S(1)}, f32[128,1536]{1,0:T(8,128)S(1)}, u32[]{:S(2)}, u32[]{:S(2)}) collective-permute-start(f32[128,1536]{1,0:T(8,128)S(1)} %subtract_add_fusion), channel_id=1, source_target_pairs={{0,1},{1,2},{2,3},{3,4},{4,5},{5,6},{6,7},{8,9},{9,10},{10,11},{11... | collective-permute-start | bytes 2359304 | tf_op jit(solution)/shard_map/ppermute | solution.py:57
  22.7 14.2 %collective-permute-start.3 = (f32[128,1536]{1,0:T(8,128)S(1)}, f32[128,1536]{1,0:T(8,128)}, u32[]{:S(2)}, u32[]{:S(2)}) collective-permute-start(f32[128,1536]{1,0:T(8,128)S(1)} %copy.9), channel_id=1, source_target_pairs={{1,0},{2,1},{3,2},{4,3},{5,4},{6,5},{7,6},{9,8},{10,9},{11,10},{12... | collective-permute-start | bytes 2359304 | tf_op jit(solution)/shard_map/ppermute | solution.py:58
  38.3 11.6 %collective-permute-start.7 = (bf16[128,1536]{1,0:T(8,128)(2,1)S(1)}, bf16[128,1536]{1,0:T(8,128)(2,1)S(1)}, u32[]{:S(2)}, u32[]{:S(2)}) collective-permute-start(bf16[128,1536]{1,0:T(8,128)(2,1)S(1)} %divide_convert_fusion.refs_2_), channel_id=1, source_target_pairs={{2,0},{3,1},{10,8},{11,9},{18,16},{19,17},{26,24},{27,25},{34,32},... | collective-permute-start | bytes 1179656 | tf_op jit(solution)/shard_map/ppermute | solution.py:96
  40.2 17.3 %collective-permute-start.4 = (bf16[128,1536]{1,0:T(8,128)(2,1)S(1)}, bf16[128,1536]{1,0:T(8,128)(2,1)S(1)}, u32[]{:S(2)}, u32[]{:S(2)}) collective-permute-start(bf16[128,1536]{1,0:T(8,128)(2,1)S(1)} %divide_convert_fusion.refs_2_), channel_id=1, source_target_pairs={{262,0},{263,1},{270,8},{271,9},{278,16},{279,17},{286,24},{287,25... | collective-permute-start | bytes 1179656 | tf_op jit(solution)/shard_map/ppermute | solution.py:97
  44.2 24.4 %collective-permute-start.13 = (bf16[128,1536]{1,0:T(8,128)(2,1)S(1)}, bf16[128,1536]{1,0:T(8,128)(2,1)S(1)}, u32[]{:S(2)}, u32[]{:S(2)}) collective-permute-start(bf16[128,1536]{1,0:T(8,128)(2,1)S(1)} %divide_convert_fusion.refs_2_), channel_id=1, source_target_pairs={{128,0},{129,1},{136,8},{137,9},{144,16},{145,17},{152,24},{153,25... | collective-permute-start | bytes 1179656 | tf_op jit(solution)/shard_map/ppermute | solution.py:255
  49.9 28.7 %collective-permute-start.8 = (bf16[128,1536]{1,0:T(8,128)(2,1)S(1)}, bf16[128,1536]{1,0:T(8,128)(2,1)S(1)}, u32[]{:S(2)}, u32[]{:S(2)}) collective-permute-start(bf16[128,1536]{1,0:T(8,128)(2,1)S(1)} %collective-permute-done.7.refs_3_), channel_id=1, source_target_pairs={{2,0},{3,1},{10,8},{11,9},{18,16},{19,17},{26,24},{27,25},{34,32},... | collective-permute-start | bytes 1179656 | tf_op jit(solution)/shard_map/ppermute | solution.py:96
  57.5 24.5 %collective-permute-start.5 = (bf16[128,1536]{1,0:T(8,128)(2,1)S(1)}, bf16[128,1536]{1,0:T(8,128)(2,1)S(1)}, u32[]{:S(2)}, u32[]{:S(2)}) collective-permute-start(bf16[128,1536]{1,0:T(8,128)(2,1)S(1)} %collective-permute-done.4.refs_10_), channel_id=1, source_target_pairs={{262,0},{263,1},{270,8},{271,9},{278,16},{279,17},{286,24},{287,25... | collective-permute-start | bytes 1179656 | tf_op jit(solution)/shard_map/ppermute | solution.py:97
  68.6 34.8 %copy-start.1 = (bf16[128,1536]{1,0:T(8,128)(2,1)}, bf16[128,1536]{1,0:T(8,128)(2,1)S(1)}, u32[]{:S(2)}) copy-start(bf16[128,1536]{1,0:T(8,128)(2,1)S(1)} %collective-permute-done.13.refs_11_) | copy-start | bytes 1179652
  68.6 16.9 %collective-permute-start.18 = (bf16[128,1536]{1,0:T(8,128)(2,1)S(1)}, bf16[128,1536]{1,0:T(8,128)(2,1)S(1)}, u32[]{:S(2)}, u32[]{:S(2)}) collective-permute-start(bf16[128,1536]{1,0:T(8,128)(2,1)S(1)} %collective-permute-done.13.refs_11_), channel_id=1, source_target_pairs={{262,0},{263,1},{270,8},{271,9},{278,16},{279,17},{286,24},{287,25... | collective-permute-start | bytes 1179656 | tf_op jit(solution)/shard_map/ppermute | solution.py:97
  71.8 15.7 %collective-permute-start.14 = (bf16[128,1536]{1,0:T(8,128)(2,1)S(1)}, bf16[128,1536]{1,0:T(8,128)(2,1)}, u32[]{:S(2)}, u32[]{:S(2)}) collective-permute-start(bf16[128,1536]{1,0:T(8,128)(2,1)S(1)} %collective-permute-done.13.refs_11_), channel_id=1, source_target_pairs={{2,0},{3,1},{10,8},{11,9},{18,16},{19,17},{26,24},{27,25},{34,32},... | collective-permute-start | bytes 1179656 | tf_op jit(solution)/shard_map/ppermute | solution.py:96
  78.7 16.1 %collective-permute-start.9 = (bf16[128,1536]{1,0:T(8,128)(2,1)S(1)}, bf16[128,1536]{1,0:T(8,128)(2,1)S(1)}, u32[]{:S(2)}, u32[]{:S(2)}) collective-permute-start(bf16[128,1536]{1,0:T(8,128)(2,1)S(1)} %collective-permute-done.8.refs_4_), channel_id=1, source_target_pairs={{2,0},{3,1},{10,8},{11,9},{18,16},{19,17},{26,24},{27,25},{34,32},... | collective-permute-start | bytes 1179656 | tf_op jit(solution)/shard_map/ppermute | solution.py:96
  82.0 18.8 %collective-permute-start.6 = (bf16[128,1536]{1,0:T(8,128)(2,1)S(1)}, bf16[128,1536]{1,0:T(8,128)(2,1)S(1)}, u32[]{:S(2)}, u32[]{:S(2)}) collective-permute-start(bf16[128,1536]{1,0:T(8,128)(2,1)S(1)} %collective-permute-done.5.refs_9_), channel_id=1, source_target_pairs={{262,0},{263,1},{270,8},{271,9},{278,16},{279,17},{286,24},{287,25... | collective-permute-start | bytes 1179656 | tf_op jit(solution)/shard_map/ppermute | solution.py:97
  85.5 18.0 %collective-permute-start.19 = (bf16[128,1536]{1,0:T(8,128)(2,1)S(1)}, bf16[128,1536]{1,0:T(8,128)(2,1)S(1)}, u32[]{:S(2)}, u32[]{:S(2)}) collective-permute-start(bf16[128,1536]{1,0:T(8,128)(2,1)S(1)} %collective-permute-done.18.refs_19_), channel_id=1, source_target_pairs={{262,0},{263,1},{270,8},{271,9},{278,16},{279,17},{286,24},{287,25... | collective-permute-start | bytes 1179656 | tf_op jit(solution)/shard_map/ppermute | solution.py:97
  87.5 19.8 %collective-permute-start.15 = (bf16[128,1536]{1,0:T(8,128)(2,1)}, bf16[128,1536]{1,0:T(8,128)(2,1)S(1)}, u32[]{:S(2)}, u32[]{:S(2)}) collective-permute-start(bf16[128,1536]{1,0:T(8,128)(2,1)} %collective-permute-done.14.refs_12_), channel_id=1, source_target_pairs={{2,0},{3,1},{10,8},{11,9},{18,16},{19,17},{26,24},{27,25},{34,32},... | collective-permute-start | bytes 1179656 | tf_op jit(solution)/shard_map/ppermute | solution.py:96
  95.5 37.3 %collective-permute-start.11 = (bf16[64,1536]{1,0:T(8,128)(2,1)}, bf16[64,1536]{1,0:T(8,128)(2,1)}, u32[]{:S(2)}, u32[]{:S(2)}) collective-permute-start(bf16[64,1536]{1,0:T(8,128)(2,1)} %slice.466), channel_id=1, source_target_pairs={{2,0},{3,1},{10,8},{11,9},{18,16},{19,17},{26,24},{27,25},{34,32},... | collective-permute-start | bytes 589832 | tf_op jit(solution)/shard_map/ppermute | solution.py:102
  101.5 31.3 %collective-permute-start.12 = (bf16[64,1536]{1,0:T(8,128)(2,1)}, bf16[64,1536]{1,0:T(8,128)(2,1)}, u32[]{:S(2)}, u32[]{:S(2)}) collective-permute-start(bf16[64,1536]{1,0:T(8,128)(2,1)} %slice.467), channel_id=1, source_target_pairs={{262,0},{263,1},{270,8},{271,9},{278,16},{279,17},{286,24},{287,25... | collective-permute-start | bytes 589832 | tf_op jit(solution)/shard_map/ppermute | solution.py:103
  103.5 13.2 %collective-permute-start.20 = (bf16[128,1536]{1,0:T(8,128)(2,1)S(1)}, bf16[128,1536]{1,0:T(8,128)(2,1)S(1)}, u32[]{:S(2)}, u32[]{:S(2)}) collective-permute-start(bf16[128,1536]{1,0:T(8,128)(2,1)S(1)} %collective-permute-done.19.refs_18_), channel_id=1, source_target_pairs={{262,0},{263,1},{270,8},{271,9},{278,16},{279,17},{286,24},{287,25... | collective-permute-start | bytes 1179656 | tf_op jit(solution)/shard_map/ppermute | solution.py:97
  107.2 12.1 %collective-permute-start.16 = (bf16[128,1536]{1,0:T(8,128)(2,1)S(1)}, bf16[128,1536]{1,0:T(8,128)(2,1)S(1)}, u32[]{:S(2)}, u32[]{:S(2)}) collective-permute-start(bf16[128,1536]{1,0:T(8,128)(2,1)S(1)} %collective-permute-done.15.refs_13_), channel_id=1, source_target_pairs={{2,0},{3,1},{10,8},{11,9},{18,16},{19,17},{26,24},{27,25},{34,32},... | collective-permute-start | bytes 1179656 | tf_op jit(solution)/shard_map/ppermute | solution.py:96
  117.4 15.4 %collective-permute-start.21 = (bf16[64,1536]{1,0:T(8,128)(2,1)}, bf16[64,1536]{1,0:T(8,128)(2,1)}, u32[]{:S(2)}, u32[]{:S(2)}) collective-permute-start(bf16[64,1536]{1,0:T(8,128)(2,1)} %slice.469), channel_id=1, source_target_pairs={{262,0},{263,1},{270,8},{271,9},{278,16},{279,17},{286,24},{287,25... | collective-permute-start | bytes 589832 | tf_op jit(solution)/shard_map/ppermute | solution.py:103
  120.0 12.8 %collective-permute-start.17 = (bf16[64,1536]{1,0:T(8,128)(2,1)}, bf16[64,1536]{1,0:T(8,128)(2,1)}, u32[]{:S(2)}, u32[]{:S(2)}) collective-permute-start(bf16[64,1536]{1,0:T(8,128)(2,1)} %slice.468), channel_id=1, source_target_pairs={{2,0},{3,1},{10,8},{11,9},{18,16},{19,17},{26,24},{27,25},{34,32},... | collective-permute-start | bytes 589832 | tf_op jit(solution)/shard_map/ppermute | solution.py:102
  125.2 7.6 %collective-permute-start.10 = (bf16[7,2,32,128]{3,2,1,0:T(8,128)(2,1)}, bf16[7,2,32,128]{3,2,1,0:T(8,128)(2,1)}, u32[]{:S(2)}, u32[]{:S(2)}) collective-permute-start(bf16[7,2,32,128]{3,2,1,0:T(8,128)(2,1)} %constant_dynamic-update-slice_fusion.2), channel_id=1, source_target_pairs={{1,0},{0,1},{9,8},{8,9},{17,16},{16,17},{25,24},{24,25},{33,32},{3... | collective-permute-start | bytes 344072 | tf_op jit(solution)/shard_map/ppermute | solution.py:264
  156.9 4.6 %collective-permute-start.22 = (f32[2,65,16,128]{3,2,1,0:T(8,128)S(1)}, f32[2,65,16,128]{3,2,1,0:T(8,128)S(1)}, u32[]{:S(2)}, u32[]{:S(2)}) collective-permute-start(f32[2,65,16,128]{3,2,1,0:T(8,128)S(1)} %get-tuple-element.8), channel_id=1, source_target_pairs={{1,0},{0,1},{9,8},{8,9},{17,16},{16,17},{25,24},{24,25},{33,32},{3... | collective-permute-start | bytes 3194888 | tf_op jit(solution)/shard_map/ppermute | solution.py:267
  (10 other events, 83.0 us)

commit v2 on v1

v2 whole, which is shorter than its diff:
```python
import functools
import math

import jax
import jax.numpy as jnp
from jax import lax
from jax.experimental import pallas as pl
from jax.experimental.pallas import tpu as pltpu
from jax.sharding import PartitionSpec as P

HF = 16
TAPS = 33
NBANDS = 4
LAGH = 32
LAGS = 65
ROUNDS = 2
EDGE = 128
PAIRS = LAGH + 1
GROUP = 11
AXES = ("ch", "ta")


class Layout:
    def __init__(self):
        self.blocks = lax.axis_size("ch")
        self.slices = lax.axis_size("ta")
        self.cols = self.blocks // 2
        self.depth = self.slices // 2
        self.ring = 2 * self.depth

    def index(self, pos, col, core):
        zh, zl = divmod(pos % self.ring, self.depth)
        return (zh * self.cols + col) * self.slices + zl * 2 + core

    def every(self):
        for pos in range(self.ring):
            for col in range(self.cols):
                for core in range(2):
                    yield pos, col, core

    def from_ring(self, step):
        return [(self.index(p + step, c, k), self.index(p, c, k)) for p, c, k in self.every()]

    def swap_columns(self):
        return [
            (self.index(p, (c + self.cols // 2) % self.cols, k), self.index(p, c, k))
            for p, c, k in self.every()
        ]

    def swap_cores(self):
        return [(self.index(p, c, 1 - k), self.index(p, c, k)) for p, c, k in self.every()]


def to_neighbours(low_part, high_part):
    count = lax.axis_size("ta")
    forward = [(i, i + 1) for i in range(count - 1)]
    backward = [(i + 1, i) for i in range(count - 1)]
    from_low = lax.ppermute(high_part, "ta", forward)
    from_high = lax.ppermute(low_part, "ta", backward)
    return from_low, from_high


def normalize(raw, band_index, filter_taps):
    length = raw.shape[1]
    time_groups = lax.axis_size("ta")
    whole_len = length * time_groups
    onehot = (band_index[:, None] == jnp.arange(NBANDS, dtype=jnp.int32)[None, :]).astype(
        jnp.float32
    )
    coeffs = jnp.dot(
        onehot, filter_taps, precision=lax.Precision.HIGHEST, preferred_element_type=jnp.float32
    )
    low, high = to_neighbours(raw[:, :HF], raw[:, length - HF :])
    extended = jnp.concatenate([low, raw, high], axis=1)
    filtered = jnp.zeros_like(raw)
    for step in range(TAPS):
        filtered = filtered + coeffs[:, step : step + 1] * extended[:, step : step + length]
    magnitude = jnp.abs(filtered)
    prefix = jnp.cumsum(magnitude, axis=1)
    total = prefix[:, length - 1 :]
    suffix = total - prefix + magnitude
    before, after = to_neighbours(prefix, suffix)
    window_sum = before + total + after
    global_time = lax.axis_index("ta") * length + jnp.arange(length, dtype=jnp.int32)
    upper = jnp.minimum(global_time + length, whole_len - 1) + 1
    lower = jnp.maximum(global_time - length, 0)
    counted = (upper - lower).astype(jnp.float32)
    level = window_sum / counted[None, :]
    return (filtered / (level + 1e-06)).astype(jnp.bfloat16)


def gather_ring(layout, piece):
    ring = layout.ring
    slots = {0: (piece,)}
    up = down = piece
    for step in range(1, ring // 2):
        up = lax.ppermute(up, AXES, layout.from_ring(1))
        down = lax.ppermute(down, AXES, layout.from_ring(-1))
        slots[step] = (up,)
        slots[ring - step] = (down,)
    half = piece.shape[0] // 2
    slots[ring // 2] = (
        lax.ppermute(up[:half], AXES, layout.from_ring(1)),
        lax.ppermute(down[half:], AXES, layout.from_ring(-1)),
    )
    return slots


class Job:
    def __init__(self, ring, steps, slots_of_rows, first_edge, last):
        self.ring = ring
        self.depth = ring // 2
        self.steps = steps
        self.slots_of_rows = slots_of_rows
        self.first_edge = first_edge
        self.last = last

    def row_slots(self):
        return sorted({s % self.ring for d in self.steps for s in (d, d - self.depth)} - {self.depth})

    def partner_slots(self):
        return sorted({(s + f) % self.ring for d in self.steps for s in (d, d - self.depth)
                       for f in (0, self.depth)})


def lagged_kernel(job, rows, length, scale, n_rows, partner_counts, has_acc, *refs):
    refs = list(refs)
    place_ref, edge_ref = refs.pop(0), refs.pop(0)
    row_refs = [refs.pop(0) for _ in range(n_rows)]
    partner_refs = {d: [refs.pop(0) for _ in range(n)] for d, n in partner_counts.items()}
    acc_in = refs.pop(0) if has_acc else None
    if job.last:
        mine_ref, other_ref, own_buf, part_buf, both_buf, row_sem, part_sem, acc = refs
    else:
        acc, own_buf, part_buf, both_buf, row_sem, part_sem = refs
    ring, depth = job.ring, job.depth
    zl, core, far = place_ref[0], place_ref[1], place_ref[2]
    channels = part_buf.shape[1]
    count = len(job.steps)
    first_step = job.steps[0]
    deep = length + EDGE

    for j, step in enumerate(job.steps):
        k = lax.rem(zl + step, depth)
        target = own_buf.at[j, :, pl.ds(EDGE, length)]
        if job.slots_of_rows:
            own_d = lax.rem(k - zl + ring, ring)
            first = pl.multiple_of(zl * rows, rows)
            for d, ref in zip(job.row_slots(), row_refs, strict=True):

                @pl.when(own_d == d)
                def _():
                    pltpu.make_async_copy(
                        ref.at[pl.ds(first, rows)], target, row_sem.at[j]
                    ).start()

        else:
            pltpu.make_async_copy(row_refs[0].at[k], target, row_sem.at[j]).start()
        wanted = lax.rem(k - zl + ring + far * depth, ring)
        for d, halves in partner_refs.items():

            @pl.when(wanted == d)
            def _():
                row = 0
                for ref in halves:
                    n = ref.shape[0]
                    pltpu.make_async_copy(
                        ref, part_buf.at[j, pl.ds(row, n), pl.ds(EDGE, length)], part_sem.at[j]
                    ).start()
                    row += n

    if has_acc:
        acc[...] = acc_in[...]
    else:
        acc[...] = jnp.zeros_like(acc)
    for j in range(count):
        own_buf[j, :, deep + EDGE :] = jnp.zeros((rows, EDGE), jnp.bfloat16)
        part_buf[j, :, :EDGE] = jnp.zeros((channels, EDGE), jnp.bfloat16)
        part_buf[j, :, deep:] = jnp.zeros((channels, EDGE), jnp.bfloat16)

    def body(j, carry):
        k = lax.rem(zl + first_step + j, depth)
        left, right = k - 1 + core, k + core
        left_ok = (left >= 0).astype(jnp.bfloat16)
        right_ok = (right < depth).astype(jnp.bfloat16)
        base = job.first_edge - zl if job.slots_of_rows else job.first_edge
        left_at = base + jnp.maximum(left, 0)
        right_at = base + jnp.minimum(right, depth - 1)
        own_buf[j, :, :EDGE] = edge_ref[left_at, 1] * left_ok
        own_buf[j, :, deep : deep + EDGE] = edge_ref[right_at, 0] * right_ok
        for buf, sem in ((own_buf, row_sem), (part_buf, part_sem)):
            whole = buf.at[j, :, pl.ds(EDGE, length)]
            pltpu.make_async_copy(whole, whole, sem.at[j]).wait()
        both_buf[:channels] = part_buf[j, :, EDGE : EDGE + deep]
        both_buf[channels:] = part_buf[j, :, EDGE - 1 : EDGE - 1 + deep]
        partner = both_buf[...]
        for group in range(PAIRS // GROUP):
            stacked = jnp.concatenate(
                [
                    own_buf[j, :, EDGE + LAGH - 2 * a : EDGE + LAGH - 2 * a + deep]
                    for a in range(group * GROUP, (group + 1) * GROUP)
                ],
                axis=0,
            )
            block = pl.ds(group * GROUP * rows, GROUP * rows)
            acc[block] += lax.dot_general(
                stacked, partner, (((1,), (1,)), ((), ())), preferred_element_type=jnp.float32
            )
        return carry

    lax.fori_loop(0, count, body, 0)
    if not job.last:
        return
    half_rows = rows // 2

    for ref, which in ((mine_ref, core), (other_ref, 1 - core)):
        for a in range(PAIRS):
            start = pl.multiple_of(a * rows + which * half_rows, half_rows)
            ref[2 * a] = acc[pl.ds(start, half_rows), :channels] * scale
            if a > 0:
                ref[2 * a - 1] = acc[pl.ds(start, half_rows), channels:] * scale


def lagged(job, place, edges, row_arrays, slots, rows, scale, acc=None):
    channels, length = slots[0][0].shape
    if job.slots_of_rows:
        row_arrays = [slots[d][0] for d in job.row_slots()]
    partners = {d: slots[d] for d in job.partner_slots()}
    operands = list(row_arrays) + [ref for d in partners for ref in partners[d]]
    count = len(job.steps)
    half = jax.ShapeDtypeStruct((LAGS, rows // 2, channels), jnp.float32)
    full = (PAIRS * rows, 2 * channels)
    vmem = pl.BlockSpec(memory_space=pltpu.VMEM)
    scratch = [
        pltpu.VMEM((count, rows, length + 3 * EDGE), jnp.bfloat16),
        pltpu.VMEM((count, channels, length + 2 * EDGE), jnp.bfloat16),
        pltpu.VMEM((2 * channels, length + EDGE), jnp.bfloat16),
        pltpu.SemaphoreType.DMA((count,)),
        pltpu.SemaphoreType.DMA((count,)),
    ]
    if job.last:
        scratch.append(pltpu.VMEM(full, jnp.float32))
    has_acc = acc is not None
    return pl.pallas_call(
        functools.partial(
            lagged_kernel,
            job,
            rows,
            length,
            scale,
            len(row_arrays),
            {d: len(p) for d, p in partners.items()},
            has_acc,
        ),
        out_shape=(half, half) if job.last else jax.ShapeDtypeStruct(full, jnp.float32),
        in_specs=[pl.BlockSpec(memory_space=pltpu.SMEM), vmem]
        + [pl.BlockSpec(memory_space=pl.ANY)] * len(operands)
        + [vmem] * has_acc,
        out_specs=(vmem, vmem) if job.last else vmem,
        scratch_shapes=scratch,
        compiler_params=pltpu.CompilerParams(vmem_limit_bytes=32 * 1024 * 1024),
        cost_estimate=pl.CostEstimate(
            flops=2 * count * full[0] * full[1] * length,
            bytes_accessed=2 * count * channels * length,
            transcendentals=0,
        ),
        name="lagged",
    )(place, edges, *operands, *([acc] if has_acc else []))


def on_device(raw_strain, band_index, filter_taps):
    layout = Layout()
    channels, length = raw_strain.shape
    depth, ring = layout.depth, layout.ring
    rows = channels // depth
    scale = 1.0 / math.sqrt(length * layout.slices)
    block = lax.axis_index("ch")
    piece = lax.axis_index("ta")
    zl, core = piece // 2, piece % 2
    upper = ((block % layout.cols) >= layout.cols // 2).astype(jnp.int32)
    place0 = jnp.stack([zl, core, upper]).astype(jnp.int32)
    place1 = jnp.stack([zl, core, jnp.int32(1)]).astype(jnp.int32)

    normalized = normalize(raw_strain, band_index, filter_taps)
    swapped = lax.ppermute(normalized, AXES, layout.swap_columns())
    slots = gather_ring(layout, normalized)
    groups = [[2 * z + c for z in range(depth)] for c in range(2)]
    guest_rows = lax.all_to_all(
        swapped.reshape(depth, rows, length), "ta", 0, 0, axis_index_groups=groups
    )

    mine = []
    for d in range(1 - depth, depth):
        part = lax.dynamic_slice_in_dim(slots[d % ring][0], zl * rows, rows, 0)
        mine.append(jnp.stack([part[:, :EDGE], part[:, length - EDGE :]]))
    guest_edges = jnp.stack([guest_rows[:, :, :EDGE], guest_rows[:, :, length - EDGE :]], axis=1)
    edges = lax.ppermute(
        jnp.concatenate([jnp.stack(mine), guest_edges], axis=0), AXES, layout.swap_cores()
    )

    guest = 2 * depth - 1
    early = Job(ring, tuple(range(1, depth)), False, guest, False)
    late = Job(ring, (0,), False, guest, True)
    own = Job(ring, tuple(range(1, depth + 1)), True, depth - 1, True)
    acc = lagged(early, place0, edges, [guest_rows], slots, rows, scale)
    kept, sent = lagged(late, place0, edges, [guest_rows], slots, rows, scale, acc)
    result = kept + lax.ppermute(sent, AXES, layout.swap_cores())
    first = lax.ppermute(result, AXES, layout.swap_columns())
    kept, sent = lagged(own, place1, edges, [], slots, rows, scale)
    second = kept + lax.ppermute(sent, AXES, layout.swap_cores())
    return jnp.stack([first, second])


def solution(mesh):
    placed = (P("ch", "ta"), P("ch"), P())
    return jax.shard_map(
        on_device,
        mesh=mesh,
        in_specs=placed,
        out_specs=P(None, None, ("ch", "ta"), None),
        check_vma=False,
    )
```

time: 164 us -> 172 us (1.049)
  the two profiles are of different devices: /device:TPU:21 before, /device:TPU:48 now
where the time goes in v2:
time: 172 us; the launch traced here: 171 us
  starting transfers between devices  73.5 us (43%)
  waiting for transfers between devices  57.7 us (34%)
  Pallas kernels  24.6 us (14%)
  other arithmetic  11.6 us (7%)
  local copies, waits for them, and re-layouts  3.18 us (2%)
    ppermute x1, waiting for transfers between devices, on_device(): first = lax.ppermute(result, AXES, layout.swap_columns())  27.7 us
    pallas_call x3, Pallas kernels, lagged(): pl.pallas_call(functools.partial(lagged_kernel, job, rows, length, scale,...  24.6 us
    ppermute x3, starting transfers between devices, gather_ring(): up = lax.ppermute(up, AXES, layout.from_ring(1))  20.5 us
    ppermute x3, waiting for transfers between devices, gather_ring(): up = lax.ppermute(up, AXES, layout.from_ring(1))  19.2 us
    ppermute x3, starting transfers between devices, gather_ring(): down = lax.ppermute(down, AXES, layout.from_ring(-1))  17.1 us
    ppermute x1, waiting for transfers between devices, on_device(): swapped = lax.ppermute(normalized, AXES, layout.swap_columns())  9.63 us
    ppermute x2, starting transfers between devices, to_neighbours(): from_low = lax.ppermute(high_part, 'ta', forward)  8.47 us
    abs x1, other arithmetic, normalize(): magnitude = jnp.abs(filtered)  8 us
  transfers between devices with their start and end apart: 18, of which 5 were waited for; matrix products, arithmetic and copies ran while one was open for 1% of the time, Pallas kernels for 12%

profile of v2, /device:TPU:48, one launch (start us, length us, event | category | flops | bytes accessed | tf_op | source)
XLA Modules:
  0.0 171.3 jit_solution(8148897359273056536)
XLA Ops:
  2.3 3.0 %collective-permute-start = (f32[128,16]{1,0:T(8,128)S(1)}, f32[128,16]{1,0:T(8,128)S(1)}, u32[]{:S(2)}, u32[]{:S(2)}) collective-permute-start(f32[128,16]{1,0:T(8,128)S(1)} %get-tuple-element.15), channel_id=1, source_target_pairs={{0,1},{1,2},{2,3},{3,4},{4,5},{5,6},{6,7},{8,9},{9,10},{10,11},{11... | collective-permute-start | bytes 24584 | tf_op jit(solution)/shard_map/ppermute | solution.py:58
  7.0 8.0 %fusion.67 = (f32[128,1536]{1,0:T(8,128)S(1)}, f32[128,1536]{1,0:T(8,128)S(1)}) fusion(f32[128,1552]{1,0:T(8,128)S(1)} %constant_dynamic-update-slice_fusion, f32[128]{0:T(128)S(1)} %get-tuple-element.34, f32[128]{0:T(128)S(1)} %get-tuple-element.35, f32[128]{0:T(128)S(1)} %get-tuple-element.36, f32[128]{0:T(128)S(1)} %get-tuple-element.37, ...), kind=kLoop, calls=%fused_computation.190 | loop fusion | flops 16121856 | bytes 14967296 | tf_op jit(solution)/shard_map/abs | solution.py:78
  17.8 5.4 %collective-permute-start.2 = (f32[128,1536]{1,0:T(8,128)S(1)}, f32[128,1536]{1,0:T(8,128)}, u32[]{:S(2)}, u32[]{:S(2)}) collective-permute-start(f32[128,1536]{1,0:T(8,128)S(1)} %subtract_add_fusion), channel_id=1, source_target_pairs={{0,1},{1,2},{2,3},{3,4},{4,5},{5,6},{6,7},{8,9},{9,10},{10,11},{11... | collective-permute-start | bytes 2359304 | tf_op jit(solution)/shard_map/ppermute | solution.py:58
  25.8 13.3 %collective-permute-start.4 = (bf16[128,1536]{1,0:T(8,128)(2,1)S(1)}, bf16[128,1536]{1,0:T(8,128)(2,1)S(1)}, u32[]{:S(2)}, u32[]{:S(2)}) collective-permute-start(bf16[128,1536]{1,0:T(8,128)(2,1)S(1)} %divide_convert_fusion.refs_3_.refs_2_.refs_9_), channel_id=1, source_target_pairs={{262,0},{263,1},{270,8},{271,9},{278,16},{279,17},{286,24},{287,25... | collective-permute-start | bytes 1179656 | tf_op jit(solution)/shard_map/ppermute | solution.py:98
  39.1 3.8 %collective-permute-start.10 = (bf16[128,1536]{1,0:T(8,128)(2,1)S(1)}, bf16[128,1536]{1,0:T(8,128)(2,1)}, u32[]{:S(2)}, u32[]{:S(2)}) collective-permute-start(bf16[128,1536]{1,0:T(8,128)(2,1)S(1)} %divide_convert_fusion.refs_3_.refs_2_.refs_9_), channel_id=1, source_target_pairs={{128,0},{129,1},{136,8},{137,9},{144,16},{145,17},{152,24},{153,25... | collective-permute-start | bytes 1179656 | tf_op jit(solution)/shard_map/ppermute | solution.py:285
  42.9 8.6 %collective-permute-start.7 = (bf16[128,1536]{1,0:T(8,128)(2,1)S(1)}, bf16[128,1536]{1,0:T(8,128)(2,1)S(1)}, u32[]{:S(2)}, u32[]{:S(2)}) collective-permute-start(bf16[128,1536]{1,0:T(8,128)(2,1)S(1)} %divide_convert_fusion.refs_3_.refs_2_.refs_9_), channel_id=1, source_target_pairs={{2,0},{3,1},{10,8},{11,9},{18,16},{19,17},{26,24},{27,25},{34,32},... | collective-permute-start | bytes 1179656 | tf_op jit(solution)/shard_map/ppermute | solution.py:97
  51.5 1.9 %collective-permute-start.5 = (bf16[128,1536]{1,0:T(8,128)(2,1)S(1)}, bf16[128,1536]{1,0:T(8,128)(2,1)S(1)}, u32[]{:S(2)}, u32[]{:S(2)}) collective-permute-start(bf16[128,1536]{1,0:T(8,128)(2,1)S(1)} %collective-permute-done.4.refs_8_.refs_17_), channel_id=1, source_target_pairs={{262,0},{263,1},{270,8},{271,9},{278,16},{279,17},{286,24},{287,25... | collective-permute-start | bytes 1179656 | tf_op jit(solution)/shard_map/ppermute | solution.py:98
  53.5 9.6 %collective-permute-done.10 = bf16[128,1536]{1,0:T(8,128)(2,1)} collective-permute-done((bf16[128,1536]{1,0:T(8,128)(2,1)S(1)}, bf16[128,1536]{1,0:T(8,128)(2,1)}, u32[]{:S(2)}, u32[]{:S(2)}) %collective-permute-start.10) | collective-permute-done | bytes 393248 | tf_op jit(solution)/shard_map/ppermute | solution.py:285
  63.1 5.5 %all-to-all-start = ((bf16[4,32,1536]{2,1,0:T(8,128)(2,1)}), bf16[4,32,1536]{2,1,0:T(8,128)(2,1)S(1)}, u32[]{:S(2)}, u32[]{:S(2)}) async-start(bf16[4,32,1536]{2,1,0:T(8,128)(2,1)} %bitcast.61), calls=%async_computation | async-start | bytes 786432 | tf_op jit(solution)/shard_map/all_to_all | solution.py:288
  68.6 8.4 %collective-permute-start.8 = (bf16[128,1536]{1,0:T(8,128)(2,1)S(1)}, bf16[128,1536]{1,0:T(8,128)(2,1)S(1)}, u32[]{:S(2)}, u32[]{:S(2)}) collective-permute-start(bf16[128,1536]{1,0:T(8,128)(2,1)S(1)} %collective-permute-done.7.refs_3_.refs_10_), channel_id=1, source_target_pairs={{2,0},{3,1},{10,8},{11,9},{18,16},{19,17},{26,24},{27,25},{34,32},... | collective-permute-start | bytes 1179656 | tf_op jit(solution)/shard_map/ppermute | solution.py:97
  77.1 1.9 %collective-permute-start.6 = (bf16[128,1536]{1,0:T(8,128)(2,1)S(1)}, bf16[128,1536]{1,0:T(8,128)(2,1)S(1)}, u32[]{:S(2)}, u32[]{:S(2)}) collective-permute-start(bf16[128,1536]{1,0:T(8,128)(2,1)S(1)} %collective-permute-done.5.refs_7_.refs_16_), channel_id=1, source_target_pairs={{262,0},{263,1},{270,8},{271,9},{278,16},{279,17},{286,24},{287,25... | collective-permute-start | bytes 1179656 | tf_op jit(solution)/shard_map/ppermute | solution.py:98
  79.1 8.0 %collective-permute-done.8.refs_4_.refs_11_ = bf16[128,1536]{1,0:T(8,128)(2,1)S(1)} collective-permute-done((bf16[128,1536]{1,0:T(8,128)(2,1)S(1)}, bf16[128,1536]{1,0:T(8,128)(2,1)S(1)}, u32[]{:S(2)}, u32[]{:S(2)}) %collective-permute-start.8) | collective-permute-done | bytes 393248 | tf_op jit(solution)/shard_map/ppermute | solution.py:97
  87.1 3.5 %collective-permute-start.9 = (bf16[128,1536]{1,0:T(8,128)(2,1)S(1)}, bf16[128,1536]{1,0:T(8,128)(2,1)S(1)}, u32[]{:S(2)}, u32[]{:S(2)}) collective-permute-start(bf16[128,1536]{1,0:T(8,128)(2,1)S(1)} %collective-permute-done.8.refs_4_.refs_11_), channel_id=1, source_target_pairs={{2,0},{3,1},{10,8},{11,9},{18,16},{19,17},{26,24},{27,25},{34,32},... | collective-permute-start | bytes 1179656 | tf_op jit(solution)/shard_map/ppermute | solution.py:97
  90.7 11.2 %collective-permute-done.9.refs_5_.refs_12_ = bf16[128,1536]{1,0:T(8,128)(2,1)S(1)} collective-permute-done((bf16[128,1536]{1,0:T(8,128)(2,1)S(1)}, bf16[128,1536]{1,0:T(8,128)(2,1)S(1)}, u32[]{:S(2)}, u32[]{:S(2)}) %collective-permute-start.9) | collective-permute-done | bytes 393248 | tf_op jit(solution)/shard_map/ppermute | solution.py:97
  101.9 1.9 %collective-permute-start.11 = (bf16[11,2,32,128]{3,2,1,0:T(8,128)(2,1)S(1)}, bf16[11,2,32,128]{3,2,1,0:T(8,128)(2,1)S(1)}, u32[]{:S(2)}, u32[]{:S(2)}) collective-permute-start(bf16[11,2,32,128]{3,2,1,0:T(8,128)(2,1)S(1)} %maximum_dynamic-update-slice_fusion), channel_id=1, source_target_pairs={{1,0},{0,1},{9,8},{8,9},{17,16},{16,17},{25,24},{24,25},{33,32},{3... | collective-permute-start | bytes 540680 | tf_op jit(solution)/shard_map/ppermute | solution.py:297
  104.0 1.9 %collective-permute-start.12 = (bf16[64,1536]{1,0:T(8,128)(2,1)S(1)}, bf16[64,1536]{1,0:T(8,128)(2,1)S(1)}, u32[]{:S(2)}, u32[]{:S(2)}) collective-permute-start(bf16[64,1536]{1,0:T(8,128)(2,1)S(1)} %slice.468), channel_id=1, source_target_pairs={{2,0},{3,1},{10,8},{11,9},{18,16},{19,17},{26,24},{27,25},{34,32},... | collective-permute-start | bytes 589832 | tf_op jit(solution)/shard_map/ppermute | solution.py:103
  106.0 3.9 %collective-permute-start.13 = (bf16[64,1536]{1,0:T(8,128)(2,1)S(1)}, bf16[64,1536]{1,0:T(8,128)(2,1)S(1)}, u32[]{:S(2)}, u32[]{:S(2)}) collective-permute-start(bf16[64,1536]{1,0:T(8,128)(2,1)S(1)} %slice.469), channel_id=1, source_target_pairs={{262,0},{263,1},{270,8},{271,9},{278,16},{279,17},{286,24},{287,25... | collective-permute-start | bytes 589832 | tf_op jit(solution)/shard_map/ppermute | solution.py:104
  109.9 8.9 %lagged.3.refs_6_ = f32[1056,256]{1,0:T(8,128)S(1)} custom-call(s32[3]{0:T(128)S(1)} %pad_add_fusion.refs_0_, bf16[11,2,32,128]{3,2,1,0:T(8,128)(2,1)S(1)} %collective-permute-done.11.refs_1_, bf16[4,32,1536]{2,1,0:T(8,128)(2,1)S(1)} %all-to-all-done.refs_2_, bf16[128,1536]{1,0:T(8,128)(2,1)S(1)} %collective-permute-done.7.refs_3_.refs_10_, ...), custom_call_target="tpu_custom_call" | custom-call | flops 2491416576 | bytes 1179648 | tf_op jit(solution)/shard_map/lagged/pallas_call | solution.py:244
  118.9 3.5 %lagged.4 = (f32[65,16,128]{2,1,0:T(8,128)S(1)}, f32[65,16,128]{2,1,0:T(8,128)S(1)}) custom-call(s32[3]{0:T(128)S(1)} %pad_add_fusion.refs_0_, bf16[11,2,32,128]{3,2,1,0:T(8,128)(2,1)S(1)} %collective-permute-done.11.refs_1_, bf16[4,32,1536]{2,1,0:T(8,128)(2,1)S(1)} %all-to-all-done.refs_2_, ...), custom_call_target="tpu_custom_call" | custom-call | flops 830472192 | bytes 393216 | tf_op jit(solution)/shard_map/lagged/pallas_call | solution.py:244
  122.4 1.9 %collective-permute-start.14 = (f32[65,16,128]{2,1,0:T(8,128)S(1)}, f32[65,16,128]{2,1,0:T(8,128)S(1)}, u32[]{:S(2)}, u32[]{:S(2)}) collective-permute-start(f32[65,16,128]{2,1,0:T(8,128)S(1)} %get-tuple-element.10), channel_id=1, source_target_pairs={{1,0},{0,1},{9,8},{8,9},{17,16},{16,17},{25,24},{24,25},{33,32},{3... | collective-permute-start | bytes 1597448 | tf_op jit(solution)/shard_map/ppermute | solution.py:307
  124.3 12.2 %lagged.5 = (f32[65,16,128]{2,1,0:T(8,128)S(1)}, f32[65,16,128]{2,1,0:T(8,128)S(1)}) custom-call(s32[3]{0:T(128)S(1)} %pad_add_fusion.2.refs_0_, bf16[11,2,32,128]{3,2,1,0:T(8,128)(2,1)S(1)} %collective-permute-done.11.refs_1_, bf16[128,1536]{1,0:T(8,128)(2,1)S(1)} %divide_convert_fusion.refs_3_.refs_2_.refs_9_, ...), custom_call_target="tpu_custom_call" | custom-call | flops 3321888768 | bytes 1572864 | tf_op jit(solution)/shard_map/lagged/pallas_call | solution.py:244
  136.5 2.4 %collective-permute-start.16 = (f32[65,16,128]{2,1,0:T(8,128)S(1)}, f32[65,16,128]{2,1,0:T(8,128)S(1)}, u32[]{:S(2)}, u32[]{:S(2)}) collective-permute-start(f32[65,16,128]{2,1,0:T(8,128)S(1)} %get-tuple-element.12), channel_id=1, source_target_pairs={{1,0},{0,1},{9,8},{8,9},{17,16},{16,17},{25,24},{24,25},{33,32},{3... | collective-permute-start | bytes 1597448 | tf_op jit(solution)/shard_map/ppermute | solution.py:310
  139.0 3.4 %collective-permute-start.15 = (f32[65,16,128]{2,1,0:T(8,128)S(1)}, f32[65,16,128]{2,1,0:T(8,128)S(1)}, u32[]{:S(2)}, u32[]{:S(2)}) collective-permute-start(f32[65,16,128]{2,1,0:T(8,128)S(1)} %add.214), channel_id=1, source_target_pairs={{128,0},{129,1},{136,8},{137,9},{144,16},{145,17},{152,24},{153,25... | collective-permute-start | bytes 1597448 | tf_op jit(solution)/shard_map/ppermute | solution.py:308
  142.5 27.7 %collective-permute-done.15 = f32[65,16,128]{2,1,0:T(8,128)S(1)} collective-permute-done((f32[65,16,128]{2,1,0:T(8,128)S(1)}, f32[65,16,128]{2,1,0:T(8,128)S(1)}, u32[]{:S(2)}, u32[]{:S(2)}) %collective-permute-start.15) | collective-permute-done | bytes 532512 | tf_op jit(solution)/shard_map/ppermute | solution.py:308
  (62 shorter events, 10.7 us)
Async XLA Ops:
  0.0 6.6 %copy-start = (f32[4,33]{1,0:T(4,128)S(1)}, f32[4,33]{1,0:T(4,128)}, u32[]{:S(2)}) copy-start(f32[4,33]{1,0:T(4,128)} %param.5) | copy-start | bytes 1588
  0.0 6.9 %copy-start.1 = (f32[128,1536]{1,0:T(8,128)S(1)}, f32[128,1536]{1,0:T(8,128)}, u32[]{:S(2)}) copy-start(f32[128,1536]{1,0:T(8,128)} %param.3) | copy-start | bytes 2359300
  0.0 6.6 %copy-start.2 = (s32[128]{0:T(128)S(1)}, s32[128]{0:T(128)}, u32[]{:S(2)}) copy-start(s32[128]{0:T(128)} %param.4) | copy-start | bytes 1540
  1.0 5.9 %collective-permute-start.1 = (f32[128,16]{1,0:T(8,128)S(1)}, f32[128,16]{1,0:T(8,128)S(1)}, u32[]{:S(2)}, u32[]{:S(2)}) collective-permute-start(f32[128,16]{1,0:T(8,128)S(1)} %get-tuple-element.16), channel_id=1, source_target_pairs={{1,0},{2,1},{3,2},{4,3},{5,4},{6,5},{7,6},{9,8},{10,9},{11,10},{12... | collective-permute-start | bytes 24584 | tf_op jit(solution)/shard_map/ppermute | solution.py:59
  2.3 4.6 %collective-permute-start = (f32[128,16]{1,0:T(8,128)S(1)}, f32[128,16]{1,0:T(8,128)S(1)}, u32[]{:S(2)}, u32[]{:S(2)}) collective-permute-start(f32[128,16]{1,0:T(8,128)S(1)} %get-tuple-element.15), channel_id=1, source_target_pairs={{0,1},{1,2},{2,3},{3,4},{4,5},{5,6},{6,7},{8,9},{9,10},{10,11},{11... | collective-permute-start | bytes 24584 | tf_op jit(solution)/shard_map/ppermute | solution.py:58
  16.4 6.9 %collective-permute-start.3 = (f32[128,1536]{1,0:T(8,128)S(1)}, f32[128,1536]{1,0:T(8,128)S(1)}, u32[]{:S(2)}, u32[]{:S(2)}) collective-permute-start(f32[128,1536]{1,0:T(8,128)S(1)} %copy.10), channel_id=1, source_target_pairs={{1,0},{2,1},{3,2},{4,3},{5,4},{6,5},{7,6},{9,8},{10,9},{11,10},{12... | collective-permute-start | bytes 2359304 | tf_op jit(solution)/shard_map/ppermute | solution.py:59
  17.8 6.6 %collective-permute-start.2 = (f32[128,1536]{1,0:T(8,128)S(1)}, f32[128,1536]{1,0:T(8,128)}, u32[]{:S(2)}, u32[]{:S(2)}) collective-permute-start(f32[128,1536]{1,0:T(8,128)S(1)} %subtract_add_fusion), channel_id=1, source_target_pairs={{0,1},{1,2},{2,3},{3,4},{4,5},{5,6},{6,7},{8,9},{9,10},{10,11},{11... | collective-permute-start | bytes 2359304 | tf_op jit(solution)/shard_map/ppermute | solution.py:58
  25.8 25.7 %collective-permute-start.4 = (bf16[128,1536]{1,0:T(8,128)(2,1)S(1)}, bf16[128,1536]{1,0:T(8,128)(2,1)S(1)}, u32[]{:S(2)}, u32[]{:S(2)}) collective-permute-start(bf16[128,1536]{1,0:T(8,128)(2,1)S(1)} %divide_convert_fusion.refs_3_.refs_2_.refs_9_), channel_id=1, source_target_pairs={{262,0},{263,1},{270,8},{271,9},{278,16},{279,17},{286,24},{287,25... | collective-permute-start | bytes 1179656 | tf_op jit(solution)/shard_map/ppermute | solution.py:98
  39.1 24.0 %collective-permute-start.10 = (bf16[128,1536]{1,0:T(8,128)(2,1)S(1)}, bf16[128,1536]{1,0:T(8,128)(2,1)}, u32[]{:S(2)}, u32[]{:S(2)}) collective-permute-start(bf16[128,1536]{1,0:T(8,128)(2,1)S(1)} %divide_convert_fusion.refs_3_.refs_2_.refs_9_), channel_id=1, source_target_pairs={{128,0},{129,1},{136,8},{137,9},{144,16},{145,17},{152,24},{153,25... | collective-permute-start | bytes 1179656 | tf_op jit(solution)/shard_map/ppermute | solution.py:285
  42.9 25.7 %collective-permute-start.7 = (bf16[128,1536]{1,0:T(8,128)(2,1)S(1)}, bf16[128,1536]{1,0:T(8,128)(2,1)S(1)}, u32[]{:S(2)}, u32[]{:S(2)}) collective-permute-start(bf16[128,1536]{1,0:T(8,128)(2,1)S(1)} %divide_convert_fusion.refs_3_.refs_2_.refs_9_), channel_id=1, source_target_pairs={{2,0},{3,1},{10,8},{11,9},{18,16},{19,17},{26,24},{27,25},{34,32},... | collective-permute-start | bytes 1179656 | tf_op jit(solution)/shard_map/ppermute | solution.py:97
  51.5 25.6 %collective-permute-start.5 = (bf16[128,1536]{1,0:T(8,128)(2,1)S(1)}, bf16[128,1536]{1,0:T(8,128)(2,1)S(1)}, u32[]{:S(2)}, u32[]{:S(2)}) collective-permute-start(bf16[128,1536]{1,0:T(8,128)(2,1)S(1)} %collective-permute-done.4.refs_8_.refs_17_), channel_id=1, source_target_pairs={{262,0},{263,1},{270,8},{271,9},{278,16},{279,17},{286,24},{287,25... | collective-permute-start | bytes 1179656 | tf_op jit(solution)/shard_map/ppermute | solution.py:98
  63.1 27.5 %all-to-all-start = ((bf16[4,32,1536]{2,1,0:T(8,128)(2,1)}), bf16[4,32,1536]{2,1,0:T(8,128)(2,1)S(1)}, u32[]{:S(2)}, u32[]{:S(2)}) async-start(bf16[4,32,1536]{2,1,0:T(8,128)(2,1)} %bitcast.61), calls=%async_computation | async-start | bytes 786432 | tf_op jit(solution)/shard_map/all_to_all | solution.py:288
  68.6 18.5 %collective-permute-start.8 = (bf16[128,1536]{1,0:T(8,128)(2,1)S(1)}, bf16[128,1536]{1,0:T(8,128)(2,1)S(1)}, u32[]{:S(2)}, u32[]{:S(2)}) collective-permute-start(bf16[128,1536]{1,0:T(8,128)(2,1)S(1)} %collective-permute-done.7.refs_3_.refs_10_), channel_id=1, source_target_pairs={{2,0},{3,1},{10,8},{11,9},{18,16},{19,17},{26,24},{27,25},{34,32},... | collective-permute-start | bytes 1179656 | tf_op jit(solution)/shard_map/ppermute | solution.py:97
  77.1 13.5 %collective-permute-start.6 = (bf16[128,1536]{1,0:T(8,128)(2,1)S(1)}, bf16[128,1536]{1,0:T(8,128)(2,1)S(1)}, u32[]{:S(2)}, u32[]{:S(2)}) collective-permute-start(bf16[128,1536]{1,0:T(8,128)(2,1)S(1)} %collective-permute-done.5.refs_7_.refs_16_), channel_id=1, source_target_pairs={{262,0},{263,1},{270,8},{271,9},{278,16},{279,17},{286,24},{287,25... | collective-permute-start | bytes 1179656 | tf_op jit(solution)/shard_map/ppermute | solution.py:98
  87.1 14.8 %collective-permute-start.9 = (bf16[128,1536]{1,0:T(8,128)(2,1)S(1)}, bf16[128,1536]{1,0:T(8,128)(2,1)S(1)}, u32[]{:S(2)}, u32[]{:S(2)}) collective-permute-start(bf16[128,1536]{1,0:T(8,128)(2,1)S(1)} %collective-permute-done.8.refs_4_.refs_11_), channel_id=1, source_target_pairs={{2,0},{3,1},{10,8},{11,9},{18,16},{19,17},{26,24},{27,25},{34,32},... | collective-permute-start | bytes 1179656 | tf_op jit(solution)/shard_map/ppermute | solution.py:97
  101.9 8.0 %collective-permute-start.11 = (bf16[11,2,32,128]{3,2,1,0:T(8,128)(2,1)S(1)}, bf16[11,2,32,128]{3,2,1,0:T(8,128)(2,1)S(1)}, u32[]{:S(2)}, u32[]{:S(2)}) collective-permute-start(bf16[11,2,32,128]{3,2,1,0:T(8,128)(2,1)S(1)} %maximum_dynamic-update-slice_fusion), channel_id=1, source_target_pairs={{1,0},{0,1},{9,8},{8,9},{17,16},{16,17},{25,24},{24,25},{33,32},{3... | collective-permute-start | bytes 540680 | tf_op jit(solution)/shard_map/ppermute | solution.py:297
  104.0 14.8 %collective-permute-start.12 = (bf16[64,1536]{1,0:T(8,128)(2,1)S(1)}, bf16[64,1536]{1,0:T(8,128)(2,1)S(1)}, u32[]{:S(2)}, u32[]{:S(2)}) collective-permute-start(bf16[64,1536]{1,0:T(8,128)(2,1)S(1)} %slice.468), channel_id=1, source_target_pairs={{2,0},{3,1},{10,8},{11,9},{18,16},{19,17},{26,24},{27,25},{34,32},... | collective-permute-start | bytes 589832 | tf_op jit(solution)/shard_map/ppermute | solution.py:103
  106.0 12.9 %collective-permute-start.13 = (bf16[64,1536]{1,0:T(8,128)(2,1)S(1)}, bf16[64,1536]{1,0:T(8,128)(2,1)S(1)}, u32[]{:S(2)}, u32[]{:S(2)}) collective-permute-start(bf16[64,1536]{1,0:T(8,128)(2,1)S(1)} %slice.469), channel_id=1, source_target_pairs={{262,0},{263,1},{270,8},{271,9},{278,16},{279,17},{286,24},{287,25... | collective-permute-start | bytes 589832 | tf_op jit(solution)/shard_map/ppermute | solution.py:104
  122.4 16.6 %collective-permute-start.14 = (f32[65,16,128]{2,1,0:T(8,128)S(1)}, f32[65,16,128]{2,1,0:T(8,128)S(1)}, u32[]{:S(2)}, u32[]{:S(2)}) collective-permute-start(f32[65,16,128]{2,1,0:T(8,128)S(1)} %get-tuple-element.10), channel_id=1, source_target_pairs={{1,0},{0,1},{9,8},{8,9},{17,16},{16,17},{25,24},{24,25},{33,32},{3... | collective-permute-start | bytes 1597448 | tf_op jit(solution)/shard_map/ppermute | solution.py:307
  136.5 5.9 %collective-permute-start.16 = (f32[65,16,128]{2,1,0:T(8,128)S(1)}, f32[65,16,128]{2,1,0:T(8,128)S(1)}, u32[]{:S(2)}, u32[]{:S(2)}) collective-permute-start(f32[65,16,128]{2,1,0:T(8,128)S(1)} %get-tuple-element.12), channel_id=1, source_target_pairs={{1,0},{0,1},{9,8},{8,9},{17,16},{16,17},{25,24},{24,25},{33,32},{3... | collective-permute-start | bytes 1597448 | tf_op jit(solution)/shard_map/ppermute | solution.py:310
  139.0 31.2 %collective-permute-start.15 = (f32[65,16,128]{2,1,0:T(8,128)S(1)}, f32[65,16,128]{2,1,0:T(8,128)S(1)}, u32[]{:S(2)}, u32[]{:S(2)}) collective-permute-start(f32[65,16,128]{2,1,0:T(8,128)S(1)} %add.214), channel_id=1, source_target_pairs={{128,0},{129,1},{136,8},{137,9},{144,16},{145,17},{152,24},{153,25... | collective-permute-start | bytes 1597448 | tf_op jit(solution)/shard_map/ppermute | solution.py:308

commit v3 on v0

v3 whole, which is shorter than its diff:
```python
import functools
import math

import jax
import jax.numpy as jnp
from jax import lax
from jax.experimental import pallas as pl
from jax.experimental.pallas import tpu as pltpu
from jax.sharding import Mesh
from jax.sharding import PartitionSpec as P

HF = 16
TAPS = 33
NBANDS = 4
LAGH = 32
LAGS = 65
PAIRS = LAGH + 1
LANES = 128
CHUNK = 64


def to_neighbours(low_part, high_part):
    count = lax.axis_size("ta")
    forward = [(i, i + 1) for i in range(count - 1)]
    backward = [(i + 1, i) for i in range(count - 1)]
    from_low = lax.ppermute(high_part, "ta", forward)
    from_high = lax.ppermute(low_part, "ta", backward)
    return from_low, from_high


def filter_kernel(
    taps_ref, band_ref, raw_ref, low_ref, high_ref, out_ref, prefix_ref, suffix_ref, tall, wide, coeff
):
    channels, length = raw_ref.shape
    tiles = length // LANES
    tall[:HF] = low_ref[...]
    tall[HF + length :] = high_ref[...]
    for i in range(tiles):
        tall[HF + i * LANES : HF + (i + 1) * LANES] = raw_ref[:, i * LANES : (i + 1) * LANES].T
    band = jnp.broadcast_to(band_ref[...], (8, channels))
    for k in range(TAPS):
        value = jnp.full((8, channels), taps_ref[NBANDS - 1, k])
        for b in range(NBANDS - 1):
            value = jnp.where(band == b, taps_ref[b, k], value)
        coeff[k] = value

    def chunk(i, carry):
        base = pl.multiple_of(i * CHUNK, CHUNK)
        total = jnp.zeros((CHUNK, channels), jnp.float32)
        for k in range(TAPS):
            factor = jnp.broadcast_to(coeff[k][None], (CHUNK // 8, 8, channels))
            total = total + factor.reshape(CHUNK, channels) * tall[pl.ds(base + k, CHUNK), :]
        wide[pl.ds(base, CHUNK), :] = total
        return carry

    lax.fori_loop(0, length // CHUNK, chunk, 0)
    inner = jnp.zeros((channels, LANES), jnp.float32)
    for r in range(tiles):
        piece = wide[pl.ds(r, LANES, stride=tiles), :].T
        cols = slice(r * LANES, (r + 1) * LANES)
        out_ref[:, cols] = piece
        inner = inner + jnp.abs(piece)
        prefix_ref[:, cols] = inner
    row = lax.broadcasted_iota(jnp.int32, (LANES, LANES), 0)
    col = lax.broadcasted_iota(jnp.int32, (LANES, LANES), 1)
    before = jnp.dot(
        inner,
        (row < col).astype(jnp.float32),
        precision=lax.Precision.HIGHEST,
        preferred_element_type=jnp.float32,
    )
    total = (before + inner)[:, LANES - 1 :]
    for r in range(tiles):
        cols = slice(r * LANES, (r + 1) * LANES)
        prefix = prefix_ref[:, cols] + before
        prefix_ref[:, cols] = prefix
        suffix_ref[:, cols] = (total - prefix) + jnp.abs(out_ref[:, cols])


def filtered_sums(raw, band_index, filter_taps):
    channels, length = raw.shape
    low, high = to_neighbours(raw[:, :HF].T, raw[:, length - HF :].T)
    shape = jax.ShapeDtypeStruct((channels, length), jnp.float32)
    vmem = pl.BlockSpec(memory_space=pltpu.VMEM)
    return pl.pallas_call(
        filter_kernel,
        out_shape=(shape,) * 3,
        in_specs=[pl.BlockSpec(memory_space=pltpu.SMEM)] + [vmem] * 4,
        out_specs=(vmem,) * 3,
        scratch_shapes=[
            pltpu.VMEM((length + 2 * HF, channels), jnp.float32),
            pltpu.VMEM((length, channels), jnp.float32),
            pltpu.VMEM((TAPS, 8, channels), jnp.float32),
        ],
        compiler_params=pltpu.CompilerParams(vmem_limit_bytes=24 * 1024 * 1024),
        name="filter",
    )(filter_taps, band_index[None, :], raw, low, high)


def normalize(raw, band_index, filter_taps):
    channels, length = raw.shape
    tiles = length // LANES
    whole_len = length * lax.axis_size("ta")
    filtered, prefix, suffix = filtered_sums(raw, band_index, filter_taps)
    before, after = to_neighbours(prefix, suffix)
    window_sum = before + prefix[:, length - 1 :] + after
    at = jnp.arange(length, dtype=jnp.int32)
    local_time = tiles * (at % LANES) + at // LANES
    global_time = lax.axis_index("ta") * length + local_time
    upper = jnp.minimum(global_time + length, whole_len - 1) + 1
    lower = jnp.maximum(global_time - length, 0)
    counted = (upper - lower).astype(jnp.float32)
    level = window_sum / counted[None, :]
    return (filtered / (level + 1e-06)).astype(jnp.bfloat16)


def lagged_kernel(
    count, scale, place_ref, own_ref, left_ref, right_ref, part_ref, out_ref, fan, both, carry, acc
):
    step = pl.program_id(0)
    rows = own_ref.shape[1]
    channels, length = part_ref.shape[1:]
    tiles = length // LANES
    reach = -(-LAGH // tiles)
    lead = reach * tiles + LAGH

    @pl.when(step == 0)
    def _():
        acc[...] = jnp.zeros_like(acc)
        carry[...] = jnp.zeros_like(carry)

    lane = lax.broadcasted_iota(jnp.int32, (rows, length), 1) % LANES
    inside = own_ref[0].astype(jnp.float32)
    left = jnp.where(step > 0, left_ref[0].astype(jnp.float32), 0.0)
    right = jnp.where(step < count - 1, right_ref[0].astype(jnp.float32), 0.0)
    for j in range(-reach, reach + 1):
        if j < 0:
            mixed = jnp.where(lane >= LANES + j, left, inside)
        else:
            mixed = jnp.where(lane < j, right, inside)
        for r in range(tiles):
            tile = mixed[:, r * LANES : (r + 1) * LANES]
            if j != 0:
                tile = pltpu.roll(tile, (-j) % LANES, 1)
            at = (j + reach) * tiles + r
            fan[:, at * LANES : (at + 1) * LANES] = tile.astype(jnp.bfloat16)

    both[:channels] = part_ref[0]
    both[channels:, LANES:] = part_ref[0, :, : length - LANES]
    final = part_ref[0, :, length - LANES :].astype(jnp.float32)
    part_lane = lax.broadcasted_iota(jnp.int32, (channels, LANES), 1)
    late = pltpu.roll(jnp.where(part_lane == LANES - 1, carry[...], final), 1, 1)
    both[channels:, :LANES] = late.astype(jnp.bfloat16)
    carry[...] = final

    def moved(width, offset):
        return jnp.concatenate(
            [
                fan[:, (lead - 2 * a + offset) * LANES : (lead - 2 * a + offset + width) * LANES]
                for a in range(PAIRS)
            ],
            axis=0,
        )

    acc[...] += lax.dot_general(
        moved(tiles, 0), both[...], (((1,), (1,)), ((), ())), preferred_element_type=jnp.float32
    )

    @pl.when(step == count - 1)
    def _():
        tail = jnp.where(part_lane == LANES - 1, final, 0.0).astype(jnp.bfloat16)
        acc[:, channels:] += lax.dot_general(
            moved(1, tiles), tail, (((1,), (1,)), ((), ())), preferred_element_type=jnp.float32
        )
        for a in range(PAIRS):
            block = acc[a * rows : (a + 1) * rows] * scale
            out_ref[2 * a] = block[:, :channels].astype(out_ref.dtype)
            if a > 0:
                out_ref[2 * a - 1] = block[:, channels:].astype(out_ref.dtype)


def lagged(place, own_rows, partner, rows, count, scale, out_dtype=jnp.float32):
    channels, length = partner.shape[1:]
    tiles = length // LANES
    fan_tiles = (2 * -(-LAGH // tiles) + 1) * tiles
    row_block = (1, rows, length)
    spec = pltpu.PrefetchScalarGridSpec(
        num_scalar_prefetch=1,
        grid=(count,),
        in_specs=[
            pl.BlockSpec(row_block, lambda t, p: (p[0] + t, p[1], 0)),
            pl.BlockSpec(row_block, lambda t, p: (p[0] + jnp.maximum(t - 1, 0), p[1], 0)),
            pl.BlockSpec(row_block, lambda t, p: (p[0] + jnp.minimum(t + 1, count - 1), p[1], 0)),
            pl.BlockSpec((1, channels, length), lambda t, p: (p[2] + t, 0, 0)),
        ],
        out_specs=pl.BlockSpec((LAGS, rows, channels), lambda t, p: (0, 0, 0)),
        scratch_shapes=[
            pltpu.VMEM((rows, fan_tiles * LANES), jnp.bfloat16),
            pltpu.VMEM((2 * channels, length), jnp.bfloat16),
            pltpu.VMEM((channels, LANES), jnp.float32),
            pltpu.VMEM((PAIRS * rows, 2 * channels), jnp.float32),
        ],
    )
    return pl.pallas_call(
        functools.partial(lagged_kernel, count, scale),
        out_shape=jax.ShapeDtypeStruct((LAGS, rows, channels), out_dtype),
        grid_spec=spec,
        compiler_params=pltpu.CompilerParams(vmem_limit_bytes=24 * 1024 * 1024),
        cost_estimate=pl.CostEstimate(
            flops=4 * count * PAIRS * rows * channels * length,
            bytes_accessed=2 * count * channels * length,
            transcendentals=0,
        ),
        name="lagged",
    )(place, own_rows, own_rows, own_rows, partner)


def on_device(raw_strain, band_index, filter_taps):
    channels, length = raw_strain.shape
    count = lax.axis_size("ta")
    rows = channels // count
    scale = 1.0 / math.sqrt(length * count)
    swap = [(0, 1), (1, 0)]
    half, upper, piece = lax.axis_index("zh"), lax.axis_index("cp"), lax.axis_index("ta")

    normalized = normalize(raw_strain, band_index, filter_taps)
    ring = lax.all_gather(normalized, ("zh", "ta"), axis=0, tiled=False)
    guest = lax.ppermute(normalized, "cp", swap)
    guest = lax.all_to_all(guest.reshape(count, rows, length), "ta", 0, 0)

    other = (1 - half) * count
    near = jnp.where(upper == 1, other, half * count)
    place0 = jnp.stack([0 * piece, 0 * piece, near]).astype(jnp.int32)
    place1 = jnp.stack([half * count, piece, other]).astype(jnp.int32)
    first = lagged(place0, guest, ring, rows, count, scale)
    first = lax.ppermute(first, "cp", swap)
    second = lagged(place1, ring, ring, rows, count, scale)
    return jnp.stack([first, second])


def solution(mesh):
    blocks, slices = mesh.devices.shape
    axes = ("zh", "cp", "col", "ta")
    parts = Mesh(mesh.devices.reshape(2, 2, blocks // 4, slices), axes)
    channel_axes = axes[:3]
    return jax.shard_map(
        on_device,
        mesh=parts,
        in_specs=(P(channel_axes, "ta"), P(channel_axes), P()),
        out_specs=P(None, None, axes, None),
        check_vma=False,
    )
```

time: 586 us -> 151 us (0.26)
  the two profiles are of different devices: /device:TPU:18 before, /device:TPU:17 now
where the time goes in v3:
time: 151 us; the launch traced here: 150 us
  waiting for transfers between devices  73 us (48%)
  starting transfers between devices  37.3 us (25%)
  Pallas kernels  16.8 us (11%)
  between operations  13.5 us (9%)
  local copies, waits for them, and re-layouts  6.55 us (4%)
  other arithmetic  3.28 us (2%)
    ppermute x1, waiting for transfers between devices, on_device(): first = lax.ppermute(first, 'cp', swap)  19.2 us
    all_gather x1, waiting for transfers between devices, on_device(): ring = lax.all_gather(normalized, ('zh', 'ta'), axis=0, tiled=False)  16.2 us
    all_to_all x1, starting transfers between devices, on_device(): guest = lax.all_to_all(guest.reshape(count, rows, length), 'ta', 0, 0)  15.5 us
    all_to_all x1, waiting for transfers between devices, on_device(): guest = lax.all_to_all(guest.reshape(count, rows, length), 'ta', 0, 0)  14.6 us
    pallas_call x2, Pallas kernels, lagged(): pl.pallas_call(functools.partial(lagged_kernel, count, scale), out_shape=...  13.2 us
    ppermute x1, waiting for transfers between devices, on_device(): guest = lax.ppermute(normalized, 'cp', swap)  8.45 us
    ppermute x2, waiting for transfers between devices, to_neighbours(): from_high = lax.ppermute(low_part, 'ta', backward)  8.2 us
    ppermute x2, starting transfers between devices, to_neighbours(): from_low = lax.ppermute(high_part, 'ta', forward)  6.57 us
  transfers between devices with their start and end apart: 8, of which 7 were waited for; matrix products, arithmetic and copies ran while one was open for 0% of the time, Pallas kernels for 4%

profile of v3, /device:TPU:17, one launch (start us, length us, event | category | flops | bytes accessed | tf_op | source)
XLA Modules:
  0.0 150.5 jit_solution(15702498645472775789)
XLA Ops:
  6.5 1.0 fusion.10
  7.5 4.6 %collective-permute-start = (f32[16,128]{1,0:T(8,128)S(1)}, f32[16,128]{1,0:T(8,128)S(1)}, u32[]{:S(2)}, u32[]{:S(2)}) collective-permute-start(f32[16,128]{1,0:T(8,128)S(1)} %bitcast.19), channel_id=1, source_target_pairs={{0,1},{1,2},{2,3},{3,4},{4,5},{5,6},{6,7},{8,9},{9,10},{10,11},{11... | collective-permute-start | bytes 24584 | tf_op jit(solution)/shard_map/ppermute | solution.py:26
  12.2 1.9 %collective-permute-start.1 = (f32[16,128]{1,0:T(8,128)S(1)}, f32[16,128]{1,0:T(8,128)S(1)}, u32[]{:S(2)}, u32[]{:S(2)}) collective-permute-start(f32[16,128]{1,0:T(8,128)S(1)} %bitcast.20), channel_id=1, source_target_pairs={{1,0},{2,1},{3,2},{4,3},{5,4},{6,5},{7,6},{9,8},{10,9},{11,10},{12... | collective-permute-start | bytes 24584 | tf_op jit(solution)/shard_map/ppermute | solution.py:27
  14.1 3.0 %collective-permute-done.1.high_ref = f32[16,128]{1,0:T(8,128)S(1)} collective-permute-done((f32[16,128]{1,0:T(8,128)S(1)}, f32[16,128]{1,0:T(8,128)S(1)}, u32[]{:S(2)}, u32[]{:S(2)}) %collective-permute-start.1) | collective-permute-done | bytes 8224 | tf_op jit(solution)/shard_map/ppermute | solution.py:27
  17.2 1.1 copy-done.2
  18.3 0.7 copy-done.3
  19.0 0.7 copy-done.4
  19.6 3.6 %filter.1 = (f32[128,1536]{1,0:T(8,128)S(1)}, f32[128,1536]{1,0:T(8,128)S(1)}, f32[128,1536]{1,0:T(8,128)S(1)}) custom-call(f32[4,33]{1,0:T(4,128)S(1)} %copy-done.3, s32[1,128]{1,0:T(1,128)S(1)} %bitcast.17, f32[128,1536]{1,0:T(8,128)S(1)} %copy-done.2, f32[16,128]{1,0:T(8,128)S(1)} %collective-permute-done.low_ref, ...), custom_call_target="tpu_custom_call" | custom-call | tf_op jit(solution)/shard_map/filter/pallas_call | solution.py:85
  23.3 2.0 %collective-permute-start.2 = (f32[128,1536]{1,0:T(8,128)S(1)}, f32[128,1536]{1,0:T(8,128)S(1)}, u32[]{:S(2)}, u32[]{:S(2)}) collective-permute-start(f32[128,1536]{1,0:T(8,128)S(1)} %get-tuple-element.9), channel_id=1, source_target_pairs={{0,1},{1,2},{2,3},{3,4},{4,5},{5,6},{6,7},{8,9},{9,10},{10,11},{11... | collective-permute-start | bytes 2359304 | tf_op jit(solution)/shard_map/ppermute | solution.py:26
  25.3 2.4 %collective-permute-start.3 = (f32[128,1536]{1,0:T(8,128)S(1)}, f32[128,1536]{1,0:T(8,128)}, u32[]{:S(2)}, u32[]{:S(2)}) collective-permute-start(f32[128,1536]{1,0:T(8,128)S(1)} %get-tuple-element.10), channel_id=1, source_target_pairs={{1,0},{2,1},{3,2},{4,3},{5,4},{6,5},{7,6},{9,8},{10,9},{11,10},{12... | collective-permute-start | bytes 2359304 | tf_op jit(solution)/shard_map/ppermute | solution.py:27
  27.9 6.3 %collective-permute-done.2 = f32[128,1536]{1,0:T(8,128)S(1)} collective-permute-done((f32[128,1536]{1,0:T(8,128)S(1)}, f32[128,1536]{1,0:T(8,128)S(1)}, u32[]{:S(2)}, u32[]{:S(2)}) %collective-permute-start.2) | collective-permute-done | bytes 786464 | tf_op jit(solution)/shard_map/ppermute | solution.py:26
  34.2 5.2 %collective-permute-done.3 = f32[128,1536]{1,0:T(8,128)} collective-permute-done((f32[128,1536]{1,0:T(8,128)S(1)}, f32[128,1536]{1,0:T(8,128)}, u32[]{:S(2)}, u32[]{:S(2)}) %collective-permute-start.3) | collective-permute-done | bytes 786464 | tf_op jit(solution)/shard_map/ppermute | solution.py:27
  39.4 2.1 %divide_convert_fusion = bf16[128,1536]{1,0:T(8,128)(2,1)} fusion(f32[128,1536]{1,0:T(8,128)S(1)} %get-tuple-element.8, f32[128,1536]{1,0:T(8,128)} %collective-permute-done.3, f32[128,1536]{1,0:T(8,128)S(1)} %collective-permute-done.2, f32[1536]{0:T(1024)S(1)} %subtract_convert_fusion, f32[128]{0:T(128)S(1)} %slice_reduce_fusion), kind=kLoop, calls=%fused_computation.1 | loop fusion | flops 1179648 | bytes 2759168 | tf_op jit(solution)/shard_map/convert_element_type | solution.py:114
  41.5 5.7 %collective-permute-start.4 = (bf16[128,1536]{1,0:T(8,128)(2,1)}, bf16[128,1536]{1,0:T(8,128)(2,1)}, u32[]{:S(2)}, u32[]{:S(2)}) collective-permute-start(bf16[128,1536]{1,0:T(8,128)(2,1)} %divide_convert_fusion), channel_id=1, source_target_pairs={{0,128},{128,0},{1,129},{129,1},{2,130},{130,2},{3,131},{131,3},{4... | collective-permute-start | bytes 1179656 | tf_op jit(solution)/shard_map/ppermute | solution.py:228
  47.2 8.5 %collective-permute-done.4 = bf16[128,1536]{1,0:T(8,128)(2,1)} collective-permute-done((bf16[128,1536]{1,0:T(8,128)(2,1)}, bf16[128,1536]{1,0:T(8,128)(2,1)}, u32[]{:S(2)}, u32[]{:S(2)}) %collective-permute-start.4) | collective-permute-done | bytes 393248 | tf_op jit(solution)/shard_map/ppermute | solution.py:228
  55.7 15.5 %all-to-all-start = ((bf16[8,16,1536]{2,1,0:T(8,128)(2,1)}), bf16[8,16,1536]{2,1,0:T(8,128)(2,1)S(1)}, u32[]{:S(2)}, u32[]{:S(2)}) async-start(bf16[8,16,1536]{2,1,0:T(8,128)(2,1)} %bitcast.4), calls=%async_computation | async-start | bytes 786432 | tf_op jit(solution)/shard_map/all_to_all | solution.py:229
  71.2 14.6 %all-to-all-done.own_ref.left_ref.right_ref = bf16[8,16,1536]{2,1,0:T(8,128)(2,1)S(1)} async-done(((bf16[8,16,1536]{2,1,0:T(8,128)(2,1)}), bf16[8,16,1536]{2,1,0:T(8,128)(2,1)S(1)}, u32[]{:S(2)}, u32[]{:S(2)}) %all-to-all-start) | async-done | bytes 393248 | tf_op jit(solution)/shard_map/all_to_all | solution.py:229
  85.8 16.2 %all-gather.3.cloned.1.call-done = bf16[2048,1536]{1,0:T(8,128)(2,1)} async-done(((bf16[128,1536]{1,0:T(8,128)(2,1)}), bf16[2048,1536]{1,0:T(8,128)(2,1)}) %all-gather.3.cloned.1.call-update) | async-done | bytes 6291472 | tf_op jit(solution)/shard_map/all_gather | solution.py:227
  102.0 2.8 %copy-done = bf16[2048,1536]{1,0:T(8,128)(2,1)S(1)} copy-done((bf16[2048,1536]{1,0:T(8,128)(2,1)S(1)}, bf16[2048,1536]{1,0:T(8,128)(2,1)}, u32[]{:S(2)}) %copy-start) | copy-done | bytes 6291480
  104.8 6.5 %lagged.2 = f32[65,16,128]{2,1,0:T(8,128)S(1)} custom-call(s32[3]{0:T(128)S(1)} %stack.28.place_ref, bf16[8,16,1536]{2,1,0:T(8,128)(2,1)S(1)} %all-to-all-done.own_ref.left_ref.right_ref, bf16[8,16,1536]{2,1,0:T(8,128)(2,1)S(1)} %all-to-all-done.own_ref.left_ref.right_ref, bf16[8,16,1536]{2,1,0:T(8,128)(2,1)S(1)} %all-to-all-done.own_ref.left_ref.right_ref, ...), custom_call_target="tpu_custom_call" | custom-call | flops 3321888768 | bytes 3145728 | tf_op jit(solution)/shard_map/lagged/pallas_call | solution.py:204
  111.4 5.3 %collective-permute-start.5 = (f32[65,16,128]{2,1,0:T(8,128)S(1)}, f32[65,16,128]{2,1,0:T(8,128)S(1)}, u32[]{:S(2)}, u32[]{:S(2)}) collective-permute-start(f32[65,16,128]{2,1,0:T(8,128)S(1)} %lagged.2), channel_id=1, source_target_pairs={{0,128},{128,0},{1,129},{129,1},{2,130},{130,2},{3,131},{131,3},{4... | collective-permute-start | bytes 1597448 | tf_op jit(solution)/shard_map/ppermute | solution.py:236
  116.7 6.6 %lagged.3 = f32[65,16,128]{2,1,0:T(8,128)S(1)} custom-call(s32[3]{0:T(128)S(1)} %pad_add_fusion.place_ref, bf16[16,128,1536]{2,1,0:T(8,128)(2,1)S(1)} %bitcast.12, bf16[16,128,1536]{2,1,0:T(8,128)(2,1)S(1)} %bitcast.13, bf16[16,128,1536]{2,1,0:T(8,128)(2,1)S(1)} %bitcast.14, bf16[16,128,1536]{2,1,0:T(8,128)(2,1)S(1)} %bitcast.15), custom_call_target="tpu_custom_call" | custom-call | flops 3321888768 | bytes 3145728 | tf_op jit(solution)/shard_map/lagged/pallas_call | solution.py:204
  123.4 19.2 %collective-permute-done.5 = f32[65,16,128]{2,1,0:T(8,128)S(1)} collective-permute-done((f32[65,16,128]{2,1,0:T(8,128)S(1)}, f32[65,16,128]{2,1,0:T(8,128)S(1)}, u32[]{:S(2)}, u32[]{:S(2)}) %collective-permute-start.5) | collective-permute-done | bytes 532512 | tf_op jit(solution)/shard_map/ppermute | solution.py:236
  142.6 1.0 pad_maximum_fusion
  (15 shorter events, 0.5 us)
Async XLA Ops:
  6.5 95.5 %all-gather.3.cloned.1.call-start = ((), (), s32[]{:S(2)}) async-start(), calls=%async_computation.1 | async-start | bytes 6684672 | tf_op jit(solution)/shard_map/all_gather | solution.py:227
  7.5 6.6 %collective-permute-start = (f32[16,128]{1,0:T(8,128)S(1)}, f32[16,128]{1,0:T(8,128)S(1)}, u32[]{:S(2)}, u32[]{:S(2)}) collective-permute-start(f32[16,128]{1,0:T(8,128)S(1)} %bitcast.19), channel_id=1, source_target_pairs={{0,1},{1,2},{2,3},{3,4},{4,5},{5,6},{6,7},{8,9},{9,10},{10,11},{11... | collective-permute-start | bytes 24584 | tf_op jit(solution)/shard_map/ppermute | solution.py:26
  12.2 5.0 %collective-permute-start.1 = (f32[16,128]{1,0:T(8,128)S(1)}, f32[16,128]{1,0:T(8,128)S(1)}, u32[]{:S(2)}, u32[]{:S(2)}) collective-permute-start(f32[16,128]{1,0:T(8,128)S(1)} %bitcast.20), channel_id=1, source_target_pairs={{1,0},{2,1},{3,2},{4,3},{5,4},{6,5},{7,6},{9,8},{10,9},{11,10},{12... | collective-permute-start | bytes 24584 | tf_op jit(solution)/shard_map/ppermute | solution.py:27
  17.2 1.1 copy-start.2
  18.3 0.7 copy-start.3
  19.0 0.7 copy-start.4
  23.3 10.9 %collective-permute-start.2 = (f32[128,1536]{1,0:T(8,128)S(1)}, f32[128,1536]{1,0:T(8,128)S(1)}, u32[]{:S(2)}, u32[]{:S(2)}) collective-permute-start(f32[128,1536]{1,0:T(8,128)S(1)} %get-tuple-element.9), channel_id=1, source_target_pairs={{0,1},{1,2},{2,3},{3,4},{4,5},{5,6},{6,7},{8,9},{9,10},{10,11},{11... | collective-permute-start | bytes 2359304 | tf_op jit(solution)/shard_map/ppermute | solution.py:26
  25.3 14.1 %collective-permute-start.3 = (f32[128,1536]{1,0:T(8,128)S(1)}, f32[128,1536]{1,0:T(8,128)}, u32[]{:S(2)}, u32[]{:S(2)}) collective-permute-start(f32[128,1536]{1,0:T(8,128)S(1)} %get-tuple-element.10), channel_id=1, source_target_pairs={{1,0},{2,1},{3,2},{4,3},{5,4},{6,5},{7,6},{9,8},{10,9},{11,10},{12... | collective-permute-start | bytes 2359304 | tf_op jit(solution)/shard_map/ppermute | solution.py:27
  41.5 14.1 %collective-permute-start.4 = (bf16[128,1536]{1,0:T(8,128)(2,1)}, bf16[128,1536]{1,0:T(8,128)(2,1)}, u32[]{:S(2)}, u32[]{:S(2)}) collective-permute-start(bf16[128,1536]{1,0:T(8,128)(2,1)} %divide_convert_fusion), channel_id=1, source_target_pairs={{0,128},{128,0},{1,129},{129,1},{2,130},{130,2},{3,131},{131,3},{4... | collective-permute-start | bytes 1179656 | tf_op jit(solution)/shard_map/ppermute | solution.py:228
  55.7 30.2 %all-to-all-start = ((bf16[8,16,1536]{2,1,0:T(8,128)(2,1)}), bf16[8,16,1536]{2,1,0:T(8,128)(2,1)S(1)}, u32[]{:S(2)}, u32[]{:S(2)}) async-start(bf16[8,16,1536]{2,1,0:T(8,128)(2,1)} %bitcast.4), calls=%async_computation | async-start | bytes 786432 | tf_op jit(solution)/shard_map/all_to_all | solution.py:229
  102.0 2.8 %copy-start = (bf16[2048,1536]{1,0:T(8,128)(2,1)S(1)}, bf16[2048,1536]{1,0:T(8,128)(2,1)}, u32[]{:S(2)}) copy-start(bf16[2048,1536]{1,0:T(8,128)(2,1)} %all-gather.3.cloned.1.call-done) | copy-start | bytes 18874372
  104.8 11.9 %copy-start.1 = (bf16[2048,1536]{1,0:T(8,128)(2,1)S(1)}, bf16[2048,1536]{1,0:T(8,128)(2,1)}, u32[]{:S(2)}) copy-start(bf16[2048,1536]{1,0:T(8,128)(2,1)} %all-gather.3.cloned.1.call-done) | copy-start | bytes 18874372
  111.4 31.2 %collective-permute-start.5 = (f32[65,16,128]{2,1,0:T(8,128)S(1)}, f32[65,16,128]{2,1,0:T(8,128)S(1)}, u32[]{:S(2)}, u32[]{:S(2)}) collective-permute-start(f32[65,16,128]{2,1,0:T(8,128)S(1)} %lagged.2), channel_id=1, source_target_pairs={{0,128},{128,0},{1,129},{129,1},{2,130},{130,2},{3,131},{131,3},{4... | collective-permute-start | bytes 1597448 | tf_op jit(solution)/shard_map/ppermute | solution.py:236
Sparse Core Ops, SparseCore 0:
  41.7 60.3 all-gather.2

commit v4 on v3

--- a/solution.py
+++ b/solution.py
@@ -17,6 +17,7 @@
 PAIRS = LAGH + 1
 LANES = 128
 CHUNK = 64
+VMEM_BYTES = 58 * 1024 * 1024
 
 
 def to_neighbours(low_part, high_part):
@@ -205,7 +206,7 @@
         functools.partial(lagged_kernel, count, scale),
         out_shape=jax.ShapeDtypeStruct((LAGS, rows, channels), out_dtype),
         grid_spec=spec,
-        compiler_params=pltpu.CompilerParams(vmem_limit_bytes=24 * 1024 * 1024),
+        compiler_params=pltpu.CompilerParams(vmem_limit_bytes=VMEM_BYTES),
         cost_estimate=pl.CostEstimate(
             flops=4 * count * PAIRS * rows * channels * length,
             bytes_accessed=2 * count * channels * length,
@@ -225,17 +226,17 @@
 
     normalized = normalize(raw_strain, band_index, filter_taps)
     ring = lax.all_gather(normalized, ("zh", "ta"), axis=0, tiled=False)
-    guest = lax.ppermute(normalized, "cp", swap)
-    guest = lax.all_to_all(guest.reshape(count, rows, length), "ta", 0, 0)
+    guest = lax.all_to_all(normalized.reshape(count, rows, length), "ta", 0, 0)
+    guest = lax.ppermute(guest, "cp", swap)
 
     other = (1 - half) * count
     near = jnp.where(upper == 1, other, half * count)
     place0 = jnp.stack([0 * piece, 0 * piece, near]).astype(jnp.int32)
     place1 = jnp.stack([half * count, piece, other]).astype(jnp.int32)
-    first = lagged(place0, guest, ring, rows, count, scale)
+    first = lagged(place0, guest, ring, rows, count, scale, jnp.bfloat16)
     first = lax.ppermute(first, "cp", swap)
     second = lagged(place1, ring, ring, rows, count, scale)
-    return jnp.stack([first, second])
+    return jnp.stack([first.astype(jnp.float32), second])
 
 
 def solution(mesh):

time: 151 us -> 132 us (0.87)
  waiting for transfers between devices: 73 us -> 48.5 us
  blocking collectives: 0 us -> 16.5 us
  starting transfers between devices: 37.3 us -> 21.8 us
  Pallas kernels: 16.8 us -> 23 us
  local copies, waits for them, and re-layouts: 6.55 us -> 4.26 us
    all_to_all x0 -> x1, blocking collectives: none -> 16.5 us  [on_device(): guest = lax.all_to_all(normalized.reshape(count, rows, length), 'ta', 0, 0)]
    all_to_all x1 -> x0, starting transfers between devices: 15.5 us -> none  [on_device(): guest = lax.all_to_all(guest.reshape(count, rows, length), 'ta', 0, 0)]
    all_to_all x1 -> x0, waiting for transfers between devices: 14.6 us -> none  [on_device(): guest = lax.all_to_all(guest.reshape(count, rows, length), 'ta', 0, 0)]
    ppermute x1, waiting for transfers between devices: 19.2 us -> 4.99 us  [on_device(): first = lax.ppermute(first, 'cp', swap)]
    ppermute x1, waiting for transfers between devices: 8.45 us -> 18.4 us  [on_device(): guest = lax.ppermute(guest, 'cp', swap)]
    pallas_call x2, Pallas kernels: 13.2 us -> 19.4 us  [lagged(): pl.pallas_call(functools.partial(lagged_kernel, count, scale), out_shape=...]
    all_gather x1, waiting for transfers between devices: 16.2 us -> 10.6 us  [on_device(): ring = lax.all_gather(normalized, ('zh', 'ta'), axis=0, tiled=False)]
    unnamed x12, local copies, waits for them, and re-layouts: 5.36 us -> 2.58 us
  transfers between devices with their start and end apart: 8 -> 7, of which waited for: 7 -> 6; matrix products, arithmetic and copies ran while one was open for 0% -> 1% of each run, Pallas kernels for 4% -> 7%
where the time goes in v4:
time: 132 us; the launch traced here: 131 us
  waiting for transfers between devices  48.5 us (37%)
  Pallas kernels  23 us (17%)
  starting transfers between devices  21.8 us (17%)
  blocking collectives  16.5 us (12%)
  between operations  13.5 us (10%)
  local copies, waits for them, and re-layouts  4.26 us (3%)
  other arithmetic  3.87 us (3%)
    pallas_call x2, Pallas kernels, lagged(): pl.pallas_call(functools.partial(lagged_kernel, count, scale), out_shape=...  19.4 us
    ppermute x1, waiting for transfers between devices, on_device(): guest = lax.ppermute(guest, 'cp', swap)  18.4 us
    all_to_all x1, blocking collectives, on_device(): guest = lax.all_to_all(normalized.reshape(count, rows, length), 'ta', 0, 0)  16.5 us
    all_gather x1, waiting for transfers between devices, on_device(): ring = lax.all_gather(normalized, ('zh', 'ta'), axis=0, tiled=False)  10.6 us
    ppermute x2, waiting for transfers between devices, to_neighbours(): from_high = lax.ppermute(low_part, 'ta', backward)  8.2 us
    ppermute x2, starting transfers between devices, to_neighbours(): from_low = lax.ppermute(high_part, 'ta', forward)  6.57 us
    ppermute x2, waiting for transfers between devices, to_neighbours(): from_low = lax.ppermute(high_part, 'ta', forward)  6.33 us
    ppermute x1, starting transfers between devices, on_device(): guest = lax.ppermute(guest, 'cp', swap)  5.64 us
  transfers between devices with their start and end apart: 7, of which 6 were waited for; matrix products, arithmetic and copies ran while one was open for 1% of the time, Pallas kernels for 7%

profile of v4, /device:TPU:17, one launch (start us, length us, event | category | flops | bytes accessed | tf_op | source)
XLA Modules:
  0.0 131.5 jit_solution(7722867479216830090)
XLA Ops:
  6.5 1.0 fusion.10
  7.5 4.6 %collective-permute-start = (f32[16,128]{1,0:T(8,128)S(1)}, f32[16,128]{1,0:T(8,128)S(1)}, u32[]{:S(2)}, u32[]{:S(2)}) collective-permute-start(f32[16,128]{1,0:T(8,128)S(1)} %bitcast.21), channel_id=1, source_target_pairs={{0,1},{1,2},{2,3},{3,4},{4,5},{5,6},{6,7},{8,9},{9,10},{10,11},{11... | collective-permute-start | bytes 24584 | tf_op jit(solution)/shard_map/ppermute | solution.py:27
  12.2 1.9 %collective-permute-start.1 = (f32[16,128]{1,0:T(8,128)S(1)}, f32[16,128]{1,0:T(8,128)S(1)}, u32[]{:S(2)}, u32[]{:S(2)}) collective-permute-start(f32[16,128]{1,0:T(8,128)S(1)} %bitcast.22), channel_id=1, source_target_pairs={{1,0},{2,1},{3,2},{4,3},{5,4},{6,5},{7,6},{9,8},{10,9},{11,10},{12... | collective-permute-start | bytes 24584 | tf_op jit(solution)/shard_map/ppermute | solution.py:28
  14.1 3.0 %collective-permute-done.1.high_ref = f32[16,128]{1,0:T(8,128)S(1)} collective-permute-done((f32[16,128]{1,0:T(8,128)S(1)}, f32[16,128]{1,0:T(8,128)S(1)}, u32[]{:S(2)}, u32[]{:S(2)}) %collective-permute-start.1) | collective-permute-done | bytes 8224 | tf_op jit(solution)/shard_map/ppermute | solution.py:28
  17.2 1.1 copy-done
  18.3 0.7 copy-done.1
  19.0 0.7 copy-done.2
  19.6 3.6 %filter.1 = (f32[128,1536]{1,0:T(8,128)S(1)}, f32[128,1536]{1,0:T(8,128)S(1)}, f32[128,1536]{1,0:T(8,128)S(1)}) custom-call(f32[4,33]{1,0:T(4,128)S(1)} %copy-done.1, s32[1,128]{1,0:T(1,128)S(1)} %bitcast.13, f32[128,1536]{1,0:T(8,128)S(1)} %copy-done, f32[16,128]{1,0:T(8,128)S(1)} %collective-permute-done.low_ref, f32[16,128]{1,0:T(8,128)S(1)} %collective-permute-done.1.high_ref), custom_call_target="tpu_custom_call" | custom-call | tf_op jit(solution)/shard_map/filter/pallas_call | solution.py:86
  23.3 2.0 %collective-permute-start.2 = (f32[128,1536]{1,0:T(8,128)S(1)}, f32[128,1536]{1,0:T(8,128)S(1)}, u32[]{:S(2)}, u32[]{:S(2)}) collective-permute-start(f32[128,1536]{1,0:T(8,128)S(1)} %get-tuple-element.9), channel_id=1, source_target_pairs={{0,1},{1,2},{2,3},{3,4},{4,5},{5,6},{6,7},{8,9},{9,10},{10,11},{11... | collective-permute-start | bytes 2359304 | tf_op jit(solution)/shard_map/ppermute | solution.py:27
  25.3 2.4 %collective-permute-start.3 = (f32[128,1536]{1,0:T(8,128)S(1)}, f32[128,1536]{1,0:T(8,128)}, u32[]{:S(2)}, u32[]{:S(2)}) collective-permute-start(f32[128,1536]{1,0:T(8,128)S(1)} %get-tuple-element.10), channel_id=1, source_target_pairs={{1,0},{2,1},{3,2},{4,3},{5,4},{6,5},{7,6},{9,8},{10,9},{11,10},{12... | collective-permute-start | bytes 2359304 | tf_op jit(solution)/shard_map/ppermute | solution.py:28
  27.9 6.3 %collective-permute-done.2 = f32[128,1536]{1,0:T(8,128)S(1)} collective-permute-done((f32[128,1536]{1,0:T(8,128)S(1)}, f32[128,1536]{1,0:T(8,128)S(1)}, u32[]{:S(2)}, u32[]{:S(2)}) %collective-permute-start.2) | collective-permute-done | bytes 786464 | tf_op jit(solution)/shard_map/ppermute | solution.py:27
  34.2 5.2 %collective-permute-done.3 = f32[128,1536]{1,0:T(8,128)} collective-permute-done((f32[128,1536]{1,0:T(8,128)S(1)}, f32[128,1536]{1,0:T(8,128)}, u32[]{:S(2)}, u32[]{:S(2)}) %collective-permute-start.3) | collective-permute-done | bytes 786464 | tf_op jit(solution)/shard_map/ppermute | solution.py:28
  39.4 2.1 %divide_convert_fusion = bf16[128,1536]{1,0:T(8,128)(2,1)} fusion(f32[128,1536]{1,0:T(8,128)S(1)} %get-tuple-element.8, f32[128,1536]{1,0:T(8,128)} %collective-permute-done.3, f32[128,1536]{1,0:T(8,128)S(1)} %collective-permute-done.2, f32[1536]{0:T(1024)S(1)} %subtract_convert_fusion, f32[128]{0:T(128)S(1)} %slice_reduce_fusion), kind=kLoop, calls=%fused_computation.1 | loop fusion | flops 1179648 | bytes 2759168 | tf_op jit(solution)/shard_map/convert_element_type | solution.py:115
  41.5 16.5 %all_to_all.5 = bf16[8,16,1536]{2,1,0:T(8,128)(2,1)S(1)} all-to-all(bf16[8,16,1536]{2,1,0:T(8,128)(2,1)} %bitcast.19), channel_id=1, replica_groups=mesh['zh'=2,'cp'=2,'col'=16,'ta'=8] {'ta'}, dimensions={0} | all-to-all | bytes 786432 | tf_op jit(solution)/shard_map/all_to_all | solution.py:229
  58.1 5.6 %collective-permute-start.4 = (bf16[8,16,1536]{2,1,0:T(8,128)(2,1)S(1)}, bf16[8,16,1536]{2,1,0:T(8,128)(2,1)S(1)}, u32[]{:S(2)}, u32[]{:S(2)}) collective-permute-start(bf16[8,16,1536]{2,1,0:T(8,128)(2,1)S(1)} %all_to_all.5), channel_id=1, source_target_pairs={{0,128},{128,0},{1,129},{129,1},{2,130},{130,2},{3,131},{131,3},{4... | collective-permute-start | bytes 1179656 | tf_op jit(solution)/shard_map/ppermute | solution.py:230
  63.7 0.6 stack.31.place_ref
  64.3 0.7 pad_add_fusion.place_ref
  64.9 18.4 %collective-permute-done.4.own_ref.left_ref.right_ref = bf16[8,16,1536]{2,1,0:T(8,128)(2,1)S(1)} collective-permute-done((bf16[8,16,1536]{2,1,0:T(8,128)(2,1)S(1)}, bf16[8,16,1536]{2,1,0:T(8,128)(2,1)S(1)}, u32[]{:S(2)}, u32[]{:S(2)}) %collective-permute-start.4) | collective-permute-done | bytes 393248 | tf_op jit(solution)/shard_map/ppermute | solution.py:230
  83.3 10.6 %all-gather.3.cloned.1.call-done = bf16[2048,1536]{1,0:T(8,128)(2,1)} async-done(((bf16[128,1536]{1,0:T(8,128)(2,1)}), bf16[2048,1536]{1,0:T(8,128)(2,1)}) %all-gather.3.cloned.1.call-update) | async-done | bytes 6291472 | tf_op jit(solution)/shard_map/all_gather | solution.py:228
  93.9 9.6 %lagged.2 = bf16[65,16,128]{2,1,0:T(8,128)(2,1)} custom-call(s32[3]{0:T(128)} %stack.31.place_ref, bf16[8,16,1536]{2,1,0:T(8,128)(2,1)} %copy-done.4, bf16[8,16,1536]{2,1,0:T(8,128)(2,1)} %copy-done.4, bf16[8,16,1536]{2,1,0:T(8,128)(2,1)} %copy-done.4, bf16[16,128,1536]{2,1,0:T(8,128)(2,1)} %bitcast.14), custom_call_target="tpu_custom_call" | custom-call | flops 3321888768 | bytes 3145728 | tf_op jit(solution)/shard_map/lagged/pallas_call | solution.py:205
  103.5 5.3 %collective-permute-start.5 = (bf16[65,16,128]{2,1,0:T(8,128)(2,1)}, bf16[65,16,128]{2,1,0:T(8,128)(2,1)S(1)}, u32[]{:S(2)}, u32[]{:S(2)}) collective-permute-start(bf16[65,16,128]{2,1,0:T(8,128)(2,1)} %lagged.2), channel_id=1, source_target_pairs={{0,128},{128,0},{1,129},{129,1},{2,130},{130,2},{3,131},{131,3},{4... | collective-permute-start | bytes 798728 | tf_op jit(solution)/shard_map/ppermute | solution.py:237
  108.8 9.7 %lagged.3 = f32[65,16,128]{2,1,0:T(8,128)} custom-call(s32[3]{0:T(128)} %pad_add_fusion.place_ref, bf16[16,128,1536]{2,1,0:T(8,128)(2,1)} %bitcast.15, bf16[16,128,1536]{2,1,0:T(8,128)(2,1)} %bitcast.16, bf16[16,128,1536]{2,1,0:T(8,128)(2,1)} %bitcast.17, bf16[16,128,1536]{2,1,0:T(8,128)(2,1)} %bitcast.18), custom_call_target="tpu_custom_call" | custom-call | flops 3321888768 | bytes 3145728 | tf_op jit(solution)/shard_map/lagged/pallas_call | solution.py:205
  118.5 5.0 %collective-permute-done.5 = bf16[65,16,128]{2,1,0:T(8,128)(2,1)S(1)} collective-permute-done((bf16[65,16,128]{2,1,0:T(8,128)(2,1)}, bf16[65,16,128]{2,1,0:T(8,128)(2,1)S(1)}, u32[]{:S(2)}, u32[]{:S(2)}) %collective-permute-start.5) | collective-permute-done | bytes 266272 | tf_op jit(solution)/shard_map/ppermute | solution.py:237
  123.6 1.0 pad_maximum_fusion
  (15 shorter events, 0.4 us)
Async XLA Ops:
  6.5 87.3 %all-gather.3.cloned.1.call-start = ((), (), s32[]{:S(2)}) async-start(), calls=%async_computation.1 | async-start | bytes 6684672 | tf_op jit(solution)/shard_map/all_gather | solution.py:228
  7.5 6.6 %collective-permute-start = (f32[16,128]{1,0:T(8,128)S(1)}, f32[16,128]{1,0:T(8,128)S(1)}, u32[]{:S(2)}, u32[]{:S(2)}) collective-permute-start(f32[16,128]{1,0:T(8,128)S(1)} %bitcast.21), channel_id=1, source_target_pairs={{0,1},{1,2},{2,3},{3,4},{4,5},{5,6},{6,7},{8,9},{9,10},{10,11},{11... | collective-permute-start | bytes 24584 | tf_op jit(solution)/shard_map/ppermute | solution.py:27
  12.2 5.0 %collective-permute-start.1 = (f32[16,128]{1,0:T(8,128)S(1)}, f32[16,128]{1,0:T(8,128)S(1)}, u32[]{:S(2)}, u32[]{:S(2)}) collective-permute-start(f32[16,128]{1,0:T(8,128)S(1)} %bitcast.22), channel_id=1, source_target_pairs={{1,0},{2,1},{3,2},{4,3},{5,4},{6,5},{7,6},{9,8},{10,9},{11,10},{12... | collective-permute-start | bytes 24584 | tf_op jit(solution)/shard_map/ppermute | solution.py:28
  17.2 1.1 copy-start
  18.3 0.7 copy-start.1
  19.0 0.7 copy-start.2
  23.3 10.9 %collective-permute-start.2 = (f32[128,1536]{1,0:T(8,128)S(1)}, f32[128,1536]{1,0:T(8,128)S(1)}, u32[]{:S(2)}, u32[]{:S(2)}) collective-permute-start(f32[128,1536]{1,0:T(8,128)S(1)} %get-tuple-element.9), channel_id=1, source_target_pairs={{0,1},{1,2},{2,3},{3,4},{4,5},{5,6},{6,7},{8,9},{9,10},{10,11},{11... | collective-permute-start | bytes 2359304 | tf_op jit(solution)/shard_map/ppermute | solution.py:27
  25.3 14.1 %collective-permute-start.3 = (f32[128,1536]{1,0:T(8,128)S(1)}, f32[128,1536]{1,0:T(8,128)}, u32[]{:S(2)}, u32[]{:S(2)}) collective-permute-start(f32[128,1536]{1,0:T(8,128)S(1)} %get-tuple-element.10), channel_id=1, source_target_pairs={{1,0},{2,1},{3,2},{4,3},{5,4},{6,5},{7,6},{9,8},{10,9},{11,10},{12... | collective-permute-start | bytes 2359304 | tf_op jit(solution)/shard_map/ppermute | solution.py:28
  58.1 25.2 %collective-permute-start.4 = (bf16[8,16,1536]{2,1,0:T(8,128)(2,1)S(1)}, bf16[8,16,1536]{2,1,0:T(8,128)(2,1)S(1)}, u32[]{:S(2)}, u32[]{:S(2)}) collective-permute-start(bf16[8,16,1536]{2,1,0:T(8,128)(2,1)S(1)} %all_to_all.5), channel_id=1, source_target_pairs={{0,128},{128,0},{1,129},{129,1},{2,130},{130,2},{3,131},{131,3},{4... | collective-permute-start | bytes 1179656 | tf_op jit(solution)/shard_map/ppermute | solution.py:230
  83.3 10.6 %copy-start.4 = (bf16[8,16,1536]{2,1,0:T(8,128)(2,1)}, bf16[8,16,1536]{2,1,0:T(8,128)(2,1)S(1)}, u32[]{:S(2)}) copy-start(bf16[8,16,1536]{2,1,0:T(8,128)(2,1)S(1)} %collective-permute-done.4.own_ref.left_ref.right_ref) | copy-start | bytes 1179652
  103.5 20.0 %collective-permute-start.5 = (bf16[65,16,128]{2,1,0:T(8,128)(2,1)}, bf16[65,16,128]{2,1,0:T(8,128)(2,1)S(1)}, u32[]{:S(2)}, u32[]{:S(2)}) collective-permute-start(bf16[65,16,128]{2,1,0:T(8,128)(2,1)} %lagged.2), channel_id=1, source_target_pairs={{0,128},{128,0},{1,129},{129,1},{2,130},{130,2},{3,131},{131,3},{4... | collective-permute-start | bytes 798728 | tf_op jit(solution)/shard_map/ppermute | solution.py:237
  118.5 5.0 %copy-start.3 = (f32[65,16,128]{2,1,0:T(8,128)S(1)}, f32[65,16,128]{2,1,0:T(8,128)}, u32[]{:S(2)}) copy-start(f32[65,16,128]{2,1,0:T(8,128)} %lagged.3) | copy-start | bytes 1597444
Sparse Core Ops, SparseCore 0:
  41.6 52.2 all-gather.2

commit v5 on v4

v5 whole, which is shorter than its diff:
```python
import functools
import math

import jax
import jax.numpy as jnp
from jax import lax
from jax.experimental import pallas as pl
from jax.experimental.pallas import tpu as pltpu
from jax.sharding import Mesh
from jax.sharding import PartitionSpec as P

HF = 16
TAPS = 33
NBANDS = 4
LAGH = 32
LAGS = 65
PAIRS = LAGH + 1
LANES = 128
AHEAD = 3
ROUNDS = 2
CHUNK = 64
VMEM_BYTES = 58 * 1024 * 1024


def to_neighbours(on_chip, off_chip):
    count = lax.axis_size("ta")
    inner = [(i, i ^ 1) for i in range(count)]
    outer = [(i, i - 1 + 2 * (i % 2)) for i in range(1, count - 1)]
    off_chip = lax.ppermute(off_chip, "ta", outer)
    return lax.ppermute(on_chip, "ta", inner), off_chip


def filter_kernel(
    place_ref, coeff_ref, tall_ref, inner_ref, outer_ref, out_ref, total_ref, on_chip_ref, off_chip_ref, tall, wide
):
    length, channels = tall_ref.shape
    tiles = length // LANES
    first_core = place_ref[1] == 0
    tall[:HF] = jnp.where(first_core, outer_ref[...], inner_ref[...])
    tall[HF : HF + length] = tall_ref[...]
    tall[HF + length :] = jnp.where(first_core, inner_ref[...], outer_ref[...])

    def chunk(i, carry):
        base = pl.multiple_of(i * CHUNK, CHUNK)
        total = jnp.zeros((CHUNK, channels), jnp.float32)
        for k in range(TAPS):
            total = total + coeff_ref[k : k + 1, :] * tall[pl.ds(base + k, CHUNK), :]
        wide[pl.ds(base, CHUNK), :] = total
        return carry

    lax.fori_loop(0, length // CHUNK, chunk, 0)
    lane_total = jnp.zeros((channels, LANES), jnp.float32)
    for r in range(tiles):
        piece = wide[pl.ds(r, LANES, stride=tiles), :].T
        out_ref[:, r * LANES : (r + 1) * LANES] = piece
        lane_total = lane_total + jnp.abs(piece)
    row = lax.broadcasted_iota(jnp.int32, (LANES, LANES), 0)
    col = lax.broadcasted_iota(jnp.int32, (LANES, LANES), 1)
    earlier = jnp.dot(
        lane_total,
        (row < col).astype(jnp.float32),
        precision=lax.Precision.HIGHEST,
        preferred_element_type=jnp.float32,
    )
    total = jnp.broadcast_to((earlier + lane_total)[:, LANES - 1 :], (channels, LANES))
    total_ref[...] = total

    def pack(ref, lanes_sum, order):
        inner = jnp.zeros((channels, LANES), jnp.float32)
        for r in order:
            cols = slice(r * LANES, (r + 1) * LANES)
            inner = inner + jnp.abs(out_ref[:, cols])
            ref[:, cols] = inner.astype(jnp.bfloat16)
        rest = lanes_sum
        for i in range(3):
            term = rest.astype(jnp.bfloat16)
            ref[:, length + i * LANES : length + (i + 1) * LANES] = term
            rest = rest - term.astype(jnp.float32)

    later = total - earlier - lane_total

    @pl.when(first_core)
    def _():
        pack(off_chip_ref, earlier, range(tiles))
        pack(on_chip_ref, later, range(tiles - 1, -1, -1))

    @pl.when(jnp.logical_not(first_core))
    def _():
        pack(on_chip_ref, earlier, range(tiles))
        pack(off_chip_ref, later, range(tiles - 1, -1, -1))


def normalize_kernel(place_ref, filtered_ref, total_ref, on_chip_ref, off_chip_ref, out_ref):
    channels, length = filtered_ref.shape
    tiles = length // LANES
    count = place_ref[3]
    base = total_ref[...]
    for i in range(3):
        cols = slice(length + i * LANES, length + (i + 1) * LANES)
        base = base + on_chip_ref[:, cols].astype(jnp.float32)
        base = base + off_chip_ref[:, cols].astype(jnp.float32)
    lane = lax.broadcasted_iota(jnp.int32, (channels, LANES), 1)
    for r in range(tiles):
        cols = slice(r * LANES, (r + 1) * LANES)
        time = place_ref[2] * length + tiles * lane + r
        upper = jnp.minimum(time + length, length * count - 1) + 1
        lower = jnp.maximum(time - length, 0)
        window = base + (
            on_chip_ref[:, cols].astype(jnp.float32) + off_chip_ref[:, cols].astype(jnp.float32)
        )
        level = window / (upper - lower).astype(jnp.float32)
        out_ref[:, cols] = (filtered_ref[:, cols] / (level + 1e-06)).astype(jnp.bfloat16)


def normalize(raw, band_index, filter_taps, place):
    channels, length = raw.shape
    first_core = place[1] == 0
    low, high = raw[:, :HF].T, raw[:, length - HF :].T
    inner, outer = to_neighbours(
        jnp.where(first_core, high, low), jnp.where(first_core, low, high)
    )
    band = band_index[None, :]
    coeff = jnp.broadcast_to(filter_taps[NBANDS - 1][:, None], (TAPS, channels))
    for i in range(NBANDS - 1):
        coeff = jnp.where(band == i, filter_taps[i][:, None], coeff)
    vmem = pl.BlockSpec(memory_space=pltpu.VMEM)
    smem = pl.BlockSpec(memory_space=pltpu.SMEM)
    packed = jax.ShapeDtypeStruct((channels, length + 3 * LANES), jnp.bfloat16)
    filtered, total, on_chip, off_chip = pl.pallas_call(
        filter_kernel,
        out_shape=(
            jax.ShapeDtypeStruct((channels, length), jnp.float32),
            jax.ShapeDtypeStruct((channels, LANES), jnp.float32),
            packed,
            packed,
        ),
        in_specs=[smem] + [vmem] * 4,
        out_specs=(vmem,) * 4,
        scratch_shapes=[
            pltpu.VMEM((length + 2 * HF, channels), jnp.float32),
            pltpu.VMEM((length, channels), jnp.float32),
        ],
        compiler_params=pltpu.CompilerParams(vmem_limit_bytes=24 * 1024 * 1024),
        name="filter",
    )(place, coeff, raw.T, inner, outer)
    on_chip, off_chip = to_neighbours(on_chip, off_chip)
    return pl.pallas_call(
        normalize_kernel,
        out_shape=jax.ShapeDtypeStruct((channels, length), jnp.bfloat16),
        in_specs=[smem] + [vmem] * 4,
        out_specs=vmem,
        compiler_params=pltpu.CompilerParams(vmem_limit_bytes=24 * 1024 * 1024),
        name="normalize",
    )(place, filtered, total, on_chip, off_chip)


def lagged_kernel(
    count, scale, place_ref, row_hbm, part_hbm, out_hbm, fan, both, carry, acc, row_buf, part_buf, out_buf, row_sem, part_sem, out_sem
):
    rows = row_buf.shape[1]
    channels, length = part_buf.shape[1:]
    tiles = length // LANES
    reach = -(-LAGH // tiles)
    lead = reach * tiles + LAGH
    first_row = pl.multiple_of(place_ref[1] * rows, rows)

    def row_copy(t):
        return pltpu.make_async_copy(
            row_hbm.at[place_ref[0] + t, pl.ds(first_row, rows)], row_buf.at[t + 1], row_sem.at[t]
        )

    def part_copy(t):
        return pltpu.make_async_copy(
            part_hbm.at[place_ref[2] + t], part_buf.at[t], part_sem.at[t]
        )

    for t in range(AHEAD):
        row_copy(t).start()
        part_copy(t).start()
    acc[...] = jnp.zeros_like(acc)
    carry[...] = jnp.zeros_like(carry)
    row_buf[0] = jnp.zeros((rows, length), jnp.bfloat16)
    row_buf[count + 1] = jnp.zeros((rows, length), jnp.bfloat16)
    lane = lax.broadcasted_iota(jnp.int32, (rows, length), 1) % LANES
    part_lane = lax.broadcasted_iota(jnp.int32, (channels, LANES), 1)
    row_copy(0).wait()

    def moved(width, offset):
        return jnp.concatenate(
            [
                fan[:, (lead - 2 * a + offset) * LANES : (lead - 2 * a + offset + width) * LANES]
                for a in range(PAIRS)
            ],
            axis=0,
        )

    def body(step, unused):
        @pl.when(step + AHEAD < count)
        def _():
            row_copy(step + AHEAD).start()
            part_copy(step + AHEAD).start()

        @pl.when(step + 1 < count)
        def _():
            row_copy(step + 1).wait()

        inside = row_buf[step + 1].astype(jnp.float32)
        left = row_buf[step].astype(jnp.float32)
        right = row_buf[step + 2].astype(jnp.float32)
        for j in range(-reach, reach + 1):
            if j < 0:
                mixed = jnp.where(lane >= LANES + j, left, inside)
            else:
                mixed = jnp.where(lane < j, right, inside)
            for r in range(tiles):
                tile = mixed[:, r * LANES : (r + 1) * LANES]
                if j != 0:
                    tile = pltpu.roll(tile, (-j) % LANES, 1)
                at = (j + reach) * tiles + r
                fan[:, at * LANES : (at + 1) * LANES] = tile.astype(jnp.bfloat16)

        part_copy(step).wait()
        both[:channels] = part_buf[step]
        both[channels:, LANES:] = part_buf[step, :, : length - LANES]
        final = part_buf[step, :, length - LANES :].astype(jnp.float32)
        late = pltpu.roll(jnp.where(part_lane == LANES - 1, carry[...], final), 1, 1)
        both[channels:, :LANES] = late.astype(jnp.bfloat16)
        carry[...] = final
        acc[...] += lax.dot_general(
            moved(tiles, 0), both[...], (((1,), (1,)), ((), ())), preferred_element_type=jnp.float32
        )
        return unused

    lax.fori_loop(0, count, body, 0)
    tail = jnp.where(part_lane == LANES - 1, carry[...], 0.0).astype(jnp.bfloat16)
    acc[:, channels:] += lax.dot_general(
        moved(1, tiles), tail, (((1,), (1,)), ((), ())), preferred_element_type=jnp.float32
    )
    outs = []
    for a in range(PAIRS):
        block = acc[a * rows : (a + 1) * rows] * scale
        out_buf[2 * a] = block[:, :channels].astype(out_buf.dtype)
        if a > 0:
            out_buf[2 * a - 1] = block[:, channels:].astype(out_buf.dtype)
        if a in (PAIRS // 2, PAIRS - 1):
            done = 2 * (PAIRS // 2) + 1 if outs else 0
            span = pl.ds(done, 2 * a + 1 - done)
            outs.append(
                pltpu.make_async_copy(
                    out_buf.at[span], out_hbm.at[out_hbm.shape[0] - 1, span], out_sem.at[len(outs)]
                )
            )
            outs[-1].start()
    for copy in outs:
        copy.wait()


def lagged(place, own_rows, partner, rows, count, scale, out_dtype, rounds):
    channels, length = partner.shape[1:]
    tiles = length // LANES
    fan_tiles = (2 * -(-LAGH // tiles) + 1) * tiles
    anywhere = pl.BlockSpec(memory_space=pl.ANY)
    return pl.pallas_call(
        functools.partial(lagged_kernel, count, scale),
        out_shape=jax.ShapeDtypeStruct((rounds, LAGS, rows, channels), out_dtype),
        in_specs=[pl.BlockSpec(memory_space=pltpu.SMEM), anywhere, anywhere],
        out_specs=anywhere,
        scratch_shapes=[
            pltpu.VMEM((rows, fan_tiles * LANES), jnp.bfloat16),
            pltpu.VMEM((2 * channels, length), jnp.bfloat16),
            pltpu.VMEM((channels, LANES), jnp.float32),
            pltpu.VMEM((PAIRS * rows, 2 * channels), jnp.float32),
            pltpu.VMEM((count + 2, rows, length), jnp.bfloat16),
            pltpu.VMEM((count, channels, length), jnp.bfloat16),
            pltpu.VMEM((LAGS, rows, channels), out_dtype),
            pltpu.SemaphoreType.DMA((count,)),
            pltpu.SemaphoreType.DMA((count,)),
            pltpu.SemaphoreType.DMA((2,)),
        ],
        compiler_params=pltpu.CompilerParams(vmem_limit_bytes=VMEM_BYTES),
        cost_estimate=pl.CostEstimate(
            flops=4 * count * PAIRS * rows * channels * length,
            bytes_accessed=2 * count * channels * length,
            transcendentals=0,
        ),
        name="lagged",
    )(place, own_rows, partner)


def on_device(raw_strain, band_index, filter_taps):
    channels, length = raw_strain.shape
    count = lax.axis_size("ta")
    rows = channels // count
    scale = 1.0 / math.sqrt(length * count)
    swap = [(0, 1), (1, 0)]
    half, upper, piece = lax.axis_index("zh"), lax.axis_index("cp"), lax.axis_index("ta")

    zero = 0 * piece
    here = jnp.stack([zero, piece % 2, piece, zero + count]).astype(jnp.int32)
    normalized = normalize(raw_strain, band_index, filter_taps, here)
    ring = lax.all_gather(normalized, ("zh", "ta"), axis=0, tiled=False)
    guest = lax.all_to_all(normalized.reshape(count, rows, length), "ta", 0, 0)
    guest = lax.ppermute(guest, "cp", swap)

    other = (1 - half) * count
    near = jnp.where(upper == 1, other, half * count)
    place0 = jnp.stack([zero, zero, near]).astype(jnp.int32)
    place1 = jnp.stack([half * count, piece, other]).astype(jnp.int32)
    first = lagged(place0, guest, ring, rows, count, scale, jnp.bfloat16, 1)
    place1, first = lax.optimization_barrier((place1, first))
    first = lax.ppermute(first, "cp", swap)
    result = lagged(place1, ring, ring, rows, count, scale, jnp.float32, ROUNDS)
    return lax.dynamic_update_slice_in_dim(result, first.astype(jnp.float32), 0, 0)


def solution(mesh):
    blocks, slices = mesh.devices.shape
    axes = ("zh", "cp", "col", "ta")
    parts = Mesh(mesh.devices.reshape(2, 2, blocks // 4, slices), axes)
    channel_axes = axes[:3]
    return jax.shard_map(
        on_device,
        mesh=parts,
        in_specs=(P(channel_axes, "ta"), P(channel_axes), P()),
        out_specs=P(None, None, axes, None),
        check_vma=False,
    )
```

time: 132 us -> 124 us (0.939)
  waiting for transfers between devices: 48.5 us -> 41.7 us
  other arithmetic: 3.87 us -> 1.65 us
  local copies, waits for them, and re-layouts: 4.26 us -> 2.05 us
  starting transfers between devices: 21.8 us -> 23.7 us
    ppermute x4, waiting for transfers between devices: 14.5 us -> 7.41 us  [the longest x2 6.49 us: to_neighbours(): off_chip = lax.ppermute(off_chip, 'ta', outer)]
    convert_element_type x2 -> x0, other arithmetic: 2.13 us -> none  [the longest x1 2.12 us: normalize(): return (filtered / (level + 1e-06)).astype(jnp.bfloat16)]
    ppermute x4, starting transfers between devices: 10.9 us -> 12.8 us  [the longest x2 8.78 us: to_neighbours(): off_chip = lax.ppermute(off_chip, 'ta', outer)]
    pallas_call x1 -> x2, Pallas kernels: 3.64 us -> 5.16 us  [the longest x1 3.59 us: normalize(): pl.pallas_call(filter_kernel, out_shape=(jax.ShapeDtypeStruct((channels,...]
  transfers between devices with their start and end apart: 7 -> 7, of which waited for: 6 -> 5; matrix products, arithmetic and copies ran while one was open for 1% -> 1% of each run, Pallas kernels for 7% -> 8%
where the time goes in v5:
time: 124 us; the launch traced here: 123 us
  waiting for transfers between devices  41.7 us (34%)
  starting transfers between devices  23.7 us (19%)
  Pallas kernels  23.7 us (19%)
  blocking collectives  16.9 us (14%)
  between operations  13.5 us (11%)
  local copies, waits for them, and re-layouts  2.05 us (2%)
  other arithmetic  1.65 us (1%)
    pallas_call x2, Pallas kernels, lagged(): pl.pallas_call(functools.partial(lagged_kernel, count, scale), out_shape=...  18.6 us
    ppermute x1, waiting for transfers between devices, on_device(): guest = lax.ppermute(guest, 'cp', swap)  18.3 us
    all_to_all x1, blocking collectives, on_device(): guest = lax.all_to_all(normalized.reshape(count, rows, length), 'ta', 0, 0)  16.9 us
    all_gather x1, waiting for transfers between devices, on_device(): ring = lax.all_gather(normalized, ('zh', 'ta'), axis=0, tiled=False)  10.6 us
    ppermute x2, starting transfers between devices, to_neighbours(): off_chip = lax.ppermute(off_chip, 'ta', outer)  8.78 us
    ppermute x2, waiting for transfers between devices, to_neighbours(): off_chip = lax.ppermute(off_chip, 'ta', outer)  6.49 us
    ppermute x1, starting transfers between devices, on_device(): guest = lax.ppermute(guest, 'cp', swap)  5.64 us
    ppermute x1, waiting for transfers between devices, on_device(): first = lax.ppermute(first, 'cp', swap)  5.39 us
  transfers between devices with their start and end apart: 7, of which 5 were waited for; matrix products, arithmetic and copies ran while one was open for 1% of the time, Pallas kernels for 8%

profile of v5, /device:TPU:17, one launch (start us, length us, event | category | flops | bytes accessed | tf_op | source)
XLA Modules:
  0.0 123.2 jit_solution(16965226851508544506)
XLA Ops:
  6.5 1.4 %copy.4 = f32[128,1536]{0,1:T(8,128)S(1)} copy(f32[128,1536]{1,0:T(8,128)} %param.3) | data formatting | bytes 1572864 | tf_op args[0]
  8.0 4.6 %collective-permute-start.1 = (f32[16,128]{1,0:T(8,128)S(1)}, f32[16,128]{1,0:T(8,128)S(1)}, u32[]{:S(2)}, u32[]{:S(2)}) collective-permute-start(f32[16,128]{1,0:T(8,128)S(1)} %get-tuple-element.17), channel_id=1, source_target_pairs={{1,2},{2,1},{3,4},{4,3},{5,6},{6,5},{9,10},{10,9},{11,12},{12,11},... | collective-permute-start | bytes 24584 | tf_op jit(solution)/shard_map/ppermute | solution.py:29
  12.5 1.9 %collective-permute-start = (f32[16,128]{1,0:T(8,128)S(1)}, f32[16,128]{1,0:T(8,128)S(1)}, u32[]{:S(2)}, u32[]{:S(2)}) collective-permute-start(f32[16,128]{1,0:T(8,128)S(1)} %get-tuple-element.18), channel_id=1, source_target_pairs={{0,1},{1,0},{2,3},{3,2},{4,5},{5,4},{6,7},{7,6},{8,9},{9,8},{10,11... | collective-permute-start | bytes 24584 | tf_op jit(solution)/shard_map/ppermute | solution.py:30
  14.5 0.1 select_select_fusion.coeff_ref
  14.6 0.1 pad_add_fusion.1.place_ref
  14.7 0.0 collective-permute-done.1.outer_ref
  14.7 0.9 collective-permute-done.inner_ref
  15.6 3.6 %filter.1 = (f32[128,1536]{1,0:T(8,128)S(1)}, f32[128,128]{1,0:T(8,128)S(1)}, bf16[128,1920]{1,0:T(8,128)(2,1)S(1)}, bf16[128,1920]{1,0:T(8,128)(2,1)S(1)}) custom-call(s32[4]{0:T(128)S(1)} %pad_add_fusion.1.place_ref, f32[33,128]{1,0:T(8,128)S(1)} %select_select_fusion.coeff_ref, f32[1536,128]{1,0:T(8,128)S(1)} %bitcast.20, ...), custom_call_target="tpu_custom_call" | custom-call | tf_op jit(solution)/shard_map/filter/pallas_call | solution.py:129
  19.2 2.1 %collective-permute-start.2 = (bf16[128,1920]{1,0:T(8,128)(2,1)S(1)}, bf16[128,1920]{1,0:T(8,128)(2,1)S(1)}, u32[]{:S(2)}, u32[]{:S(2)}) collective-permute-start(bf16[128,1920]{1,0:T(8,128)(2,1)S(1)} %get-tuple-element.13), channel_id=1, source_target_pairs={{0,1},{1,0},{2,3},{3,2},{4,5},{5,4},{6,7},{7,6},{8,9},{9,8},{10,11... | collective-permute-start | bytes 1474568 | tf_op jit(solution)/shard_map/ppermute | solution.py:30
  21.3 4.2 %collective-permute-start.3 = (bf16[128,1920]{1,0:T(8,128)(2,1)S(1)}, bf16[128,1920]{1,0:T(8,128)(2,1)S(1)}, u32[]{:S(2)}, u32[]{:S(2)}) collective-permute-start(bf16[128,1920]{1,0:T(8,128)(2,1)S(1)} %get-tuple-element.14), channel_id=1, source_target_pairs={{1,2},{2,1},{3,4},{4,3},{5,6},{6,5},{9,10},{10,9},{11,12},{12,11},... | collective-permute-start | bytes 1474568 | tf_op jit(solution)/shard_map/ppermute | solution.py:29
  25.5 6.5 %collective-permute-done.3.off_chip_ref = bf16[128,1920]{1,0:T(8,128)(2,1)S(1)} collective-permute-done((bf16[128,1920]{1,0:T(8,128)(2,1)S(1)}, bf16[128,1920]{1,0:T(8,128)(2,1)S(1)}, u32[]{:S(2)}, u32[]{:S(2)}) %collective-permute-start.3) | collective-permute-done | bytes 491552 | tf_op jit(solution)/shard_map/ppermute | solution.py:29
  32.0 1.6 %normalize.1 = bf16[128,1536]{1,0:T(8,128)(2,1)} custom-call(s32[4]{0:T(128)S(1)} %pad_add_fusion.1.place_ref, f32[128,1536]{1,0:T(8,128)S(1)} %get-tuple-element.11.filtered_ref, f32[128,128]{1,0:T(8,128)S(1)} %get-tuple-element.12.total_ref, bf16[128,1920]{1,0:T(8,128)(2,1)S(1)} %collective-permute-done.2.on_chip_ref, ...), custom_call_target="tpu_custom_call" | custom-call | tf_op jit(solution)/shard_map/normalize/pallas_call | solution.py:147
  33.6 0.0 all-gather.3.cloned.1.call-update
  33.6 16.9 %all_to_all.5 = bf16[8,16,1536]{2,1,0:T(8,128)(2,1)S(1)} all-to-all(bf16[8,16,1536]{2,1,0:T(8,128)(2,1)} %bitcast.12), channel_id=1, replica_groups=mesh['zh'=2,'cp'=2,'col'=16,'ta'=8] {'ta'}, dimensions={0} | all-to-all | bytes 786432 | tf_op jit(solution)/shard_map/all_to_all | solution.py:302
  50.5 5.6 %collective-permute-start.4 = (bf16[8,16,1536]{2,1,0:T(8,128)(2,1)S(1)}, bf16[8,16,1536]{2,1,0:T(8,128)(2,1)S(1)}, u32[]{:S(2)}, u32[]{:S(2)}) collective-permute-start(bf16[8,16,1536]{2,1,0:T(8,128)(2,1)S(1)} %all_to_all.5), channel_id=1, source_target_pairs={{0,128},{128,0},{1,129},{129,1},{2,130},{130,2},{3,131},{131,3},{4... | collective-permute-start | bytes 1179656 | tf_op jit(solution)/shard_map/ppermute | solution.py:303
  56.2 0.6 stack.30.place_ref
  56.8 0.7 pad_add_fusion.place_ref
  57.5 18.3 %collective-permute-done.4.row_hbm = bf16[8,16,1536]{2,1,0:T(8,128)(2,1)S(1)} collective-permute-done((bf16[8,16,1536]{2,1,0:T(8,128)(2,1)S(1)}, bf16[8,16,1536]{2,1,0:T(8,128)(2,1)S(1)}, u32[]{:S(2)}, u32[]{:S(2)}) %collective-permute-start.4) | collective-permute-done | bytes 393248 | tf_op jit(solution)/shard_map/ppermute | solution.py:303
  75.8 10.6 %all-gather.3.cloned.1.call-done = bf16[2048,1536]{1,0:T(8,128)(2,1)} async-done(((bf16[128,1536]{1,0:T(8,128)(2,1)}), bf16[2048,1536]{1,0:T(8,128)(2,1)}) %all-gather.3.cloned.1.call-update) | async-done | bytes 6291472 | tf_op jit(solution)/shard_map/all_gather | solution.py:301
  86.3 9.2 %lagged.2 = bf16[1,65,16,128]{3,2,1,0:T(8,128)(2,1)} custom-call(s32[3]{0:T(128)} %stack.30.place_ref, bf16[8,16,1536]{2,1,0:T(8,128)(2,1)} %copy-done.2, bf16[16,128,1536]{2,1,0:T(8,128)(2,1)} %bitcast.21), custom_call_target="tpu_custom_call" | custom-call | flops 3321888768 | bytes 3145728 | tf_op jit(solution)/shard_map/lagged/pallas_call | solution.py:263
  95.6 5.3 %collective-permute-start.5 = (bf16[1,65,16,128]{3,2,1,0:T(8,128)(2,1)}, bf16[1,65,16,128]{3,2,1,0:T(8,128)(2,1)S(1)}, u32[]{:S(2)}, u32[]{:S(2)}) collective-permute-start(bf16[1,65,16,128]{3,2,1,0:T(8,128)(2,1)} %lagged.2), channel_id=1, source_target_pairs={{0,128},{128,0},{1,129},{129,1},{2,130},{130,2},{3,131},{131,3},{4... | collective-permute-start | bytes 798728 | tf_op jit(solution)/shard_map/ppermute | solution.py:311
  100.9 9.3 %lagged.3 = f32[2,65,16,128]{3,2,1,0:T(8,128)} custom-call(s32[3]{0:T(128)} %pad_add_fusion.place_ref, bf16[16,128,1536]{2,1,0:T(8,128)(2,1)} %bitcast.22, bf16[16,128,1536]{2,1,0:T(8,128)(2,1)} %bitcast.23), custom_call_target="tpu_custom_call" | custom-call | flops 3321888768 | bytes 3145728 | tf_op jit(solution)/shard_map/lagged/pallas_call | solution.py:263
  110.2 5.4 %collective-permute-done.5 = bf16[1,65,16,128]{3,2,1,0:T(8,128)(2,1)S(1)} collective-permute-done((bf16[1,65,16,128]{3,2,1,0:T(8,128)(2,1)}, bf16[1,65,16,128]{3,2,1,0:T(8,128)(2,1)S(1)}, u32[]{:S(2)}, u32[]{:S(2)}) %collective-permute-start.5) | collective-permute-done | bytes 266272 | tf_op jit(solution)/shard_map/ppermute | solution.py:311
  115.6 0.8 convert_dynamic-update-slice_fusion
  (11 shorter events, 0.0 us)
Async XLA Ops:
  6.5 7.9 %copy-start.1 = (s32[128]{0:T(128)S(1)}, s32[128]{0:T(128)}, u32[]{:S(2)}) copy-start(s32[128]{0:T(128)} %param.4) | copy-start | bytes 1540
  6.5 8.0 %copy-start = (f32[4,33]{1,0:T(4,128)S(1)}, f32[4,33]{1,0:T(4,128)}, u32[]{:S(2)}) copy-start(f32[4,33]{1,0:T(4,128)} %param.5) | copy-start | bytes 1588
  6.5 79.8 %all-gather.3.cloned.1.call-start = ((), (), s32[]{:S(2)}) async-start(), calls=%async_computation.1 | async-start | bytes 6684672 | tf_op jit(solution)/shard_map/all_gather | solution.py:301
  8.0 6.7 %collective-permute-start.1 = (f32[16,128]{1,0:T(8,128)S(1)}, f32[16,128]{1,0:T(8,128)S(1)}, u32[]{:S(2)}, u32[]{:S(2)}) collective-permute-start(f32[16,128]{1,0:T(8,128)S(1)} %get-tuple-element.17), channel_id=1, source_target_pairs={{1,2},{2,1},{3,4},{4,3},{5,6},{6,5},{9,10},{10,9},{11,12},{12,11},... | collective-permute-start | bytes 24584 | tf_op jit(solution)/shard_map/ppermute | solution.py:29
  12.5 3.1 %collective-permute-start = (f32[16,128]{1,0:T(8,128)S(1)}, f32[16,128]{1,0:T(8,128)S(1)}, u32[]{:S(2)}, u32[]{:S(2)}) collective-permute-start(f32[16,128]{1,0:T(8,128)S(1)} %get-tuple-element.18), channel_id=1, source_target_pairs={{0,1},{1,0},{2,3},{3,2},{4,5},{5,4},{6,7},{7,6},{8,9},{9,8},{10,11... | collective-permute-start | bytes 24584 | tf_op jit(solution)/shard_map/ppermute | solution.py:30
  19.2 6.3 %collective-permute-start.2 = (bf16[128,1920]{1,0:T(8,128)(2,1)S(1)}, bf16[128,1920]{1,0:T(8,128)(2,1)S(1)}, u32[]{:S(2)}, u32[]{:S(2)}) collective-permute-start(bf16[128,1920]{1,0:T(8,128)(2,1)S(1)} %get-tuple-element.13), channel_id=1, source_target_pairs={{0,1},{1,0},{2,3},{3,2},{4,5},{5,4},{6,7},{7,6},{8,9},{9,8},{10,11... | collective-permute-start | bytes 1474568 | tf_op jit(solution)/shard_map/ppermute | solution.py:30
  21.3 10.7 %collective-permute-start.3 = (bf16[128,1920]{1,0:T(8,128)(2,1)S(1)}, bf16[128,1920]{1,0:T(8,128)(2,1)S(1)}, u32[]{:S(2)}, u32[]{:S(2)}) collective-permute-start(bf16[128,1920]{1,0:T(8,128)(2,1)S(1)} %get-tuple-element.14), channel_id=1, source_target_pairs={{1,2},{2,1},{3,4},{4,3},{5,6},{6,5},{9,10},{10,9},{11,12},{12,11},... | collective-permute-start | bytes 1474568 | tf_op jit(solution)/shard_map/ppermute | solution.py:29
  50.5 25.2 %collective-permute-start.4 = (bf16[8,16,1536]{2,1,0:T(8,128)(2,1)S(1)}, bf16[8,16,1536]{2,1,0:T(8,128)(2,1)S(1)}, u32[]{:S(2)}, u32[]{:S(2)}) collective-permute-start(bf16[8,16,1536]{2,1,0:T(8,128)(2,1)S(1)} %all_to_all.5), channel_id=1, source_target_pairs={{0,128},{128,0},{1,129},{129,1},{2,130},{130,2},{3,131},{131,3},{4... | collective-permute-start | bytes 1179656 | tf_op jit(solution)/shard_map/ppermute | solution.py:303
  75.8 10.6 %copy-start.2 = (bf16[8,16,1536]{2,1,0:T(8,128)(2,1)}, bf16[8,16,1536]{2,1,0:T(8,128)(2,1)S(1)}, u32[]{:S(2)}) copy-start(bf16[8,16,1536]{2,1,0:T(8,128)(2,1)S(1)} %collective-permute-done.4.row_hbm) | copy-start | bytes 1179652
  95.6 20.0 %collective-permute-start.5 = (bf16[1,65,16,128]{3,2,1,0:T(8,128)(2,1)}, bf16[1,65,16,128]{3,2,1,0:T(8,128)(2,1)S(1)}, u32[]{:S(2)}, u32[]{:S(2)}) collective-permute-start(bf16[1,65,16,128]{3,2,1,0:T(8,128)(2,1)} %lagged.2), channel_id=1, source_target_pairs={{0,128},{128,0},{1,129},{129,1},{2,130},{130,2},{3,131},{131,3},{4... | collective-permute-start | bytes 798728 | tf_op jit(solution)/shard_map/ppermute | solution.py:311
Sparse Core Ops, SparseCore 0:
  33.7 52.5 all-gather.2

commit v6 on v5

--- a/solution.py
+++ b/solution.py
@@ -19,7 +19,7 @@
 AHEAD = 3
 ROUNDS = 2
 CHUNK = 64
-VMEM_BYTES = 58 * 1024 * 1024
+VMEM_BYTES = 52 * 1024 * 1024
 
 
 def to_neighbours(on_chip, off_chip):
@@ -31,14 +31,14 @@
 
 
 def filter_kernel(
-    place_ref, coeff_ref, tall_ref, inner_ref, outer_ref, out_ref, total_ref, on_chip_ref, off_chip_ref, tall, wide
+    place_ref, coeff_ref, tall_ref, inner_ref, outer_ref, out_ref, total_ref, lanes_ref, off_chip_ref, tall, wide
 ):
     length, channels = tall_ref.shape
     tiles = length // LANES
     first_core = place_ref[1] == 0
-    tall[:HF] = jnp.where(first_core, outer_ref[...], inner_ref[...])
+    tall[:HF] = jnp.where(first_core, outer_ref[...], inner_ref[...]).T[LANES - HF :]
     tall[HF : HF + length] = tall_ref[...]
-    tall[HF + length :] = jnp.where(first_core, inner_ref[...], outer_ref[...])
+    tall[HF + length :] = jnp.where(first_core, inner_ref[...], outer_ref[...]).T[:HF]
 
     def chunk(i, carry):
         base = pl.multiple_of(i * CHUNK, CHUNK)
@@ -65,29 +65,43 @@
     total = jnp.broadcast_to((earlier + lane_total)[:, LANES - 1 :], (channels, LANES))
     total_ref[...] = total
 
-    def pack(ref, lanes_sum, order):
-        inner = jnp.zeros((channels, LANES), jnp.float32)
-        for r in order:
-            cols = slice(r * LANES, (r + 1) * LANES)
-            inner = inner + jnp.abs(out_ref[:, cols])
-            ref[:, cols] = inner.astype(jnp.bfloat16)
-        rest = lanes_sum
-        for i in range(3):
-            term = rest.astype(jnp.bfloat16)
-            ref[:, length + i * LANES : length + (i + 1) * LANES] = term
-            rest = rest - term.astype(jnp.float32)
-
     later = total - earlier - lane_total
+    lanes_ref[...] = jnp.where(first_core, later, earlier)
 
     @pl.when(first_core)
     def _():
-        pack(off_chip_ref, earlier, range(tiles))
-        pack(on_chip_ref, later, range(tiles - 1, -1, -1))
+        pack(off_chip_ref, out_ref, earlier, range(tiles))
 
     @pl.when(jnp.logical_not(first_core))
     def _():
-        pack(on_chip_ref, earlier, range(tiles))
-        pack(off_chip_ref, later, range(tiles - 1, -1, -1))
+        pack(off_chip_ref, out_ref, later, range(tiles - 1, -1, -1))
+
+
+def pack(ref, filtered_ref, lanes_sum, order):
+    channels, length = filtered_ref.shape
+    inner = jnp.zeros((channels, LANES), jnp.float32)
+    for r in order:
+        cols = slice(r * LANES, (r + 1) * LANES)
+        inner = inner + jnp.abs(filtered_ref[:, cols])
+        ref[:, cols] = inner.astype(jnp.bfloat16)
+    rest = lanes_sum
+    for i in range(ref.shape[1] // LANES - len(order)):
+        term = rest.astype(jnp.bfloat16)
+        ref[:, length + i * LANES : length + (i + 1) * LANES] = term
+        rest = rest - term.astype(jnp.float32)
+
+
+def pack_kernel(place_ref, filtered_ref, lanes_ref, on_chip_ref):
+    tiles = filtered_ref.shape[1] // LANES
+    first_core = place_ref[1] == 0
+
+    @pl.when(first_core)
+    def _():
+        pack(on_chip_ref, filtered_ref, lanes_ref[...], range(tiles - 1, -1, -1))
+
+    @pl.when(jnp.logical_not(first_core))
+    def _():
+        pack(on_chip_ref, filtered_ref, lanes_ref[...], range(tiles))
 
 
 def normalize_kernel(place_ref, filtered_ref, total_ref, on_chip_ref, off_chip_ref, out_ref):
@@ -95,10 +109,9 @@
     tiles = length // LANES
     count = place_ref[3]
     base = total_ref[...]
-    for i in range(3):
-        cols = slice(length + i * LANES, length + (i + 1) * LANES)
-        base = base + on_chip_ref[:, cols].astype(jnp.float32)
-        base = base + off_chip_ref[:, cols].astype(jnp.float32)
+    for ref in (on_chip_ref, off_chip_ref):
+        for start in range(length, ref.shape[1], LANES):
+            base = base + ref[:, start : start + LANES].astype(jnp.float32)
     lane = lax.broadcasted_iota(jnp.int32, (channels, LANES), 1)
     for r in range(tiles):
         cols = slice(r * LANES, (r + 1) * LANES)
@@ -115,7 +128,7 @@
 def normalize(raw, band_index, filter_taps, place):
     channels, length = raw.shape
     first_core = place[1] == 0
-    low, high = raw[:, :HF].T, raw[:, length - HF :].T
+    low, high = raw[:, :LANES], raw[:, length - LANES :]
     inner, outer = to_neighbours(
         jnp.where(first_core, high, low), jnp.where(first_core, low, high)
     )
@@ -126,12 +139,13 @@
     vmem = pl.BlockSpec(memory_space=pltpu.VMEM)
     smem = pl.BlockSpec(memory_space=pltpu.SMEM)
     packed = jax.ShapeDtypeStruct((channels, length + 3 * LANES), jnp.bfloat16)
-    filtered, total, on_chip, off_chip = pl.pallas_call(
+    lanes = jax.ShapeDtypeStruct((channels, LANES), jnp.float32)
+    filtered, total, part, off_chip = pl.pallas_call(
         filter_kernel,
         out_shape=(
             jax.ShapeDtypeStruct((channels, length), jnp.float32),
-            jax.ShapeDtypeStruct((channels, LANES), jnp.float32),
-            packed,
+            lanes,
+            lanes,
             packed,
         ),
         in_specs=[smem] + [vmem] * 4,
@@ -142,7 +156,18 @@
         ],
         compiler_params=pltpu.CompilerParams(vmem_limit_bytes=24 * 1024 * 1024),
         name="filter",
-    )(place, coeff, raw.T, inner, outer)
+    )(place, coeff, lax.optimization_barrier(raw).T, inner, outer)
+    on_chip = pl.pallas_call(
+        pack_kernel,
+        out_shape=jax.ShapeDtypeStruct((channels, length + 2 * LANES), jnp.bfloat16),
+        in_specs=[smem, vmem, vmem],
+        out_specs=vmem,
+        compiler_params=pltpu.CompilerParams(vmem_limit_bytes=24 * 1024 * 1024),
+        cost_estimate=pl.CostEstimate(
+            flops=2 * channels * length, bytes_accessed=16 * channels * length, transcendentals=0
+        ),
+        name="pack",
+    )(place, filtered, part)
     on_chip, off_chip = to_neighbours(on_chip, off_chip)
     return pl.pallas_call(
         normalize_kernel,
@@ -155,8 +180,9 @@
 
 
 def lagged_kernel(
-    count, scale, place_ref, row_hbm, part_hbm, out_hbm, fan, both, carry, acc, row_buf, part_buf, out_buf, row_sem, part_sem, out_sem
+    count, scale, place_ref, row_hbm, part_hbm, out_hbm, fan, both, carry, acc, row_buf, part_buf, row_sem, part_sem, *buffer
 ):
+    out_buf, out_sem = buffer if buffer else (out_hbm.at[0], None)
     rows = row_buf.shape[1]
     channels, length = part_buf.shape[1:]
     tiles = length // LANES
@@ -242,7 +268,7 @@
         out_buf[2 * a] = block[:, :channels].astype(out_buf.dtype)
         if a > 0:
             out_buf[2 * a - 1] = block[:, channels:].astype(out_buf.dtype)
-        if a in (PAIRS // 2, PAIRS - 1):
+        if buffer and a in (PAIRS // 2, PAIRS - 1):
             done = 2 * (PAIRS // 2) + 1 if outs else 0
             span = pl.ds(done, 2 * a + 1 - done)
             outs.append(
@@ -260,11 +286,14 @@
     tiles = length // LANES
     fan_tiles = (2 * -(-LAGH // tiles) + 1) * tiles
     anywhere = pl.BlockSpec(memory_space=pl.ANY)
+    buffer = []
+    if rounds > 1:
+        buffer = [pltpu.VMEM((LAGS, rows, channels), out_dtype), pltpu.SemaphoreType.DMA((2,))]
     return pl.pallas_call(
         functools.partial(lagged_kernel, count, scale),
         out_shape=jax.ShapeDtypeStruct((rounds, LAGS, rows, channels), out_dtype),
         in_specs=[pl.BlockSpec(memory_space=pltpu.SMEM), anywhere, anywhere],
-        out_specs=anywhere,
+        out_specs=anywhere if buffer else pl.BlockSpec(memory_space=pltpu.VMEM),
         scratch_shapes=[
             pltpu.VMEM((rows, fan_tiles * LANES), jnp.bfloat16),
             pltpu.VMEM((2 * channels, length), jnp.bfloat16),
@@ -272,11 +301,10 @@
             pltpu.VMEM((PAIRS * rows, 2 * channels), jnp.float32),
             pltpu.VMEM((count + 2, rows, length), jnp.bfloat16),
             pltpu.VMEM((count, channels, length), jnp.bfloat16),
-            pltpu.VMEM((LAGS, rows, channels), out_dtype),
             pltpu.SemaphoreType.DMA((count,)),
             pltpu.SemaphoreType.DMA((count,)),
-            pltpu.SemaphoreType.DMA((2,)),
-        ],
+        ]
+        + buffer,
         compiler_params=pltpu.CompilerParams(vmem_limit_bytes=VMEM_BYTES),
         cost_estimate=pl.CostEstimate(
             flops=4 * count * PAIRS * rows * channels * length,

time: 124 us -> 122 us (0.984)
  waiting for transfers between devices: 41.7 us -> 39.2 us
    ppermute x2, waiting for transfers between devices: 6.49 us -> 2.13 us  [to_neighbours(): off_chip = lax.ppermute(off_chip, 'ta', outer)]
    unnamed x7 -> x0, local copies, waits for them, and re-layouts: 1.42 us -> none
    optimization_barrier x0 -> x1, local copies, waits for them, and re-layouts: none -> 1.39 us  [normalize(): lax.optimization_barrier(raw)]
  transfers between devices with their start and end apart: 7 -> 7, of which waited for: 5 -> 5; matrix products, arithmetic and copies ran while one was open for 1% -> 3% of each run, Pallas kernels for 8% -> 8%
where the time goes in v6:
time: 122 us
  waiting for transfers between devices  39.2 us (32%)
  starting transfers between devices  23.7 us (19%)
  Pallas kernels  23.5 us (19%)
  blocking collectives  16.9 us (14%)
  between operations  13.5 us (11%)
  other arithmetic  2.61 us (2%)
  local copies, waits for them, and re-layouts  2.29 us (2%)
    ppermute x1, waiting for transfers between devices, on_device(): guest = lax.ppermute(guest, 'cp', swap)  19.4 us
    pallas_call x2, Pallas kernels, lagged(): pl.pallas_call(functools.partial(lagged_kernel, count, scale), out_shape=...  17.8 us
    all_to_all x1, blocking collectives, on_device(): guest = lax.all_to_all(normalized.reshape(count, rows, length), 'ta', 0, 0)  16.9 us
    all_gather x1, waiting for transfers between devices, on_device(): ring = lax.all_gather(normalized, ('zh', 'ta'), axis=0, tiled=False)  10.5 us
    ppermute x2, starting transfers between devices, to_neighbours(): off_chip = lax.ppermute(off_chip, 'ta', outer)  8.94 us
    ppermute x1, starting transfers between devices, on_device(): guest = lax.ppermute(guest, 'cp', swap)  5.64 us
    ppermute x1, waiting for transfers between devices, on_device(): first = lax.ppermute(first, 'cp', swap)  5.3 us
    ppermute x1, starting transfers between devices, on_device(): first = lax.ppermute(first, 'cp', swap)  5.29 us
  transfers between devices with their start and end apart: 7, of which 5 were waited for; matrix products, arithmetic and copies ran while one was open for 3% of the time, Pallas kernels for 8%

profile of v6, /device:TPU:17, one launch (start us, length us, event | category | flops | bytes accessed | tf_op | source)
XLA Modules:
  0.0 121.8 jit_solution(979847003369574058)
XLA Ops:
  6.5 0.9 slice_select_fusion
  7.4 4.6 %collective-permute-start.1 = (f32[128,128]{1,0:T(8,128)S(1)}, f32[128,128]{1,0:T(8,128)S(1)}, u32[]{:S(2)}, u32[]{:S(2)}) collective-permute-start(f32[128,128]{1,0:T(8,128)S(1)} %get-tuple-element.17), channel_id=1, source_target_pairs={{1,2},{2,1},{3,4},{4,3},{5,6},{6,5},{9,10},{10,9},{11,12},{12,11},... | collective-permute-start | bytes 196616 | tf_op jit(solution)/shard_map/ppermute | solution.py:29
  12.0 1.9 %collective-permute-start = (f32[128,128]{1,0:T(8,128)S(1)}, f32[128,128]{1,0:T(8,128)S(1)}, u32[]{:S(2)}, u32[]{:S(2)}) collective-permute-start(f32[128,128]{1,0:T(8,128)S(1)} %get-tuple-element.18), channel_id=1, source_target_pairs={{0,1},{1,0},{2,3},{3,2},{4,5},{5,4},{6,7},{7,6},{8,9},{9,8},{10,11... | collective-permute-start | bytes 196616 | tf_op jit(solution)/shard_map/ppermute | solution.py:30
  13.9 0.7 broadcast_compare_fusion.2
  14.6 0.8 slice_bitcast_fusion.3
  15.4 1.4 %copy.4 = f32[128,1536]{0,1:T(8,128)S(1)} copy(f32[128,1536]{1,0:T(8,128)} %param.3) | data formatting | bytes 1572864 | tf_op jit(solution)/shard_map/optimization_barrier | solution.py:159
  16.8 0.1 select_select_fusion.coeff_ref
  16.9 0.1 pad_add_fusion.1.place_ref
  17.0 3.5 %filter.1 = (f32[128,1536]{1,0:T(8,128)S(1)}, f32[128,128]{1,0:T(8,128)S(1)}, f32[128,128]{1,0:T(8,128)S(1)}, bf16[128,1920]{1,0:T(8,128)(2,1)S(1)}) custom-call(s32[4]{0:T(128)S(1)} %pad_add_fusion.1.place_ref, f32[33,128]{1,0:T(8,128)S(1)} %select_select_fusion.coeff_ref, f32[1536,128]{1,0:T(8,128)S(1)} %bitcast.16, ...), custom_call_target="tpu_custom_call" | custom-call | tf_op jit(solution)/shard_map/filter/pallas_call | solution.py:143
  20.5 4.4 %collective-permute-start.3 = (bf16[128,1920]{1,0:T(8,128)(2,1)S(1)}, bf16[128,1920]{1,0:T(8,128)(2,1)S(1)}, u32[]{:S(2)}, u32[]{:S(2)}) collective-permute-start(bf16[128,1920]{1,0:T(8,128)(2,1)S(1)} %get-tuple-element.14), channel_id=1, source_target_pairs={{1,2},{2,1},{3,4},{4,3},{5,6},{6,5},{9,10},{10,9},{11,12},{12,11},... | collective-permute-start | bytes 1474568 | tf_op jit(solution)/shard_map/ppermute | solution.py:29
  24.9 0.7 pack.1
  25.6 1.9 %collective-permute-start.2 = (bf16[128,1792]{1,0:T(8,128)(2,1)S(1)}, bf16[128,1792]{1,0:T(8,128)(2,1)S(1)}, u32[]{:S(2)}, u32[]{:S(2)}) collective-permute-start(bf16[128,1792]{1,0:T(8,128)(2,1)S(1)} %pack.1), channel_id=1, source_target_pairs={{0,1},{1,0},{2,3},{3,2},{4,5},{5,4},{6,7},{7,6},{8,9},{9,8},{10,11... | collective-permute-start | bytes 1376264 | tf_op jit(solution)/shard_map/ppermute | solution.py:30
  27.5 1.8 %collective-permute-done.2.on_chip_ref = bf16[128,1792]{1,0:T(8,128)(2,1)S(1)} collective-permute-done((bf16[128,1792]{1,0:T(8,128)(2,1)S(1)}, bf16[128,1792]{1,0:T(8,128)(2,1)S(1)}, u32[]{:S(2)}, u32[]{:S(2)}) %collective-permute-start.2) | collective-permute-done | bytes 458784 | tf_op jit(solution)/shard_map/ppermute | solution.py:30
  29.3 2.1 %collective-permute-done.3.off_chip_ref = bf16[128,1920]{1,0:T(8,128)(2,1)S(1)} collective-permute-done((bf16[128,1920]{1,0:T(8,128)(2,1)S(1)}, bf16[128,1920]{1,0:T(8,128)(2,1)S(1)}, u32[]{:S(2)}, u32[]{:S(2)}) %collective-permute-start.3) | collective-permute-done | bytes 491552 | tf_op jit(solution)/shard_map/ppermute | solution.py:29
  31.4 1.6 %normalize.1 = bf16[128,1536]{1,0:T(8,128)(2,1)} custom-call(s32[4]{0:T(128)S(1)} %pad_add_fusion.1.place_ref, f32[128,1536]{1,0:T(8,128)S(1)} %get-tuple-element.11.filtered_ref, f32[128,128]{1,0:T(8,128)S(1)} %get-tuple-element.12.total_ref, bf16[128,1792]{1,0:T(8,128)(2,1)S(1)} %collective-permute-done.2.on_chip_ref, ...), custom_call_target="tpu_custom_call" | custom-call | tf_op jit(solution)/shard_map/normalize/pallas_call | solution.py:172
  33.0 16.9 %all_to_all.5 = bf16[8,16,1536]{2,1,0:T(8,128)(2,1)S(1)} all-to-all(bf16[8,16,1536]{2,1,0:T(8,128)(2,1)} %bitcast.10), channel_id=1, replica_groups=mesh['zh'=2,'cp'=2,'col'=16,'ta'=8] {'ta'}, dimensions={0} | all-to-all | bytes 786432 | tf_op jit(solution)/shard_map/all_to_all | solution.py:330
  49.9 5.6 %collective-permute-start.4 = (bf16[8,16,1536]{2,1,0:T(8,128)(2,1)S(1)}, bf16[8,16,1536]{2,1,0:T(8,128)(2,1)S(1)}, u32[]{:S(2)}, u32[]{:S(2)}) collective-permute-start(bf16[8,16,1536]{2,1,0:T(8,128)(2,1)S(1)} %all_to_all.5), channel_id=1, source_target_pairs={{0,128},{128,0},{1,129},{129,1},{2,130},{130,2},{3,131},{131,3},{4... | collective-permute-start | bytes 1179656 | tf_op jit(solution)/shard_map/ppermute | solution.py:331
  55.7 19.4 %collective-permute-done.4.row_hbm = bf16[8,16,1536]{2,1,0:T(8,128)(2,1)S(1)} collective-permute-done((bf16[8,16,1536]{2,1,0:T(8,128)(2,1)S(1)}, bf16[8,16,1536]{2,1,0:T(8,128)(2,1)S(1)}, u32[]{:S(2)}, u32[]{:S(2)}) %collective-permute-start.4) | collective-permute-done | bytes 393248 | tf_op jit(solution)/shard_map/ppermute | solution.py:331
  75.1 10.5 %all-gather.3.cloned.1.call-done = bf16[2048,1536]{1,0:T(8,128)(2,1)} async-done(((bf16[128,1536]{1,0:T(8,128)(2,1)}), bf16[2048,1536]{1,0:T(8,128)(2,1)}) %all-gather.3.cloned.1.call-update) | async-done | bytes 6291472 | tf_op jit(solution)/shard_map/all_gather | solution.py:329
  85.7 8.6 %lagged.2 = bf16[1,65,16,128]{3,2,1,0:T(8,128)(2,1)S(1)} custom-call(s32[3]{0:T(128)S(1)} %stack.30.place_ref, bf16[8,16,1536]{2,1,0:T(8,128)(2,1)S(1)} %collective-permute-done.4.row_hbm, bf16[16,128,1536]{2,1,0:T(8,128)(2,1)} %bitcast.17), custom_call_target="tpu_custom_call" | custom-call | flops 3321888768 | bytes 3145728 | tf_op jit(solution)/shard_map/lagged/pallas_call | solution.py:292
  94.3 5.3 %collective-permute-start.5 = (bf16[1,65,16,128]{3,2,1,0:T(8,128)(2,1)S(1)}, bf16[1,65,16,128]{3,2,1,0:T(8,128)(2,1)S(1)}, u32[]{:S(2)}, u32[]{:S(2)}) collective-permute-start(bf16[1,65,16,128]{3,2,1,0:T(8,128)(2,1)S(1)} %lagged.2), channel_id=1, source_target_pairs={{0,128},{128,0},{1,129},{129,1},{2,130},{130,2},{3,131},{131,3},{4... | collective-permute-start | bytes 798728 | tf_op jit(solution)/shard_map/ppermute | solution.py:339
  99.6 9.2 %lagged.3 = f32[2,65,16,128]{3,2,1,0:T(8,128)} custom-call(s32[3]{0:T(128)S(1)} %pad_add_fusion.place_ref, bf16[16,128,1536]{2,1,0:T(8,128)(2,1)} %bitcast.18, bf16[16,128,1536]{2,1,0:T(8,128)(2,1)} %bitcast.19), custom_call_target="tpu_custom_call" | custom-call | flops 3321888768 | bytes 3145728 | tf_op jit(solution)/shard_map/lagged/pallas_call | solution.py:292
  108.8 5.3 %collective-permute-done.5 = bf16[1,65,16,128]{3,2,1,0:T(8,128)(2,1)S(1)} collective-permute-done((bf16[1,65,16,128]{3,2,1,0:T(8,128)(2,1)S(1)}, bf16[1,65,16,128]{3,2,1,0:T(8,128)(2,1)S(1)}, u32[]{:S(2)}, u32[]{:S(2)}) %collective-permute-start.5) | collective-permute-done | bytes 266272 | tf_op jit(solution)/shard_map/ppermute | solution.py:339
  114.1 0.8 convert_dynamic-update-slice_fusion
  (6 shorter events, 0.2 us)
Async XLA Ops:
  6.5 79.1 %all-gather.3.cloned.1.call-start = ((), (), s32[]{:S(2)}) async-start(), calls=%async_computation.1 | async-start | bytes 6684672 | tf_op jit(solution)/shard_map/all_gather | solution.py:329
  7.4 9.6 %collective-permute-start.1 = (f32[128,128]{1,0:T(8,128)S(1)}, f32[128,128]{1,0:T(8,128)S(1)}, u32[]{:S(2)}, u32[]{:S(2)}) collective-permute-start(f32[128,128]{1,0:T(8,128)S(1)} %get-tuple-element.17), channel_id=1, source_target_pairs={{1,2},{2,1},{3,4},{4,3},{5,6},{6,5},{9,10},{10,9},{11,12},{12,11},... | collective-permute-start | bytes 196616 | tf_op jit(solution)/shard_map/ppermute | solution.py:29
  12.0 5.0 %collective-permute-start = (f32[128,128]{1,0:T(8,128)S(1)}, f32[128,128]{1,0:T(8,128)S(1)}, u32[]{:S(2)}, u32[]{:S(2)}) collective-permute-start(f32[128,128]{1,0:T(8,128)S(1)} %get-tuple-element.18), channel_id=1, source_target_pairs={{0,1},{1,0},{2,3},{3,2},{4,5},{5,4},{6,7},{7,6},{8,9},{9,8},{10,11... | collective-permute-start | bytes 196616 | tf_op jit(solution)/shard_map/ppermute | solution.py:30
  20.5 10.9 %collective-permute-start.3 = (bf16[128,1920]{1,0:T(8,128)(2,1)S(1)}, bf16[128,1920]{1,0:T(8,128)(2,1)S(1)}, u32[]{:S(2)}, u32[]{:S(2)}) collective-permute-start(bf16[128,1920]{1,0:T(8,128)(2,1)S(1)} %get-tuple-element.14), channel_id=1, source_target_pairs={{1,2},{2,1},{3,4},{4,3},{5,6},{6,5},{9,10},{10,9},{11,12},{12,11},... | collective-permute-start | bytes 1474568 | tf_op jit(solution)/shard_map/ppermute | solution.py:29
  25.6 3.7 %collective-permute-start.2 = (bf16[128,1792]{1,0:T(8,128)(2,1)S(1)}, bf16[128,1792]{1,0:T(8,128)(2,1)S(1)}, u32[]{:S(2)}, u32[]{:S(2)}) collective-permute-start(bf16[128,1792]{1,0:T(8,128)(2,1)S(1)} %pack.1), channel_id=1, source_target_pairs={{0,1},{1,0},{2,3},{3,2},{4,5},{5,4},{6,7},{7,6},{8,9},{9,8},{10,11... | collective-permute-start | bytes 1376264 | tf_op jit(solution)/shard_map/ppermute | solution.py:30
  49.9 25.2 %collective-permute-start.4 = (bf16[8,16,1536]{2,1,0:T(8,128)(2,1)S(1)}, bf16[8,16,1536]{2,1,0:T(8,128)(2,1)S(1)}, u32[]{:S(2)}, u32[]{:S(2)}) collective-permute-start(bf16[8,16,1536]{2,1,0:T(8,128)(2,1)S(1)} %all_to_all.5), channel_id=1, source_target_pairs={{0,128},{128,0},{1,129},{129,1},{2,130},{130,2},{3,131},{131,3},{4... | collective-permute-start | bytes 1179656 | tf_op jit(solution)/shard_map/ppermute | solution.py:331
  94.3 19.8 %collective-permute-start.5 = (bf16[1,65,16,128]{3,2,1,0:T(8,128)(2,1)S(1)}, bf16[1,65,16,128]{3,2,1,0:T(8,128)(2,1)S(1)}, u32[]{:S(2)}, u32[]{:S(2)}) collective-permute-start(bf16[1,65,16,128]{3,2,1,0:T(8,128)(2,1)S(1)} %lagged.2), channel_id=1, source_target_pairs={{0,128},{128,0},{1,129},{129,1},{2,130},{130,2},{3,131},{131,3},{4... | collective-permute-start | bytes 798728 | tf_op jit(solution)/shard_map/ppermute | solution.py:339
Sparse Core Ops, SparseCore 0:
  33.1 52.5 all-gather.2

commit v7 on v6

--- a/solution.py
+++ b/solution.py
@@ -132,10 +132,14 @@
     inner, outer = to_neighbours(
         jnp.where(first_core, high, low), jnp.where(first_core, low, high)
     )
-    band = band_index[None, :]
-    coeff = jnp.broadcast_to(filter_taps[NBANDS - 1][:, None], (TAPS, channels))
-    for i in range(NBANDS - 1):
-        coeff = jnp.where(band == i, filter_taps[i][:, None], coeff)
+    chosen = (jnp.arange(NBANDS, dtype=jnp.int32)[:, None] == band_index[None, :]).astype(jnp.float32)
+    coeff = lax.dot_general(
+        filter_taps,
+        chosen,
+        (((0,), (0,)), ((), ())),
+        precision=lax.Precision.HIGHEST,
+        preferred_element_type=jnp.float32,
+    )
     vmem = pl.BlockSpec(memory_space=pltpu.VMEM)
     smem = pl.BlockSpec(memory_space=pltpu.SMEM)
     packed = jax.ShapeDtypeStruct((channels, length + 3 * LANES), jnp.bfloat16)
@@ -179,60 +183,18 @@
     )(place, filtered, total, on_chip, off_chip)
 
 
-def lagged_kernel(
-    count, scale, place_ref, row_hbm, part_hbm, out_hbm, fan, both, carry, acc, row_buf, part_buf, row_sem, part_sem, *buffer
-):
-    out_buf, out_sem = buffer if buffer else (out_hbm.at[0], None)
-    rows = row_buf.shape[1]
-    channels, length = part_buf.shape[1:]
+def fan_kernel(row_ref, out_ref):
+    count, rows, length = row_ref.shape
     tiles = length // LANES
     reach = -(-LAGH // tiles)
-    lead = reach * tiles + LAGH
-    first_row = pl.multiple_of(place_ref[1] * rows, rows)
-
-    def row_copy(t):
-        return pltpu.make_async_copy(
-            row_hbm.at[place_ref[0] + t, pl.ds(first_row, rows)], row_buf.at[t + 1], row_sem.at[t]
-        )
-
-    def part_copy(t):
-        return pltpu.make_async_copy(
-            part_hbm.at[place_ref[2] + t], part_buf.at[t], part_sem.at[t]
-        )
-
-    for t in range(AHEAD):
-        row_copy(t).start()
-        part_copy(t).start()
-    acc[...] = jnp.zeros_like(acc)
-    carry[...] = jnp.zeros_like(carry)
-    row_buf[0] = jnp.zeros((rows, length), jnp.bfloat16)
-    row_buf[count + 1] = jnp.zeros((rows, length), jnp.bfloat16)
     lane = lax.broadcasted_iota(jnp.int32, (rows, length), 1) % LANES
-    part_lane = lax.broadcasted_iota(jnp.int32, (channels, LANES), 1)
-    row_copy(0).wait()
-
-    def moved(width, offset):
-        return jnp.concatenate(
-            [
-                fan[:, (lead - 2 * a + offset) * LANES : (lead - 2 * a + offset + width) * LANES]
-                for a in range(PAIRS)
-            ],
-            axis=0,
-        )
 
     def body(step, unused):
-        @pl.when(step + AHEAD < count)
-        def _():
-            row_copy(step + AHEAD).start()
-            part_copy(step + AHEAD).start()
-
-        @pl.when(step + 1 < count)
-        def _():
-            row_copy(step + 1).wait()
-
-        inside = row_buf[step + 1].astype(jnp.float32)
-        left = row_buf[step].astype(jnp.float32)
-        right = row_buf[step + 2].astype(jnp.float32)
+        inside = row_ref[step].astype(jnp.float32)
+        left = row_ref[jnp.maximum(step - 1, 0)].astype(jnp.float32)
+        left = jnp.where(step > 0, left, 0.0)
+        right = row_ref[jnp.minimum(step + 1, count - 1)].astype(jnp.float32)
+        right = jnp.where(step < count - 1, right, 0.0)
         for j in range(-reach, reach + 1):
             if j < 0:
                 mixed = jnp.where(lane >= LANES + j, left, inside)
@@ -243,7 +205,72 @@
                 if j != 0:
                     tile = pltpu.roll(tile, (-j) % LANES, 1)
                 at = (j + reach) * tiles + r
-                fan[:, at * LANES : (at + 1) * LANES] = tile.astype(jnp.bfloat16)
+                out_ref[step, :, at * LANES : (at + 1) * LANES] = tile.astype(jnp.bfloat16)
+        return unused
+
+    lax.fori_loop(0, count, body, 0)
+
+
+def fan_of(own_rows):
+    count, rows, length = own_rows.shape
+    tiles = length // LANES
+    fan_tiles = (2 * -(-LAGH // tiles) + 1) * tiles
+    vmem = pl.BlockSpec(memory_space=pltpu.VMEM)
+    return pl.pallas_call(
+        fan_kernel,
+        out_shape=jax.ShapeDtypeStruct((count, rows, fan_tiles * LANES), jnp.bfloat16),
+        in_specs=[vmem],
+        out_specs=vmem,
+        compiler_params=pltpu.CompilerParams(vmem_limit_bytes=24 * 1024 * 1024),
+        cost_estimate=pl.CostEstimate(
+            flops=20 * count * rows * fan_tiles * LANES,
+            bytes_accessed=2 * count * rows * fan_tiles * LANES,
+            transcendentals=0,
+        ),
+        name="fan",
+    )(own_rows)
+
+
+def lagged_kernel(
+    count, scale, place_ref, fan_hbm, part_hbm, out_hbm, fan_buf, both, carry, acc, part_buf, fan_sem, part_sem, *buffer
+):
+    out_buf, out_sem = buffer if buffer else (out_hbm.at[0], None)
+    rows = fan_buf.shape[1]
+    channels, length = part_buf.shape[1:]
+    tiles = length // LANES
+    lead = -(-LAGH // tiles) * tiles + LAGH
+
+    def part_copy(t):
+        return pltpu.make_async_copy(
+            part_hbm.at[place_ref[0] + t], part_buf.at[t], part_sem.at[t]
+        )
+
+    def fan_copy(t):
+        return pltpu.make_async_copy(fan_hbm.at[t], fan_buf.at[t], fan_sem.at[t])
+
+    for t in range(AHEAD):
+        part_copy(t).start()
+        fan_copy(t).start()
+    acc[...] = jnp.zeros_like(acc)
+    carry[...] = jnp.zeros_like(carry)
+    part_lane = lax.broadcasted_iota(jnp.int32, (channels, LANES), 1)
+
+    def moved(step, width, offset):
+        return jnp.concatenate(
+            [
+                fan_buf[
+                    step, :, (lead - 2 * a + offset) * LANES : (lead - 2 * a + offset + width) * LANES
+                ]
+                for a in range(PAIRS)
+            ],
+            axis=0,
+        )
+
+    def body(step, unused):
+        @pl.when(step + AHEAD < count)
+        def _():
+            part_copy(step + AHEAD).start()
+            fan_copy(step + AHEAD).start()
 
         part_copy(step).wait()
         both[:channels] = part_buf[step]
@@ -252,15 +279,22 @@
         late = pltpu.roll(jnp.where(part_lane == LANES - 1, carry[...], final), 1, 1)
         both[channels:, :LANES] = late.astype(jnp.bfloat16)
         carry[...] = final
+        fan_copy(step).wait()
         acc[...] += lax.dot_general(
-            moved(tiles, 0), both[...], (((1,), (1,)), ((), ())), preferred_element_type=jnp.float32
+            moved(step, tiles, 0),
+            both[...],
+            (((1,), (1,)), ((), ())),
+            preferred_element_type=jnp.float32,
         )
         return unused
 
     lax.fori_loop(0, count, body, 0)
     tail = jnp.where(part_lane == LANES - 1, carry[...], 0.0).astype(jnp.bfloat16)
     acc[:, channels:] += lax.dot_general(
-        moved(1, tiles), tail, (((1,), (1,)), ((), ())), preferred_element_type=jnp.float32
+        moved(count - 1, 1, tiles),
+        tail,
+        (((1,), (1,)), ((), ())),
+        preferred_element_type=jnp.float32,
     )
     outs = []
     for a in range(PAIRS):
@@ -281,10 +315,9 @@
         copy.wait()
 
 
-def lagged(place, own_rows, partner, rows, count, scale, out_dtype, rounds):
+def lagged(place, fan, partner, scale, out_dtype, rounds):
+    count, rows = fan.shape[:2]
     channels, length = partner.shape[1:]
-    tiles = length // LANES
-    fan_tiles = (2 * -(-LAGH // tiles) + 1) * tiles
     anywhere = pl.BlockSpec(memory_space=pl.ANY)
     buffer = []
     if rounds > 1:
@@ -292,14 +325,17 @@
     return pl.pallas_call(
         functools.partial(lagged_kernel, count, scale),
         out_shape=jax.ShapeDtypeStruct((rounds, LAGS, rows, channels), out_dtype),
-        in_specs=[pl.BlockSpec(memory_space=pltpu.SMEM), anywhere, anywhere],
+        in_specs=[
+            pl.BlockSpec(memory_space=pltpu.SMEM),
+            anywhere,
+            anywhere,
+        ],
         out_specs=anywhere if buffer else pl.BlockSpec(memory_space=pltpu.VMEM),
         scratch_shapes=[
-            pltpu.VMEM((rows, fan_tiles * LANES), jnp.bfloat16),
+            pltpu.VMEM(fan.shape, jnp.bfloat16),
             pltpu.VMEM((2 * channels, length), jnp.bfloat16),
             pltpu.VMEM((channels, LANES), jnp.float32),
             pltpu.VMEM((PAIRS * rows, 2 * channels), jnp.float32),
-            pltpu.VMEM((count + 2, rows, length), jnp.bfloat16),
             pltpu.VMEM((count, channels, length), jnp.bfloat16),
             pltpu.SemaphoreType.DMA((count,)),
             pltpu.SemaphoreType.DMA((count,)),
@@ -312,7 +348,7 @@
             transcendentals=0,
         ),
         name="lagged",
-    )(place, own_rows, partner)
+    )(place, fan, partner)
 
 
 def on_device(raw_strain, band_index, filter_taps):
@@ -327,17 +363,18 @@
     here = jnp.stack([zero, piece % 2, piece, zero + count]).astype(jnp.int32)
     normalized = normalize(raw_strain, band_index, filter_taps, here)
     ring = lax.all_gather(normalized, ("zh", "ta"), axis=0, tiled=False)
-    guest = lax.all_to_all(normalized.reshape(count, rows, length), "ta", 0, 0)
-    guest = lax.ppermute(guest, "cp", swap)
+    own = lax.all_to_all(normalized.reshape(count, rows, length), "ta", 0, 0)
+    guest = lax.ppermute(own, "cp", swap)
+    guest_fan, own_fan = fan_of(guest), fan_of(own)
 
     other = (1 - half) * count
     near = jnp.where(upper == 1, other, half * count)
-    place0 = jnp.stack([zero, zero, near]).astype(jnp.int32)
-    place1 = jnp.stack([half * count, piece, other]).astype(jnp.int32)
-    first = lagged(place0, guest, ring, rows, count, scale, jnp.bfloat16, 1)
+    place0 = near[None].astype(jnp.int32)
+    place1 = other[None].astype(jnp.int32)
+    first = lagged(place0, guest_fan, ring, scale, jnp.bfloat16, 1)
     place1, first = lax.optimization_barrier((place1, first))
     first = lax.ppermute(first, "cp", swap)
-    result = lagged(place1, ring, ring, rows, count, scale, jnp.float32, ROUNDS)
+    result = lagged(place1, own_fan, ring, scale, jnp.float32, ROUNDS)
     return lax.dynamic_update_slice_in_dim(result, first.astype(jnp.float32), 0, 0)
 
 

time: 122 us -> 120 us (0.984)
  waiting for transfers between devices: 39.2 us -> 34.7 us
  local copies, waits for them, and re-layouts: 2.29 us -> 4.5 us
    unnamed x0 -> x8, local copies, waits for them, and re-layouts: none -> 3.1 us
    all_gather x1, waiting for transfers between devices: 10.5 us -> 7.75 us  [on_device(): ring = lax.all_gather(normalized, ('zh', 'ta'), axis=0, tiled=False)]
    ppermute x1, waiting for transfers between devices: 19.4 us -> 16.7 us  [on_device(): guest = lax.ppermute(own, 'cp', swap)]
    pallas_call x0 -> x2, Pallas kernels: none -> 2.53 us  [fan_of(): pl.pallas_call(fan_kernel, out_shape=jax.ShapeDtypeStruct((count, rows, f...]
    pallas_call x2, Pallas kernels: 17.8 us -> 15.5 us  [lagged(): pl.pallas_call(functools.partial(lagged_kernel, count, scale), out_shape=...]
  transfers between devices with their start and end apart: 7 -> 7, of which waited for: 5 -> 5; matrix products, arithmetic and copies ran while one was open for 3% -> 1% of each run, Pallas kernels for 8% -> 10%
where the time goes in v7:
time: 120 us; the launch traced here: 119 us
  waiting for transfers between devices  34.7 us (29%)
  Pallas kernels  23.8 us (20%)
  starting transfers between devices  23.7 us (20%)
  blocking collectives  16.9 us (14%)
  between operations  13.5 us (11%)
  local copies, waits for them, and re-layouts  4.5 us (4%)
  other arithmetic  1.82 us (2%)
    all_to_all x1, blocking collectives, on_device(): own = lax.all_to_all(normalized.reshape(count, rows, length), 'ta', 0, 0)  16.9 us
    ppermute x1, waiting for transfers between devices, on_device(): guest = lax.ppermute(own, 'cp', swap)  16.7 us
    pallas_call x2, Pallas kernels, lagged(): pl.pallas_call(functools.partial(lagged_kernel, count, scale), out_shape=...  15.5 us
    ppermute x2, starting transfers between devices, to_neighbours(): off_chip = lax.ppermute(off_chip, 'ta', outer)  8.94 us
    all_gather x1, waiting for transfers between devices, on_device(): ring = lax.all_gather(normalized, ('zh', 'ta'), axis=0, tiled=False)  7.75 us
    ppermute x1, waiting for transfers between devices, on_device(): first = lax.ppermute(first, 'cp', swap)  6.33 us
    ppermute x1, starting transfers between devices, on_device(): guest = lax.ppermute(own, 'cp', swap)  5.64 us
    ppermute x1, starting transfers between devices, on_device(): first = lax.ppermute(first, 'cp', swap)  5.3 us
  transfers between devices with their start and end apart: 7, of which 5 were waited for; matrix products, arithmetic and copies ran while one was open for 1% of the time, Pallas kernels for 10%

profile of v7, /device:TPU:17, one launch (start us, length us, event | category | flops | bytes accessed | tf_op | source)
XLA Modules:
  0.0 119.2 jit_solution(8616389867890834662)
XLA Ops:
  6.5 0.9 slice_select_fusion
  7.5 4.6 %collective-permute-start.1 = (f32[128,128]{1,0:T(8,128)S(1)}, f32[128,128]{1,0:T(8,128)S(1)}, u32[]{:S(2)}, u32[]{:S(2)}) collective-permute-start(f32[128,128]{1,0:T(8,128)S(1)} %get-tuple-element.17), channel_id=1, source_target_pairs={{1,2},{2,1},{3,4},{4,3},{5,6},{6,5},{9,10},{10,9},{11,12},{12,11},... | collective-permute-start | bytes 196616 | tf_op jit(solution)/shard_map/ppermute | solution.py:29
  12.0 1.9 %collective-permute-start = (f32[128,128]{1,0:T(8,128)S(1)}, f32[128,128]{1,0:T(8,128)S(1)}, u32[]{:S(2)}, u32[]{:S(2)}) collective-permute-start(f32[128,128]{1,0:T(8,128)S(1)} %get-tuple-element.18), channel_id=1, source_target_pairs={{0,1},{1,0},{2,3},{3,2},{4,5},{5,4},{6,7},{7,6},{8,9},{9,8},{10,11... | collective-permute-start | bytes 196616 | tf_op jit(solution)/shard_map/ppermute | solution.py:30
  13.9 1.4 %copy.4 = f32[128,1536]{0,1:T(8,128)S(1)} copy(f32[128,1536]{1,0:T(8,128)} %param.3) | data formatting | bytes 1572864 | tf_op jit(solution)/shard_map/optimization_barrier | solution.py:163
  15.7 3.5 %filter.1 = (f32[128,1536]{1,0:T(8,128)S(1)}, f32[128,128]{1,0:T(8,128)S(1)}, f32[128,128]{1,0:T(8,128)S(1)}, bf16[128,1920]{1,0:T(8,128)(2,1)S(1)}) custom-call(s32[4]{0:T(128)S(1)} %pad_add_fusion.place_ref, f32[33,128]{1,0:T(8,128)S(1)} %convolution_bitcast_fusion.coeff_ref, f32[1536,128]{1,0:T(8,128)S(1)} %bitcast.10, ...), custom_call_target="tpu_custom_call" | custom-call | tf_op jit(solution)/shard_map/filter/pallas_call | solution.py:147
  19.2 4.4 %collective-permute-start.3 = (bf16[128,1920]{1,0:T(8,128)(2,1)S(1)}, bf16[128,1920]{1,0:T(8,128)(2,1)S(1)}, u32[]{:S(2)}, u32[]{:S(2)}) collective-permute-start(bf16[128,1920]{1,0:T(8,128)(2,1)S(1)} %get-tuple-element.14), channel_id=1, source_target_pairs={{1,2},{2,1},{3,4},{4,3},{5,6},{6,5},{9,10},{10,9},{11,12},{12,11},... | collective-permute-start | bytes 1474568 | tf_op jit(solution)/shard_map/ppermute | solution.py:29
  23.6 0.7 pack.1
  24.3 1.9 %collective-permute-start.2 = (bf16[128,1792]{1,0:T(8,128)(2,1)S(1)}, bf16[128,1792]{1,0:T(8,128)(2,1)S(1)}, u32[]{:S(2)}, u32[]{:S(2)}) collective-permute-start(bf16[128,1792]{1,0:T(8,128)(2,1)S(1)} %pack.1), channel_id=1, source_target_pairs={{0,1},{1,0},{2,3},{3,2},{4,5},{5,4},{6,7},{7,6},{8,9},{9,8},{10,11... | collective-permute-start | bytes 1376264 | tf_op jit(solution)/shard_map/ppermute | solution.py:30
  26.2 1.8 %collective-permute-done.2.on_chip_ref = bf16[128,1792]{1,0:T(8,128)(2,1)S(1)} collective-permute-done((bf16[128,1792]{1,0:T(8,128)(2,1)S(1)}, bf16[128,1792]{1,0:T(8,128)(2,1)S(1)}, u32[]{:S(2)}, u32[]{:S(2)}) %collective-permute-start.2) | collective-permute-done | bytes 458784 | tf_op jit(solution)/shard_map/ppermute | solution.py:30
  28.0 2.1 %collective-permute-done.3.off_chip_ref = bf16[128,1920]{1,0:T(8,128)(2,1)S(1)} collective-permute-done((bf16[128,1920]{1,0:T(8,128)(2,1)S(1)}, bf16[128,1920]{1,0:T(8,128)(2,1)S(1)}, u32[]{:S(2)}, u32[]{:S(2)}) %collective-permute-start.3) | collective-permute-done | bytes 491552 | tf_op jit(solution)/shard_map/ppermute | solution.py:29
  30.1 1.6 %normalize.1 = bf16[128,1536]{1,0:T(8,128)(2,1)} custom-call(s32[4]{0:T(128)S(1)} %pad_add_fusion.place_ref, f32[128,1536]{1,0:T(8,128)S(1)} %get-tuple-element.11.filtered_ref, f32[128,128]{1,0:T(8,128)S(1)} %get-tuple-element.12.total_ref, bf16[128,1792]{1,0:T(8,128)(2,1)S(1)} %collective-permute-done.2.on_chip_ref, ...), custom_call_target="tpu_custom_call" | custom-call | tf_op jit(solution)/shard_map/normalize/pallas_call | solution.py:176
  31.7 16.9 %all_to_all.5.row_ref = bf16[8,16,1536]{2,1,0:T(8,128)(2,1)S(1)} all-to-all(bf16[8,16,1536]{2,1,0:T(8,128)(2,1)} %bitcast.6), channel_id=1, replica_groups=mesh['zh'=2,'cp'=2,'col'=16,'ta'=8] {'ta'}, dimensions={0} | all-to-all | bytes 786432 | tf_op jit(solution)/shard_map/all_to_all | solution.py:366
  48.6 5.6 %collective-permute-start.4 = (bf16[8,16,1536]{2,1,0:T(8,128)(2,1)S(1)}, bf16[8,16,1536]{2,1,0:T(8,128)(2,1)S(1)}, u32[]{:S(2)}, u32[]{:S(2)}) collective-permute-start(bf16[8,16,1536]{2,1,0:T(8,128)(2,1)S(1)} %all_to_all.5.row_ref), channel_id=1, source_target_pairs={{0,128},{128,0},{1,129},{129,1},{2,130},{130,2},{3,131},{131,3},{4... | collective-permute-start | bytes 1179656 | tf_op jit(solution)/shard_map/ppermute | solution.py:367
  54.3 1.3 %fan.3.fan_hbm = bf16[8,16,10752]{2,1,0:T(8,128)(2,1)S(1)} custom-call(bf16[8,16,1536]{2,1,0:T(8,128)(2,1)S(1)} %all_to_all.5.row_ref), custom_call_target="tpu_custom_call" | custom-call | flops 27525120 | bytes 2752512 | tf_op jit(solution)/shard_map/fan/pallas_call | solution.py:219
  55.5 1.6 %copy-done.1 = bf16[8,16,10752]{2,1,0:T(8,128)(2,1)} copy-done((bf16[8,16,10752]{2,1,0:T(8,128)(2,1)}, bf16[8,16,10752]{2,1,0:T(8,128)(2,1)S(1)}, u32[]{:S(2)}) %copy-start.1) | copy-done | bytes 2752536
  57.1 16.7 %collective-permute-done.4.row_ref = bf16[8,16,1536]{2,1,0:T(8,128)(2,1)S(1)} collective-permute-done((bf16[8,16,1536]{2,1,0:T(8,128)(2,1)S(1)}, bf16[8,16,1536]{2,1,0:T(8,128)(2,1)S(1)}, u32[]{:S(2)}, u32[]{:S(2)}) %collective-permute-start.4) | collective-permute-done | bytes 393248 | tf_op jit(solution)/shard_map/ppermute | solution.py:367
  73.8 1.3 %fan.2.fan_hbm = bf16[8,16,10752]{2,1,0:T(8,128)(2,1)S(1)} custom-call(bf16[8,16,1536]{2,1,0:T(8,128)(2,1)S(1)} %collective-permute-done.4.row_ref), custom_call_target="tpu_custom_call" | custom-call | flops 27525120 | bytes 2752512 | tf_op jit(solution)/shard_map/fan/pallas_call | solution.py:219
  75.1 1.5 %copy-done.2 = bf16[8,16,10752]{2,1,0:T(8,128)(2,1)} copy-done((bf16[8,16,10752]{2,1,0:T(8,128)(2,1)}, bf16[8,16,10752]{2,1,0:T(8,128)(2,1)S(1)}, u32[]{:S(2)}) %copy-start.2) | copy-done | bytes 2752536
  76.6 7.7 %all-gather.3.cloned.1.call-done = bf16[2048,1536]{1,0:T(8,128)(2,1)} async-done(((bf16[128,1536]{1,0:T(8,128)(2,1)}), bf16[2048,1536]{1,0:T(8,128)(2,1)}) %all-gather.3.cloned.1.call-update) | async-done | bytes 6291472 | tf_op jit(solution)/shard_map/all_gather | solution.py:365
  84.4 7.4 %lagged.2 = bf16[1,65,16,128]{3,2,1,0:T(8,128)(2,1)S(1)} custom-call(s32[1]{0:T(128)} %bitcast.1.place_ref, bf16[8,16,10752]{2,1,0:T(8,128)(2,1)} %copy-done.2, bf16[16,128,1536]{2,1,0:T(8,128)(2,1)} %bitcast.11), custom_call_target="tpu_custom_call" | custom-call | flops 3321888768 | bytes 3145728 | tf_op jit(solution)/shard_map/lagged/pallas_call | solution.py:325
  91.7 5.3 %collective-permute-start.5 = (bf16[1,65,16,128]{3,2,1,0:T(8,128)(2,1)S(1)}, bf16[1,65,16,128]{3,2,1,0:T(8,128)(2,1)S(1)}, u32[]{:S(2)}, u32[]{:S(2)}) collective-permute-start(bf16[1,65,16,128]{3,2,1,0:T(8,128)(2,1)S(1)} %lagged.2), channel_id=1, source_target_pairs={{0,128},{128,0},{1,129},{129,1},{2,130},{130,2},{3,131},{131,3},{4... | collective-permute-start | bytes 798728 | tf_op jit(solution)/shard_map/ppermute | solution.py:376
  97.1 8.2 %lagged.3 = f32[2,65,16,128]{3,2,1,0:T(8,128)} custom-call(s32[1]{0:T(128)} %bitcast.place_ref, bf16[8,16,10752]{2,1,0:T(8,128)(2,1)} %copy-done.1, bf16[16,128,1536]{2,1,0:T(8,128)(2,1)} %bitcast.12), custom_call_target="tpu_custom_call" | custom-call | flops 3321888768 | bytes 3145728 | tf_op jit(solution)/shard_map/lagged/pallas_call | solution.py:325
  105.2 6.3 %collective-permute-done.5 = bf16[1,65,16,128]{3,2,1,0:T(8,128)(2,1)S(1)} collective-permute-done((bf16[1,65,16,128]{3,2,1,0:T(8,128)(2,1)S(1)}, bf16[1,65,16,128]{3,2,1,0:T(8,128)(2,1)S(1)}, u32[]{:S(2)}, u32[]{:S(2)}) %collective-permute-start.5) | collective-permute-done | bytes 266272 | tf_op jit(solution)/shard_map/ppermute | solution.py:376
  111.6 0.8 convert_dynamic-update-slice_fusion
  (12 shorter events, 0.3 us)
Async XLA Ops:
  6.5 8.8 %copy-start = (f32[4,33]{1,0:T(4,128)S(1)}, f32[4,33]{1,0:T(4,128)}, u32[]{:S(2)}) copy-start(f32[4,33]{1,0:T(4,128)} %param.5) | copy-start | bytes 1588
  6.5 8.8 %copy-start.3 = (s32[128]{0:T(128)S(1)}, s32[128]{0:T(128)}, u32[]{:S(2)}) copy-start(s32[128]{0:T(128)} %param.4) | copy-start | bytes 1540
  6.5 77.8 %all-gather.3.cloned.1.call-start = ((), (), s32[]{:S(2)}) async-start(), calls=%async_computation.1 | async-start | bytes 6684672 | tf_op jit(solution)/shard_map/all_gather | solution.py:365
  7.5 8.2 %collective-permute-start.1 = (f32[128,128]{1,0:T(8,128)S(1)}, f32[128,128]{1,0:T(8,128)S(1)}, u32[]{:S(2)}, u32[]{:S(2)}) collective-permute-start(f32[128,128]{1,0:T(8,128)S(1)} %get-tuple-element.17), channel_id=1, source_target_pairs={{1,2},{2,1},{3,4},{4,3},{5,6},{6,5},{9,10},{10,9},{11,12},{12,11},... | collective-permute-start | bytes 196616 | tf_op jit(solution)/shard_map/ppermute | solution.py:29
  12.0 3.6 %collective-permute-start = (f32[128,128]{1,0:T(8,128)S(1)}, f32[128,128]{1,0:T(8,128)S(1)}, u32[]{:S(2)}, u32[]{:S(2)}) collective-permute-start(f32[128,128]{1,0:T(8,128)S(1)} %get-tuple-element.18), channel_id=1, source_target_pairs={{0,1},{1,0},{2,3},{3,2},{4,5},{5,4},{6,7},{7,6},{8,9},{9,8},{10,11... | collective-permute-start | bytes 196616 | tf_op jit(solution)/shard_map/ppermute | solution.py:30
  19.2 10.9 %collective-permute-start.3 = (bf16[128,1920]{1,0:T(8,128)(2,1)S(1)}, bf16[128,1920]{1,0:T(8,128)(2,1)S(1)}, u32[]{:S(2)}, u32[]{:S(2)}) collective-permute-start(bf16[128,1920]{1,0:T(8,128)(2,1)S(1)} %get-tuple-element.14), channel_id=1, source_target_pairs={{1,2},{2,1},{3,4},{4,3},{5,6},{6,5},{9,10},{10,9},{11,12},{12,11},... | collective-permute-start | bytes 1474568 | tf_op jit(solution)/shard_map/ppermute | solution.py:29
  24.3 3.7 %collective-permute-start.2 = (bf16[128,1792]{1,0:T(8,128)(2,1)S(1)}, bf16[128,1792]{1,0:T(8,128)(2,1)S(1)}, u32[]{:S(2)}, u32[]{:S(2)}) collective-permute-start(bf16[128,1792]{1,0:T(8,128)(2,1)S(1)} %pack.1), channel_id=1, source_target_pairs={{0,1},{1,0},{2,3},{3,2},{4,5},{5,4},{6,7},{7,6},{8,9},{9,8},{10,11... | collective-permute-start | bytes 1376264 | tf_op jit(solution)/shard_map/ppermute | solution.py:30
  48.6 25.2 %collective-permute-start.4 = (bf16[8,16,1536]{2,1,0:T(8,128)(2,1)S(1)}, bf16[8,16,1536]{2,1,0:T(8,128)(2,1)S(1)}, u32[]{:S(2)}, u32[]{:S(2)}) collective-permute-start(bf16[8,16,1536]{2,1,0:T(8,128)(2,1)S(1)} %all_to_all.5.row_ref), channel_id=1, source_target_pairs={{0,128},{128,0},{1,129},{129,1},{2,130},{130,2},{3,131},{131,3},{4... | collective-permute-start | bytes 1179656 | tf_op jit(solution)/shard_map/ppermute | solution.py:367
  55.5 1.6 %copy-start.1 = (bf16[8,16,10752]{2,1,0:T(8,128)(2,1)}, bf16[8,16,10752]{2,1,0:T(8,128)(2,1)S(1)}, u32[]{:S(2)}) copy-start(bf16[8,16,10752]{2,1,0:T(8,128)(2,1)S(1)} %fan.3.fan_hbm) | copy-start | bytes 8257540
  75.1 1.5 %copy-start.2 = (bf16[8,16,10752]{2,1,0:T(8,128)(2,1)}, bf16[8,16,10752]{2,1,0:T(8,128)(2,1)S(1)}, u32[]{:S(2)}) copy-start(bf16[8,16,10752]{2,1,0:T(8,128)(2,1)S(1)} %fan.2.fan_hbm) | copy-start | bytes 8257540
  91.7 19.8 %collective-permute-start.5 = (bf16[1,65,16,128]{3,2,1,0:T(8,128)(2,1)S(1)}, bf16[1,65,16,128]{3,2,1,0:T(8,128)(2,1)S(1)}, u32[]{:S(2)}, u32[]{:S(2)}) collective-permute-start(bf16[1,65,16,128]{3,2,1,0:T(8,128)(2,1)S(1)} %lagged.2), channel_id=1, source_target_pairs={{0,128},{128,0},{1,129},{129,1},{2,130},{130,2},{3,131},{131,3},{4... | collective-permute-start | bytes 798728 | tf_op jit(solution)/shard_map/ppermute | solution.py:376
Sparse Core Ops, SparseCore 0:
  31.8 52.5 all-gather.2

commit v8 on v7

--- a/solution.py
+++ b/solution.py
@@ -104,25 +104,35 @@
         pack(on_chip_ref, filtered_ref, lanes_ref[...], range(tiles))
 
 
-def normalize_kernel(place_ref, filtered_ref, total_ref, on_chip_ref, off_chip_ref, out_ref):
-    channels, length = filtered_ref.shape
+def lane_terms(ref, length):
+    return sum(
+        ref[:, start : start + LANES].astype(jnp.float32)
+        for start in range(length, ref.shape[1], LANES)
+    )
+
+
+def prepare_kernel(place_ref, filtered_ref, total_ref, on_chip_ref, top_ref, bottom_ref):
+    length = filtered_ref.shape[1]
     tiles = length // LANES
-    count = place_ref[3]
-    base = total_ref[...]
-    for ref in (on_chip_ref, off_chip_ref):
-        for start in range(length, ref.shape[1], LANES):
-            base = base + ref[:, start : start + LANES].astype(jnp.float32)
-    lane = lax.broadcasted_iota(jnp.int32, (channels, LANES), 1)
+    base = total_ref[...] + lane_terms(on_chip_ref, length)
+    lane = lax.broadcasted_iota(jnp.int32, (1, LANES), 1)
     for r in range(tiles):
         cols = slice(r * LANES, (r + 1) * LANES)
         time = place_ref[2] * length + tiles * lane + r
-        upper = jnp.minimum(time + length, length * count - 1) + 1
+        upper = jnp.minimum(time + length, length * place_ref[3] - 1) + 1
         lower = jnp.maximum(time - length, 0)
-        window = base + (
-            on_chip_ref[:, cols].astype(jnp.float32) + off_chip_ref[:, cols].astype(jnp.float32)
-        )
-        level = window / (upper - lower).astype(jnp.float32)
-        out_ref[:, cols] = (filtered_ref[:, cols] / (level + 1e-06)).astype(jnp.bfloat16)
+        counted = (upper - lower).astype(jnp.float32)
+        top_ref[:, cols] = filtered_ref[:, cols] * counted
+        bottom_ref[:, cols] = base + on_chip_ref[:, cols].astype(jnp.float32) + 1e-06 * counted
+
+
+def normalize_kernel(top_ref, bottom_ref, off_chip_ref, out_ref):
+    length = top_ref.shape[1]
+    base = lane_terms(off_chip_ref, length)
+    for r in range(length // LANES):
+        cols = slice(r * LANES, (r + 1) * LANES)
+        bottom = bottom_ref[:, cols] + (base + off_chip_ref[:, cols].astype(jnp.float32))
+        out_ref[:, cols] = (top_ref[:, cols] / bottom).astype(jnp.bfloat16)
 
 
 def normalize(raw, band_index, filter_taps, place):
@@ -173,14 +183,26 @@
         name="pack",
     )(place, filtered, part)
     on_chip, off_chip = to_neighbours(on_chip, off_chip)
+    whole = jax.ShapeDtypeStruct((channels, length), jnp.float32)
+    top, bottom = pl.pallas_call(
+        prepare_kernel,
+        out_shape=(whole, whole),
+        in_specs=[smem] + [vmem] * 3,
+        out_specs=(vmem, vmem),
+        compiler_params=pltpu.CompilerParams(vmem_limit_bytes=24 * 1024 * 1024),
+        cost_estimate=pl.CostEstimate(
+            flops=4 * channels * length, bytes_accessed=16 * channels * length, transcendentals=0
+        ),
+        name="prepare",
+    )(place, filtered, total, on_chip)
     return pl.pallas_call(
         normalize_kernel,
         out_shape=jax.ShapeDtypeStruct((channels, length), jnp.bfloat16),
-        in_specs=[smem] + [vmem] * 4,
+        in_specs=[vmem] * 3,
         out_specs=vmem,
         compiler_params=pltpu.CompilerParams(vmem_limit_bytes=24 * 1024 * 1024),
         name="normalize",
-    )(place, filtered, total, on_chip, off_chip)
+    )(top, bottom, off_chip)
 
 
 def fan_kernel(row_ref, out_ref):

time: 120 us -> 119 us (level)
  the two profiles are of different devices: /device:TPU:17 before, /device:TPU:19 now
where the time goes in v8:
time: 119 us
  waiting for transfers between devices  33.9 us (28%)
  Pallas kernels  23.9 us (20%)
  starting transfers between devices  23.7 us (20%)
  blocking collectives  16.9 us (14%)
  between operations  13.6 us (11%)
  local copies, waits for them, and re-layouts  4.48 us (4%)
  other arithmetic  1.82 us (2%)
    all_to_all x1, blocking collectives, on_device(): own = lax.all_to_all(normalized.reshape(count, rows, length), 'ta', 0, 0)  16.9 us
    ppermute x1, waiting for transfers between devices, on_device(): guest = lax.ppermute(own, 'cp', swap)  16.7 us
    pallas_call x2, Pallas kernels, lagged(): pl.pallas_call(functools.partial(lagged_kernel, count, scale), out_shape=...  15.6 us
    ppermute x2, starting transfers between devices, to_neighbours(): off_chip = lax.ppermute(off_chip, 'ta', outer)  8.94 us
    all_gather x1, waiting for transfers between devices, on_device(): ring = lax.all_gather(normalized, ('zh', 'ta'), axis=0, tiled=False)  7.73 us
    ppermute x1, waiting for transfers between devices, on_device(): first = lax.ppermute(first, 'cp', swap)  6.32 us
    ppermute x1, starting transfers between devices, on_device(): guest = lax.ppermute(own, 'cp', swap)  5.64 us
    ppermute x1, starting transfers between devices, on_device(): first = lax.ppermute(first, 'cp', swap)  5.3 us
  transfers between devices with their start and end apart: 7, of which 5 were waited for; matrix products, arithmetic and copies ran while one was open for 1% of the time, Pallas kernels for 10%

profile of v8, /device:TPU:19, one launch (start us, length us, event | category | flops | bytes accessed | tf_op | source)
XLA Modules:
  0.0 118.6 jit_solution(6794313231866576628)
XLA Ops:
  6.5 0.9 slice_select_fusion
  7.5 4.6 %collective-permute-start.1 = (f32[128,128]{1,0:T(8,128)S(1)}, f32[128,128]{1,0:T(8,128)S(1)}, u32[]{:S(2)}, u32[]{:S(2)}) collective-permute-start(f32[128,128]{1,0:T(8,128)S(1)} %get-tuple-element.21), channel_id=1, source_target_pairs={{1,2},{2,1},{3,4},{4,3},{5,6},{6,5},{9,10},{10,9},{11,12},{12,11},... | collective-permute-start | bytes 196616 | tf_op jit(solution)/shard_map/ppermute | solution.py:29
  12.0 1.9 %collective-permute-start = (f32[128,128]{1,0:T(8,128)S(1)}, f32[128,128]{1,0:T(8,128)S(1)}, u32[]{:S(2)}, u32[]{:S(2)}) collective-permute-start(f32[128,128]{1,0:T(8,128)S(1)} %get-tuple-element.22), channel_id=1, source_target_pairs={{0,1},{1,0},{2,3},{3,2},{4,5},{5,4},{6,7},{7,6},{8,9},{9,8},{10,11... | collective-permute-start | bytes 196616 | tf_op jit(solution)/shard_map/ppermute | solution.py:30
  13.9 1.4 %copy.4 = f32[128,1536]{0,1:T(8,128)S(1)} copy(f32[128,1536]{1,0:T(8,128)} %param.3) | data formatting | bytes 1572864 | tf_op jit(solution)/shard_map/optimization_barrier | solution.py:173
  15.7 3.5 %filter.1 = (f32[128,1536]{1,0:T(8,128)S(1)}, f32[128,128]{1,0:T(8,128)S(1)}, f32[128,128]{1,0:T(8,128)S(1)}, bf16[128,1920]{1,0:T(8,128)(2,1)S(1)}) custom-call(s32[4]{0:T(128)S(1)} %pad_add_fusion.place_ref, f32[33,128]{1,0:T(8,128)S(1)} %convolution_bitcast_fusion.coeff_ref, f32[1536,128]{1,0:T(8,128)S(1)} %bitcast.10, ...), custom_call_target="tpu_custom_call" | custom-call | tf_op jit(solution)/shard_map/filter/pallas_call | solution.py:157
  19.2 4.4 %collective-permute-start.3 = (bf16[128,1920]{1,0:T(8,128)(2,1)S(1)}, bf16[128,1920]{1,0:T(8,128)(2,1)S(1)}, u32[]{:S(2)}, u32[]{:S(2)}) collective-permute-start(bf16[128,1920]{1,0:T(8,128)(2,1)S(1)} %get-tuple-element.18), channel_id=1, source_target_pairs={{1,2},{2,1},{3,4},{4,3},{5,6},{6,5},{9,10},{10,9},{11,12},{12,11},... | collective-permute-start | bytes 1474568 | tf_op jit(solution)/shard_map/ppermute | solution.py:29
  24.2 1.9 %collective-permute-start.2 = (bf16[128,1792]{1,0:T(8,128)(2,1)S(1)}, bf16[128,1792]{1,0:T(8,128)(2,1)S(1)}, u32[]{:S(2)}, u32[]{:S(2)}) collective-permute-start(bf16[128,1792]{1,0:T(8,128)(2,1)S(1)} %pack.1), channel_id=1, source_target_pairs={{0,1},{1,0},{2,3},{3,2},{4,5},{5,4},{6,7},{7,6},{8,9},{9,8},{10,11... | collective-permute-start | bytes 1376264 | tf_op jit(solution)/shard_map/ppermute | solution.py:30
  26.2 1.8 %collective-permute-done.2.on_chip_ref = bf16[128,1792]{1,0:T(8,128)(2,1)S(1)} collective-permute-done((bf16[128,1792]{1,0:T(8,128)(2,1)S(1)}, bf16[128,1792]{1,0:T(8,128)(2,1)S(1)}, u32[]{:S(2)}, u32[]{:S(2)}) %collective-permute-start.2) | collective-permute-done | bytes 458784 | tf_op jit(solution)/shard_map/ppermute | solution.py:30
  27.9 0.8 prepare.1
  28.7 1.4 %collective-permute-done.3.off_chip_ref = bf16[128,1920]{1,0:T(8,128)(2,1)S(1)} collective-permute-done((bf16[128,1920]{1,0:T(8,128)(2,1)S(1)}, bf16[128,1920]{1,0:T(8,128)(2,1)S(1)}, u32[]{:S(2)}, u32[]{:S(2)}) %collective-permute-start.3) | collective-permute-done | bytes 491552 | tf_op jit(solution)/shard_map/ppermute | solution.py:29
  30.1 0.9 normalize.1
  31.0 16.9 %all_to_all.5.row_ref = bf16[8,16,1536]{2,1,0:T(8,128)(2,1)S(1)} all-to-all(bf16[8,16,1536]{2,1,0:T(8,128)(2,1)} %bitcast.6), channel_id=1, replica_groups=mesh['zh'=2,'cp'=2,'col'=16,'ta'=8] {'ta'}, dimensions={0} | all-to-all | bytes 786432 | tf_op jit(solution)/shard_map/all_to_all | solution.py:388
  47.9 5.6 %collective-permute-start.4 = (bf16[8,16,1536]{2,1,0:T(8,128)(2,1)S(1)}, bf16[8,16,1536]{2,1,0:T(8,128)(2,1)S(1)}, u32[]{:S(2)}, u32[]{:S(2)}) collective-permute-start(bf16[8,16,1536]{2,1,0:T(8,128)(2,1)S(1)} %all_to_all.5.row_ref), channel_id=1, source_target_pairs={{0,128},{128,0},{1,129},{129,1},{2,130},{130,2},{3,131},{131,3},{4... | collective-permute-start | bytes 1179656 | tf_op jit(solution)/shard_map/ppermute | solution.py:389
  53.6 1.3 %fan.3.fan_hbm = bf16[8,16,10752]{2,1,0:T(8,128)(2,1)S(1)} custom-call(bf16[8,16,1536]{2,1,0:T(8,128)(2,1)S(1)} %all_to_all.5.row_ref), custom_call_target="tpu_custom_call" | custom-call | flops 27525120 | bytes 2752512 | tf_op jit(solution)/shard_map/fan/pallas_call | solution.py:241
  54.9 1.6 %copy-done.1 = bf16[8,16,10752]{2,1,0:T(8,128)(2,1)} copy-done((bf16[8,16,10752]{2,1,0:T(8,128)(2,1)}, bf16[8,16,10752]{2,1,0:T(8,128)(2,1)S(1)}, u32[]{:S(2)}) %copy-start.1) | copy-done | bytes 2752536
  56.4 16.7 %collective-permute-done.4.row_ref = bf16[8,16,1536]{2,1,0:T(8,128)(2,1)S(1)} collective-permute-done((bf16[8,16,1536]{2,1,0:T(8,128)(2,1)S(1)}, bf16[8,16,1536]{2,1,0:T(8,128)(2,1)S(1)}, u32[]{:S(2)}, u32[]{:S(2)}) %collective-permute-start.4) | collective-permute-done | bytes 393248 | tf_op jit(solution)/shard_map/ppermute | solution.py:389
  73.2 1.3 %fan.2.fan_hbm = bf16[8,16,10752]{2,1,0:T(8,128)(2,1)S(1)} custom-call(bf16[8,16,1536]{2,1,0:T(8,128)(2,1)S(1)} %collective-permute-done.4.row_ref), custom_call_target="tpu_custom_call" | custom-call | flops 27525120 | bytes 2752512 | tf_op jit(solution)/shard_map/fan/pallas_call | solution.py:241
  74.4 1.5 %copy-done.2 = bf16[8,16,10752]{2,1,0:T(8,128)(2,1)} copy-done((bf16[8,16,10752]{2,1,0:T(8,128)(2,1)}, bf16[8,16,10752]{2,1,0:T(8,128)(2,1)S(1)}, u32[]{:S(2)}) %copy-start.2) | copy-done | bytes 2752536
  75.9 7.7 %all-gather.3.cloned.1.call-done = bf16[2048,1536]{1,0:T(8,128)(2,1)} async-done(((bf16[128,1536]{1,0:T(8,128)(2,1)}), bf16[2048,1536]{1,0:T(8,128)(2,1)}) %all-gather.3.cloned.1.call-update) | async-done | bytes 6291472 | tf_op jit(solution)/shard_map/all_gather | solution.py:387
  83.7 7.4 %lagged.2 = bf16[1,65,16,128]{3,2,1,0:T(8,128)(2,1)S(1)} custom-call(s32[1]{0:T(128)} %bitcast.1.place_ref, bf16[8,16,10752]{2,1,0:T(8,128)(2,1)} %copy-done.2, bf16[16,128,1536]{2,1,0:T(8,128)(2,1)} %bitcast.11), custom_call_target="tpu_custom_call" | custom-call | flops 3321888768 | bytes 3145728 | tf_op jit(solution)/shard_map/lagged/pallas_call | solution.py:347
  91.1 5.3 %collective-permute-start.5 = (bf16[1,65,16,128]{3,2,1,0:T(8,128)(2,1)S(1)}, bf16[1,65,16,128]{3,2,1,0:T(8,128)(2,1)S(1)}, u32[]{:S(2)}, u32[]{:S(2)}) collective-permute-start(bf16[1,65,16,128]{3,2,1,0:T(8,128)(2,1)S(1)} %lagged.2), channel_id=1, source_target_pairs={{0,128},{128,0},{1,129},{129,1},{2,130},{130,2},{3,131},{131,3},{4... | collective-permute-start | bytes 798728 | tf_op jit(solution)/shard_map/ppermute | solution.py:398
  96.4 8.2 %lagged.3 = f32[2,65,16,128]{3,2,1,0:T(8,128)} custom-call(s32[1]{0:T(128)} %bitcast.place_ref, bf16[8,16,10752]{2,1,0:T(8,128)(2,1)} %copy-done.1, bf16[16,128,1536]{2,1,0:T(8,128)(2,1)} %bitcast.12), custom_call_target="tpu_custom_call" | custom-call | flops 3321888768 | bytes 3145728 | tf_op jit(solution)/shard_map/lagged/pallas_call | solution.py:347
  104.6 6.3 %collective-permute-done.5 = bf16[1,65,16,128]{3,2,1,0:T(8,128)(2,1)S(1)} collective-permute-done((bf16[1,65,16,128]{3,2,1,0:T(8,128)(2,1)S(1)}, bf16[1,65,16,128]{3,2,1,0:T(8,128)(2,1)S(1)}, u32[]{:S(2)}, u32[]{:S(2)}) %collective-permute-start.5) | collective-permute-done | bytes 266272 | tf_op jit(solution)/shard_map/ppermute | solution.py:398
  110.9 0.8 convert_dynamic-update-slice_fusion
  (13 shorter events, 1.0 us)
Async XLA Ops:
  6.5 8.8 %copy-start = (f32[4,33]{1,0:T(4,128)S(1)}, f32[4,33]{1,0:T(4,128)}, u32[]{:S(2)}) copy-start(f32[4,33]{1,0:T(4,128)} %param.5) | copy-start | bytes 1588
  6.5 8.8 %copy-start.3 = (s32[128]{0:T(128)S(1)}, s32[128]{0:T(128)}, u32[]{:S(2)}) copy-start(s32[128]{0:T(128)} %param.4) | copy-start | bytes 1540
  6.5 77.1 %all-gather.3.cloned.1.call-start = ((), (), s32[]{:S(2)}) async-start(), calls=%async_computation.1 | async-start | bytes 6684672 | tf_op jit(solution)/shard_map/all_gather | solution.py:387
  7.5 8.2 %collective-permute-start.1 = (f32[128,128]{1,0:T(8,128)S(1)}, f32[128,128]{1,0:T(8,128)S(1)}, u32[]{:S(2)}, u32[]{:S(2)}) collective-permute-start(f32[128,128]{1,0:T(8,128)S(1)} %get-tuple-element.21), channel_id=1, source_target_pairs={{1,2},{2,1},{3,4},{4,3},{5,6},{6,5},{9,10},{10,9},{11,12},{12,11},... | collective-permute-start | bytes 196616 | tf_op jit(solution)/shard_map/ppermute | solution.py:29
  12.0 3.6 %collective-permute-start = (f32[128,128]{1,0:T(8,128)S(1)}, f32[128,128]{1,0:T(8,128)S(1)}, u32[]{:S(2)}, u32[]{:S(2)}) collective-permute-start(f32[128,128]{1,0:T(8,128)S(1)} %get-tuple-element.22), channel_id=1, source_target_pairs={{0,1},{1,0},{2,3},{3,2},{4,5},{5,4},{6,7},{7,6},{8,9},{9,8},{10,11... | collective-permute-start | bytes 196616 | tf_op jit(solution)/shard_map/ppermute | solution.py:30
  19.2 10.9 %collective-permute-start.3 = (bf16[128,1920]{1,0:T(8,128)(2,1)S(1)}, bf16[128,1920]{1,0:T(8,128)(2,1)S(1)}, u32[]{:S(2)}, u32[]{:S(2)}) collective-permute-start(bf16[128,1920]{1,0:T(8,128)(2,1)S(1)} %get-tuple-element.18), channel_id=1, source_target_pairs={{1,2},{2,1},{3,4},{4,3},{5,6},{6,5},{9,10},{10,9},{11,12},{12,11},... | collective-permute-start | bytes 1474568 | tf_op jit(solution)/shard_map/ppermute | solution.py:29
  24.2 3.7 %collective-permute-start.2 = (bf16[128,1792]{1,0:T(8,128)(2,1)S(1)}, bf16[128,1792]{1,0:T(8,128)(2,1)S(1)}, u32[]{:S(2)}, u32[]{:S(2)}) collective-permute-start(bf16[128,1792]{1,0:T(8,128)(2,1)S(1)} %pack.1), channel_id=1, source_target_pairs={{0,1},{1,0},{2,3},{3,2},{4,5},{5,4},{6,7},{7,6},{8,9},{9,8},{10,11... | collective-permute-start | bytes 1376264 | tf_op jit(solution)/shard_map/ppermute | solution.py:30
  47.9 25.2 %collective-permute-start.4 = (bf16[8,16,1536]{2,1,0:T(8,128)(2,1)S(1)}, bf16[8,16,1536]{2,1,0:T(8,128)(2,1)S(1)}, u32[]{:S(2)}, u32[]{:S(2)}) collective-permute-start(bf16[8,16,1536]{2,1,0:T(8,128)(2,1)S(1)} %all_to_all.5.row_ref), channel_id=1, source_target_pairs={{0,128},{128,0},{1,129},{129,1},{2,130},{130,2},{3,131},{131,3},{4... | collective-permute-start | bytes 1179656 | tf_op jit(solution)/shard_map/ppermute | solution.py:389
  54.9 1.6 %copy-start.1 = (bf16[8,16,10752]{2,1,0:T(8,128)(2,1)}, bf16[8,16,10752]{2,1,0:T(8,128)(2,1)S(1)}, u32[]{:S(2)}) copy-start(bf16[8,16,10752]{2,1,0:T(8,128)(2,1)S(1)} %fan.3.fan_hbm) | copy-start | bytes 8257540
  74.4 1.5 %copy-start.2 = (bf16[8,16,10752]{2,1,0:T(8,128)(2,1)}, bf16[8,16,10752]{2,1,0:T(8,128)(2,1)S(1)}, u32[]{:S(2)}) copy-start(bf16[8,16,10752]{2,1,0:T(8,128)(2,1)S(1)} %fan.2.fan_hbm) | copy-start | bytes 8257540
  91.1 19.8 %collective-permute-start.5 = (bf16[1,65,16,128]{3,2,1,0:T(8,128)(2,1)S(1)}, bf16[1,65,16,128]{3,2,1,0:T(8,128)(2,1)S(1)}, u32[]{:S(2)}, u32[]{:S(2)}) collective-permute-start(bf16[1,65,16,128]{3,2,1,0:T(8,128)(2,1)S(1)} %lagged.2), channel_id=1, source_target_pairs={{0,128},{128,0},{1,129},{129,1},{2,130},{130,2},{3,131},{131,3},{4... | collective-permute-start | bytes 798728 | tf_op jit(solution)/shard_map/ppermute | solution.py:398
Sparse Core Ops, SparseCore 0:
  31.1 52.5 all-gather.2

commit v9 on v8

--- a/solution.py
+++ b/solution.py
@@ -18,7 +18,7 @@
 LANES = 128
 AHEAD = 3
 ROUNDS = 2
-CHUNK = 64
+CHUNK = 192
 VMEM_BYTES = 52 * 1024 * 1024
 
 

time: 119 us -> 119 us (level)
  the two profiles are of different devices: /device:TPU:19 before, /device:TPU:17 now
where the time goes in v9:
time: 119 us; the launch traced here: 118 us
  waiting for transfers between devices  33.9 us (28%)
  starting transfers between devices  23.7 us (20%)
  Pallas kernels  23.5 us (20%)
  blocking collectives  16.9 us (14%)
  between operations  13.6 us (11%)
  local copies, waits for them, and re-layouts  4.48 us (4%)
  other arithmetic  1.82 us (2%)
    all_to_all x1, blocking collectives, on_device(): own = lax.all_to_all(normalized.reshape(count, rows, length), 'ta', 0, 0)  16.9 us
    ppermute x1, waiting for transfers between devices, on_device(): guest = lax.ppermute(own, 'cp', swap)  16.7 us
    pallas_call x2, Pallas kernels, lagged(): pl.pallas_call(functools.partial(lagged_kernel, count, scale), out_shape=...  15.6 us
    ppermute x2, starting transfers between devices, to_neighbours(): off_chip = lax.ppermute(off_chip, 'ta', outer)  8.94 us
    all_gather x1, waiting for transfers between devices, on_device(): ring = lax.all_gather(normalized, ('zh', 'ta'), axis=0, tiled=False)  7.76 us
    ppermute x1, waiting for transfers between devices, on_device(): first = lax.ppermute(first, 'cp', swap)  6.3 us
    ppermute x1, starting transfers between devices, on_device(): guest = lax.ppermute(own, 'cp', swap)  5.64 us
    ppermute x1, starting transfers between devices, on_device(): first = lax.ppermute(first, 'cp', swap)  5.3 us
  transfers between devices with their start and end apart: 7, of which 5 were waited for; matrix products, arithmetic and copies ran while one was open for 1% of the time, Pallas kernels for 10%

profile of v9, /device:TPU:17, one launch (start us, length us, event | category | flops | bytes accessed | tf_op | source)
XLA Modules:
  0.0 118.2 jit_solution(4399928718372616325)
XLA Ops:
  6.5 0.9 slice_select_fusion
  7.5 4.6 %collective-permute-start.1 = (f32[128,128]{1,0:T(8,128)S(1)}, f32[128,128]{1,0:T(8,128)S(1)}, u32[]{:S(2)}, u32[]{:S(2)}) collective-permute-start(f32[128,128]{1,0:T(8,128)S(1)} %get-tuple-element.21), channel_id=1, source_target_pairs={{1,2},{2,1},{3,4},{4,3},{5,6},{6,5},{9,10},{10,9},{11,12},{12,11},... | collective-permute-start | bytes 196616 | tf_op jit(solution)/shard_map/ppermute | solution.py:29
  12.0 1.9 %collective-permute-start = (f32[128,128]{1,0:T(8,128)S(1)}, f32[128,128]{1,0:T(8,128)S(1)}, u32[]{:S(2)}, u32[]{:S(2)}) collective-permute-start(f32[128,128]{1,0:T(8,128)S(1)} %get-tuple-element.22), channel_id=1, source_target_pairs={{0,1},{1,0},{2,3},{3,2},{4,5},{5,4},{6,7},{7,6},{8,9},{9,8},{10,11... | collective-permute-start | bytes 196616 | tf_op jit(solution)/shard_map/ppermute | solution.py:30
  13.9 1.4 %copy.4 = f32[128,1536]{0,1:T(8,128)S(1)} copy(f32[128,1536]{1,0:T(8,128)} %param.3) | data formatting | bytes 1572864 | tf_op jit(solution)/shard_map/optimization_barrier | solution.py:173
  15.7 3.1 %filter.1 = (f32[128,1536]{1,0:T(8,128)S(1)}, f32[128,128]{1,0:T(8,128)S(1)}, f32[128,128]{1,0:T(8,128)S(1)}, bf16[128,1920]{1,0:T(8,128)(2,1)S(1)}) custom-call(s32[4]{0:T(128)S(1)} %pad_add_fusion.place_ref, f32[33,128]{1,0:T(8,128)S(1)} %convolution_bitcast_fusion.coeff_ref, f32[1536,128]{1,0:T(8,128)S(1)} %bitcast.10, ...), custom_call_target="tpu_custom_call" | custom-call | tf_op jit(solution)/shard_map/filter/pallas_call | solution.py:157
  18.8 4.4 %collective-permute-start.3 = (bf16[128,1920]{1,0:T(8,128)(2,1)S(1)}, bf16[128,1920]{1,0:T(8,128)(2,1)S(1)}, u32[]{:S(2)}, u32[]{:S(2)}) collective-permute-start(bf16[128,1920]{1,0:T(8,128)(2,1)S(1)} %get-tuple-element.18), channel_id=1, source_target_pairs={{1,2},{2,1},{3,4},{4,3},{5,6},{6,5},{9,10},{10,9},{11,12},{12,11},... | collective-permute-start | bytes 1474568 | tf_op jit(solution)/shard_map/ppermute | solution.py:29
  23.9 1.9 %collective-permute-start.2 = (bf16[128,1792]{1,0:T(8,128)(2,1)S(1)}, bf16[128,1792]{1,0:T(8,128)(2,1)S(1)}, u32[]{:S(2)}, u32[]{:S(2)}) collective-permute-start(bf16[128,1792]{1,0:T(8,128)(2,1)S(1)} %pack.1), channel_id=1, source_target_pairs={{0,1},{1,0},{2,3},{3,2},{4,5},{5,4},{6,7},{7,6},{8,9},{9,8},{10,11... | collective-permute-start | bytes 1376264 | tf_op jit(solution)/shard_map/ppermute | solution.py:30
  25.8 1.8 %collective-permute-done.2.on_chip_ref = bf16[128,1792]{1,0:T(8,128)(2,1)S(1)} collective-permute-done((bf16[128,1792]{1,0:T(8,128)(2,1)S(1)}, bf16[128,1792]{1,0:T(8,128)(2,1)S(1)}, u32[]{:S(2)}, u32[]{:S(2)}) %collective-permute-start.2) | collective-permute-done | bytes 458784 | tf_op jit(solution)/shard_map/ppermute | solution.py:30
  27.6 0.8 prepare.1
  28.3 1.4 %collective-permute-done.3.off_chip_ref = bf16[128,1920]{1,0:T(8,128)(2,1)S(1)} collective-permute-done((bf16[128,1920]{1,0:T(8,128)(2,1)S(1)}, bf16[128,1920]{1,0:T(8,128)(2,1)S(1)}, u32[]{:S(2)}, u32[]{:S(2)}) %collective-permute-start.3) | collective-permute-done | bytes 491552 | tf_op jit(solution)/shard_map/ppermute | solution.py:29
  29.7 0.9 normalize.1
  30.6 16.9 %all_to_all.5.row_ref = bf16[8,16,1536]{2,1,0:T(8,128)(2,1)S(1)} all-to-all(bf16[8,16,1536]{2,1,0:T(8,128)(2,1)} %bitcast.6), channel_id=1, replica_groups=mesh['zh'=2,'cp'=2,'col'=16,'ta'=8] {'ta'}, dimensions={0} | all-to-all | bytes 786432 | tf_op jit(solution)/shard_map/all_to_all | solution.py:388
  47.5 5.6 %collective-permute-start.4 = (bf16[8,16,1536]{2,1,0:T(8,128)(2,1)S(1)}, bf16[8,16,1536]{2,1,0:T(8,128)(2,1)S(1)}, u32[]{:S(2)}, u32[]{:S(2)}) collective-permute-start(bf16[8,16,1536]{2,1,0:T(8,128)(2,1)S(1)} %all_to_all.5.row_ref), channel_id=1, source_target_pairs={{0,128},{128,0},{1,129},{129,1},{2,130},{130,2},{3,131},{131,3},{4... | collective-permute-start | bytes 1179656 | tf_op jit(solution)/shard_map/ppermute | solution.py:389
  53.2 1.3 %fan.3.fan_hbm = bf16[8,16,10752]{2,1,0:T(8,128)(2,1)S(1)} custom-call(bf16[8,16,1536]{2,1,0:T(8,128)(2,1)S(1)} %all_to_all.5.row_ref), custom_call_target="tpu_custom_call" | custom-call | flops 27525120 | bytes 2752512 | tf_op jit(solution)/shard_map/fan/pallas_call | solution.py:241
  54.5 1.6 %copy-done.1 = bf16[8,16,10752]{2,1,0:T(8,128)(2,1)} copy-done((bf16[8,16,10752]{2,1,0:T(8,128)(2,1)}, bf16[8,16,10752]{2,1,0:T(8,128)(2,1)S(1)}, u32[]{:S(2)}) %copy-start.1) | copy-done | bytes 2752536
  56.1 16.7 %collective-permute-done.4.row_ref = bf16[8,16,1536]{2,1,0:T(8,128)(2,1)S(1)} collective-permute-done((bf16[8,16,1536]{2,1,0:T(8,128)(2,1)S(1)}, bf16[8,16,1536]{2,1,0:T(8,128)(2,1)S(1)}, u32[]{:S(2)}, u32[]{:S(2)}) %collective-permute-start.4) | collective-permute-done | bytes 393248 | tf_op jit(solution)/shard_map/ppermute | solution.py:389
  72.8 1.3 %fan.2.fan_hbm = bf16[8,16,10752]{2,1,0:T(8,128)(2,1)S(1)} custom-call(bf16[8,16,1536]{2,1,0:T(8,128)(2,1)S(1)} %collective-permute-done.4.row_ref), custom_call_target="tpu_custom_call" | custom-call | flops 27525120 | bytes 2752512 | tf_op jit(solution)/shard_map/fan/pallas_call | solution.py:241
  74.1 1.5 %copy-done.2 = bf16[8,16,10752]{2,1,0:T(8,128)(2,1)} copy-done((bf16[8,16,10752]{2,1,0:T(8,128)(2,1)}, bf16[8,16,10752]{2,1,0:T(8,128)(2,1)S(1)}, u32[]{:S(2)}) %copy-start.2) | copy-done | bytes 2752536
  75.6 7.8 %all-gather.3.cloned.1.call-done = bf16[2048,1536]{1,0:T(8,128)(2,1)} async-done(((bf16[128,1536]{1,0:T(8,128)(2,1)}), bf16[2048,1536]{1,0:T(8,128)(2,1)}) %all-gather.3.cloned.1.call-update) | async-done | bytes 6291472 | tf_op jit(solution)/shard_map/all_gather | solution.py:387
  83.3 7.4 %lagged.2 = bf16[1,65,16,128]{3,2,1,0:T(8,128)(2,1)S(1)} custom-call(s32[1]{0:T(128)} %bitcast.1.place_ref, bf16[8,16,10752]{2,1,0:T(8,128)(2,1)} %copy-done.2, bf16[16,128,1536]{2,1,0:T(8,128)(2,1)} %bitcast.11), custom_call_target="tpu_custom_call" | custom-call | flops 3321888768 | bytes 3145728 | tf_op jit(solution)/shard_map/lagged/pallas_call | solution.py:347
  90.7 5.3 %collective-permute-start.5 = (bf16[1,65,16,128]{3,2,1,0:T(8,128)(2,1)S(1)}, bf16[1,65,16,128]{3,2,1,0:T(8,128)(2,1)S(1)}, u32[]{:S(2)}, u32[]{:S(2)}) collective-permute-start(bf16[1,65,16,128]{3,2,1,0:T(8,128)(2,1)S(1)} %lagged.2), channel_id=1, source_target_pairs={{0,128},{128,0},{1,129},{129,1},{2,130},{130,2},{3,131},{131,3},{4... | collective-permute-start | bytes 798728 | tf_op jit(solution)/shard_map/ppermute | solution.py:398
  96.0 8.2 %lagged.3 = f32[2,65,16,128]{3,2,1,0:T(8,128)} custom-call(s32[1]{0:T(128)} %bitcast.place_ref, bf16[8,16,10752]{2,1,0:T(8,128)(2,1)} %copy-done.1, bf16[16,128,1536]{2,1,0:T(8,128)(2,1)} %bitcast.12), custom_call_target="tpu_custom_call" | custom-call | flops 3321888768 | bytes 3145728 | tf_op jit(solution)/shard_map/lagged/pallas_call | solution.py:347
  104.2 6.3 %collective-permute-done.5 = bf16[1,65,16,128]{3,2,1,0:T(8,128)(2,1)S(1)} collective-permute-done((bf16[1,65,16,128]{3,2,1,0:T(8,128)(2,1)S(1)}, bf16[1,65,16,128]{3,2,1,0:T(8,128)(2,1)S(1)}, u32[]{:S(2)}, u32[]{:S(2)}) %collective-permute-start.5) | collective-permute-done | bytes 266272 | tf_op jit(solution)/shard_map/ppermute | solution.py:398
  110.5 0.8 convert_dynamic-update-slice_fusion
  (13 shorter events, 1.0 us)
Async XLA Ops:
  6.5 8.8 %copy-start = (f32[4,33]{1,0:T(4,128)S(1)}, f32[4,33]{1,0:T(4,128)}, u32[]{:S(2)}) copy-start(f32[4,33]{1,0:T(4,128)} %param.5) | copy-start | bytes 1588
  6.5 8.8 %copy-start.3 = (s32[128]{0:T(128)S(1)}, s32[128]{0:T(128)}, u32[]{:S(2)}) copy-start(s32[128]{0:T(128)} %param.4) | copy-start | bytes 1540
  6.5 76.8 %all-gather.3.cloned.1.call-start = ((), (), s32[]{:S(2)}) async-start(), calls=%async_computation.1 | async-start | bytes 6684672 | tf_op jit(solution)/shard_map/all_gather | solution.py:387
  7.5 8.2 %collective-permute-start.1 = (f32[128,128]{1,0:T(8,128)S(1)}, f32[128,128]{1,0:T(8,128)S(1)}, u32[]{:S(2)}, u32[]{:S(2)}) collective-permute-start(f32[128,128]{1,0:T(8,128)S(1)} %get-tuple-element.21), channel_id=1, source_target_pairs={{1,2},{2,1},{3,4},{4,3},{5,6},{6,5},{9,10},{10,9},{11,12},{12,11},... | collective-permute-start | bytes 196616 | tf_op jit(solution)/shard_map/ppermute | solution.py:29
  12.0 3.6 %collective-permute-start = (f32[128,128]{1,0:T(8,128)S(1)}, f32[128,128]{1,0:T(8,128)S(1)}, u32[]{:S(2)}, u32[]{:S(2)}) collective-permute-start(f32[128,128]{1,0:T(8,128)S(1)} %get-tuple-element.22), channel_id=1, source_target_pairs={{0,1},{1,0},{2,3},{3,2},{4,5},{5,4},{6,7},{7,6},{8,9},{9,8},{10,11... | collective-permute-start | bytes 196616 | tf_op jit(solution)/shard_map/ppermute | solution.py:30
  18.8 10.9 %collective-permute-start.3 = (bf16[128,1920]{1,0:T(8,128)(2,1)S(1)}, bf16[128,1920]{1,0:T(8,128)(2,1)S(1)}, u32[]{:S(2)}, u32[]{:S(2)}) collective-permute-start(bf16[128,1920]{1,0:T(8,128)(2,1)S(1)} %get-tuple-element.18), channel_id=1, source_target_pairs={{1,2},{2,1},{3,4},{4,3},{5,6},{6,5},{9,10},{10,9},{11,12},{12,11},... | collective-permute-start | bytes 1474568 | tf_op jit(solution)/shard_map/ppermute | solution.py:29
  23.9 3.7 %collective-permute-start.2 = (bf16[128,1792]{1,0:T(8,128)(2,1)S(1)}, bf16[128,1792]{1,0:T(8,128)(2,1)S(1)}, u32[]{:S(2)}, u32[]{:S(2)}) collective-permute-start(bf16[128,1792]{1,0:T(8,128)(2,1)S(1)} %pack.1), channel_id=1, source_target_pairs={{0,1},{1,0},{2,3},{3,2},{4,5},{5,4},{6,7},{7,6},{8,9},{9,8},{10,11... | collective-permute-start | bytes 1376264 | tf_op jit(solution)/shard_map/ppermute | solution.py:30
  47.5 25.2 %collective-permute-start.4 = (bf16[8,16,1536]{2,1,0:T(8,128)(2,1)S(1)}, bf16[8,16,1536]{2,1,0:T(8,128)(2,1)S(1)}, u32[]{:S(2)}, u32[]{:S(2)}) collective-permute-start(bf16[8,16,1536]{2,1,0:T(8,128)(2,1)S(1)} %all_to_all.5.row_ref), channel_id=1, source_target_pairs={{0,128},{128,0},{1,129},{129,1},{2,130},{130,2},{3,131},{131,3},{4... | collective-permute-start | bytes 1179656 | tf_op jit(solution)/shard_map/ppermute | solution.py:389
  54.5 1.6 %copy-start.1 = (bf16[8,16,10752]{2,1,0:T(8,128)(2,1)}, bf16[8,16,10752]{2,1,0:T(8,128)(2,1)S(1)}, u32[]{:S(2)}) copy-start(bf16[8,16,10752]{2,1,0:T(8,128)(2,1)S(1)} %fan.3.fan_hbm) | copy-start | bytes 8257540
  74.0 1.5 %copy-start.2 = (bf16[8,16,10752]{2,1,0:T(8,128)(2,1)}, bf16[8,16,10752]{2,1,0:T(8,128)(2,1)S(1)}, u32[]{:S(2)}) copy-start(bf16[8,16,10752]{2,1,0:T(8,128)(2,1)S(1)} %fan.2.fan_hbm) | copy-start | bytes 8257540
  90.7 19.8 %collective-permute-start.5 = (bf16[1,65,16,128]{3,2,1,0:T(8,128)(2,1)S(1)}, bf16[1,65,16,128]{3,2,1,0:T(8,128)(2,1)S(1)}, u32[]{:S(2)}, u32[]{:S(2)}) collective-permute-start(bf16[1,65,16,128]{3,2,1,0:T(8,128)(2,1)S(1)} %lagged.2), channel_id=1, source_target_pairs={{0,128},{128,0},{1,129},{129,1},{2,130},{130,2},{3,131},{131,3},{4... | collective-permute-start | bytes 798728 | tf_op jit(solution)/shard_map/ppermute | solution.py:398
Sparse Core Ops, SparseCore 0:
  30.8 52.5 all-gather.2

commit v10 on v9

--- a/solution.py
+++ b/solution.py
@@ -18,7 +18,7 @@
 LANES = 128
 AHEAD = 3
 ROUNDS = 2
-CHUNK = 192
+CHUNK = 384
 VMEM_BYTES = 52 * 1024 * 1024
 
 

time: 119 us -> 119 us (level)
  no operation moved by 1% of the time
where the time goes in v10:
time: 119 us; the launch traced here: 118 us
  waiting for transfers between devices  33.9 us (28%)
  starting transfers between devices  23.7 us (20%)
  Pallas kernels  23.4 us (20%)
  blocking collectives  16.9 us (14%)
  between operations  13.5 us (11%)
  local copies, waits for them, and re-layouts  4.48 us (4%)
  other arithmetic  1.82 us (2%)
    all_to_all x1, blocking collectives, on_device(): own = lax.all_to_all(normalized.reshape(count, rows, length), 'ta', 0, 0)  16.9 us
    ppermute x1, waiting for transfers between devices, on_device(): guest = lax.ppermute(own, 'cp', swap)  16.7 us
    pallas_call x2, Pallas kernels, lagged(): pl.pallas_call(functools.partial(lagged_kernel, count, scale), out_shape=...  15.6 us
    ppermute x2, starting transfers between devices, to_neighbours(): off_chip = lax.ppermute(off_chip, 'ta', outer)  8.94 us
    all_gather x1, waiting for transfers between devices, on_device(): ring = lax.all_gather(normalized, ('zh', 'ta'), axis=0, tiled=False)  7.76 us
    ppermute x1, waiting for transfers between devices, on_device(): first = lax.ppermute(first, 'cp', swap)  6.3 us
    ppermute x1, starting transfers between devices, on_device(): guest = lax.ppermute(own, 'cp', swap)  5.64 us
    ppermute x1, starting transfers between devices, on_device(): first = lax.ppermute(first, 'cp', swap)  5.3 us
  transfers between devices with their start and end apart: 7, of which 5 were waited for; matrix products, arithmetic and copies ran while one was open for 1% of the time, Pallas kernels for 10%

profile of v10, /device:TPU:17, one launch (start us, length us, event | category | flops | bytes accessed | tf_op | source)
XLA Modules:
  0.0 118.1 jit_solution(18241532191448894791)
XLA Ops:
  6.5 0.9 slice_select_fusion
  7.5 4.6 %collective-permute-start.1 = (f32[128,128]{1,0:T(8,128)S(1)}, f32[128,128]{1,0:T(8,128)S(1)}, u32[]{:S(2)}, u32[]{:S(2)}) collective-permute-start(f32[128,128]{1,0:T(8,128)S(1)} %get-tuple-element.21), channel_id=1, source_target_pairs={{1,2},{2,1},{3,4},{4,3},{5,6},{6,5},{9,10},{10,9},{11,12},{12,11},... | collective-permute-start | bytes 196616 | tf_op jit(solution)/shard_map/ppermute | solution.py:29
  12.0 1.9 %collective-permute-start = (f32[128,128]{1,0:T(8,128)S(1)}, f32[128,128]{1,0:T(8,128)S(1)}, u32[]{:S(2)}, u32[]{:S(2)}) collective-permute-start(f32[128,128]{1,0:T(8,128)S(1)} %get-tuple-element.22), channel_id=1, source_target_pairs={{0,1},{1,0},{2,3},{3,2},{4,5},{5,4},{6,7},{7,6},{8,9},{9,8},{10,11... | collective-permute-start | bytes 196616 | tf_op jit(solution)/shard_map/ppermute | solution.py:30
  13.9 1.4 %copy.4 = f32[128,1536]{0,1:T(8,128)S(1)} copy(f32[128,1536]{1,0:T(8,128)} %param.3) | data formatting | bytes 1572864 | tf_op jit(solution)/shard_map/optimization_barrier | solution.py:173
  15.7 3.0 %filter.1 = (f32[128,1536]{1,0:T(8,128)S(1)}, f32[128,128]{1,0:T(8,128)S(1)}, f32[128,128]{1,0:T(8,128)S(1)}, bf16[128,1920]{1,0:T(8,128)(2,1)S(1)}) custom-call(s32[4]{0:T(128)S(1)} %pad_add_fusion.place_ref, f32[33,128]{1,0:T(8,128)S(1)} %convolution_bitcast_fusion.coeff_ref, f32[1536,128]{1,0:T(8,128)S(1)} %bitcast.10, ...), custom_call_target="tpu_custom_call" | custom-call | tf_op jit(solution)/shard_map/filter/pallas_call | solution.py:157
  18.7 4.4 %collective-permute-start.3 = (bf16[128,1920]{1,0:T(8,128)(2,1)S(1)}, bf16[128,1920]{1,0:T(8,128)(2,1)S(1)}, u32[]{:S(2)}, u32[]{:S(2)}) collective-permute-start(bf16[128,1920]{1,0:T(8,128)(2,1)S(1)} %get-tuple-element.18), channel_id=1, source_target_pairs={{1,2},{2,1},{3,4},{4,3},{5,6},{6,5},{9,10},{10,9},{11,12},{12,11},... | collective-permute-start | bytes 1474568 | tf_op jit(solution)/shard_map/ppermute | solution.py:29
  23.8 1.9 %collective-permute-start.2 = (bf16[128,1792]{1,0:T(8,128)(2,1)S(1)}, bf16[128,1792]{1,0:T(8,128)(2,1)S(1)}, u32[]{:S(2)}, u32[]{:S(2)}) collective-permute-start(bf16[128,1792]{1,0:T(8,128)(2,1)S(1)} %pack.1), channel_id=1, source_target_pairs={{0,1},{1,0},{2,3},{3,2},{4,5},{5,4},{6,7},{7,6},{8,9},{9,8},{10,11... | collective-permute-start | bytes 1376264 | tf_op jit(solution)/shard_map/ppermute | solution.py:30
  25.7 1.8 %collective-permute-done.2.on_chip_ref = bf16[128,1792]{1,0:T(8,128)(2,1)S(1)} collective-permute-done((bf16[128,1792]{1,0:T(8,128)(2,1)S(1)}, bf16[128,1792]{1,0:T(8,128)(2,1)S(1)}, u32[]{:S(2)}, u32[]{:S(2)}) %collective-permute-start.2) | collective-permute-done | bytes 458784 | tf_op jit(solution)/shard_map/ppermute | solution.py:30
  27.5 0.8 prepare.1
  28.2 1.4 %collective-permute-done.3.off_chip_ref = bf16[128,1920]{1,0:T(8,128)(2,1)S(1)} collective-permute-done((bf16[128,1920]{1,0:T(8,128)(2,1)S(1)}, bf16[128,1920]{1,0:T(8,128)(2,1)S(1)}, u32[]{:S(2)}, u32[]{:S(2)}) %collective-permute-start.3) | collective-permute-done | bytes 491552 | tf_op jit(solution)/shard_map/ppermute | solution.py:29
  29.6 0.9 normalize.1
  30.5 16.9 %all_to_all.5.row_ref = bf16[8,16,1536]{2,1,0:T(8,128)(2,1)S(1)} all-to-all(bf16[8,16,1536]{2,1,0:T(8,128)(2,1)} %bitcast.6), channel_id=1, replica_groups=mesh['zh'=2,'cp'=2,'col'=16,'ta'=8] {'ta'}, dimensions={0} | all-to-all | bytes 786432 | tf_op jit(solution)/shard_map/all_to_all | solution.py:388
  47.4 5.6 %collective-permute-start.4 = (bf16[8,16,1536]{2,1,0:T(8,128)(2,1)S(1)}, bf16[8,16,1536]{2,1,0:T(8,128)(2,1)S(1)}, u32[]{:S(2)}, u32[]{:S(2)}) collective-permute-start(bf16[8,16,1536]{2,1,0:T(8,128)(2,1)S(1)} %all_to_all.5.row_ref), channel_id=1, source_target_pairs={{0,128},{128,0},{1,129},{129,1},{2,130},{130,2},{3,131},{131,3},{4... | collective-permute-start | bytes 1179656 | tf_op jit(solution)/shard_map/ppermute | solution.py:389
  53.1 1.3 %fan.3.fan_hbm = bf16[8,16,10752]{2,1,0:T(8,128)(2,1)S(1)} custom-call(bf16[8,16,1536]{2,1,0:T(8,128)(2,1)S(1)} %all_to_all.5.row_ref), custom_call_target="tpu_custom_call" | custom-call | flops 27525120 | bytes 2752512 | tf_op jit(solution)/shard_map/fan/pallas_call | solution.py:241
  54.4 1.6 %copy-done.1 = bf16[8,16,10752]{2,1,0:T(8,128)(2,1)} copy-done((bf16[8,16,10752]{2,1,0:T(8,128)(2,1)}, bf16[8,16,10752]{2,1,0:T(8,128)(2,1)S(1)}, u32[]{:S(2)}) %copy-start.1) | copy-done | bytes 2752536
  56.0 16.7 %collective-permute-done.4.row_ref = bf16[8,16,1536]{2,1,0:T(8,128)(2,1)S(1)} collective-permute-done((bf16[8,16,1536]{2,1,0:T(8,128)(2,1)S(1)}, bf16[8,16,1536]{2,1,0:T(8,128)(2,1)S(1)}, u32[]{:S(2)}, u32[]{:S(2)}) %collective-permute-start.4) | collective-permute-done | bytes 393248 | tf_op jit(solution)/shard_map/ppermute | solution.py:389
  72.7 1.3 %fan.2.fan_hbm = bf16[8,16,10752]{2,1,0:T(8,128)(2,1)S(1)} custom-call(bf16[8,16,1536]{2,1,0:T(8,128)(2,1)S(1)} %collective-permute-done.4.row_ref), custom_call_target="tpu_custom_call" | custom-call | flops 27525120 | bytes 2752512 | tf_op jit(solution)/shard_map/fan/pallas_call | solution.py:241
  74.0 1.5 %copy-done.2 = bf16[8,16,10752]{2,1,0:T(8,128)(2,1)} copy-done((bf16[8,16,10752]{2,1,0:T(8,128)(2,1)}, bf16[8,16,10752]{2,1,0:T(8,128)(2,1)S(1)}, u32[]{:S(2)}) %copy-start.2) | copy-done | bytes 2752536
  75.5 7.8 %all-gather.3.cloned.1.call-done = bf16[2048,1536]{1,0:T(8,128)(2,1)} async-done(((bf16[128,1536]{1,0:T(8,128)(2,1)}), bf16[2048,1536]{1,0:T(8,128)(2,1)}) %all-gather.3.cloned.1.call-update) | async-done | bytes 6291472 | tf_op jit(solution)/shard_map/all_gather | solution.py:387
  83.2 7.4 %lagged.2 = bf16[1,65,16,128]{3,2,1,0:T(8,128)(2,1)S(1)} custom-call(s32[1]{0:T(128)} %bitcast.1.place_ref, bf16[8,16,10752]{2,1,0:T(8,128)(2,1)} %copy-done.2, bf16[16,128,1536]{2,1,0:T(8,128)(2,1)} %bitcast.11), custom_call_target="tpu_custom_call" | custom-call | flops 3321888768 | bytes 3145728 | tf_op jit(solution)/shard_map/lagged/pallas_call | solution.py:347
  90.6 5.3 %collective-permute-start.5 = (bf16[1,65,16,128]{3,2,1,0:T(8,128)(2,1)S(1)}, bf16[1,65,16,128]{3,2,1,0:T(8,128)(2,1)S(1)}, u32[]{:S(2)}, u32[]{:S(2)}) collective-permute-start(bf16[1,65,16,128]{3,2,1,0:T(8,128)(2,1)S(1)} %lagged.2), channel_id=1, source_target_pairs={{0,128},{128,0},{1,129},{129,1},{2,130},{130,2},{3,131},{131,3},{4... | collective-permute-start | bytes 798728 | tf_op jit(solution)/shard_map/ppermute | solution.py:398
  95.9 8.2 %lagged.3 = f32[2,65,16,128]{3,2,1,0:T(8,128)} custom-call(s32[1]{0:T(128)} %bitcast.place_ref, bf16[8,16,10752]{2,1,0:T(8,128)(2,1)} %copy-done.1, bf16[16,128,1536]{2,1,0:T(8,128)(2,1)} %bitcast.12), custom_call_target="tpu_custom_call" | custom-call | flops 3321888768 | bytes 3145728 | tf_op jit(solution)/shard_map/lagged/pallas_call | solution.py:347
  104.1 6.3 %collective-permute-done.5 = bf16[1,65,16,128]{3,2,1,0:T(8,128)(2,1)S(1)} collective-permute-done((bf16[1,65,16,128]{3,2,1,0:T(8,128)(2,1)S(1)}, bf16[1,65,16,128]{3,2,1,0:T(8,128)(2,1)S(1)}, u32[]{:S(2)}, u32[]{:S(2)}) %collective-permute-start.5) | collective-permute-done | bytes 266272 | tf_op jit(solution)/shard_map/ppermute | solution.py:398
  110.4 0.8 convert_dynamic-update-slice_fusion
  (13 shorter events, 1.0 us)
Async XLA Ops:
  6.5 8.8 %copy-start = (f32[4,33]{1,0:T(4,128)S(1)}, f32[4,33]{1,0:T(4,128)}, u32[]{:S(2)}) copy-start(f32[4,33]{1,0:T(4,128)} %param.5) | copy-start | bytes 1588
  6.5 8.8 %copy-start.3 = (s32[128]{0:T(128)S(1)}, s32[128]{0:T(128)}, u32[]{:S(2)}) copy-start(s32[128]{0:T(128)} %param.4) | copy-start | bytes 1540
  6.5 76.7 %all-gather.3.cloned.1.call-start = ((), (), s32[]{:S(2)}) async-start(), calls=%async_computation.1 | async-start | bytes 6684672 | tf_op jit(solution)/shard_map/all_gather | solution.py:387
  7.5 8.2 %collective-permute-start.1 = (f32[128,128]{1,0:T(8,128)S(1)}, f32[128,128]{1,0:T(8,128)S(1)}, u32[]{:S(2)}, u32[]{:S(2)}) collective-permute-start(f32[128,128]{1,0:T(8,128)S(1)} %get-tuple-element.21), channel_id=1, source_target_pairs={{1,2},{2,1},{3,4},{4,3},{5,6},{6,5},{9,10},{10,9},{11,12},{12,11},... | collective-permute-start | bytes 196616 | tf_op jit(solution)/shard_map/ppermute | solution.py:29
  12.0 3.6 %collective-permute-start = (f32[128,128]{1,0:T(8,128)S(1)}, f32[128,128]{1,0:T(8,128)S(1)}, u32[]{:S(2)}, u32[]{:S(2)}) collective-permute-start(f32[128,128]{1,0:T(8,128)S(1)} %get-tuple-element.22), channel_id=1, source_target_pairs={{0,1},{1,0},{2,3},{3,2},{4,5},{5,4},{6,7},{7,6},{8,9},{9,8},{10,11... | collective-permute-start | bytes 196616 | tf_op jit(solution)/shard_map/ppermute | solution.py:30
  18.7 10.9 %collective-permute-start.3 = (bf16[128,1920]{1,0:T(8,128)(2,1)S(1)}, bf16[128,1920]{1,0:T(8,128)(2,1)S(1)}, u32[]{:S(2)}, u32[]{:S(2)}) collective-permute-start(bf16[128,1920]{1,0:T(8,128)(2,1)S(1)} %get-tuple-element.18), channel_id=1, source_target_pairs={{1,2},{2,1},{3,4},{4,3},{5,6},{6,5},{9,10},{10,9},{11,12},{12,11},... | collective-permute-start | bytes 1474568 | tf_op jit(solution)/shard_map/ppermute | solution.py:29
  23.8 3.7 %collective-permute-start.2 = (bf16[128,1792]{1,0:T(8,128)(2,1)S(1)}, bf16[128,1792]{1,0:T(8,128)(2,1)S(1)}, u32[]{:S(2)}, u32[]{:S(2)}) collective-permute-start(bf16[128,1792]{1,0:T(8,128)(2,1)S(1)} %pack.1), channel_id=1, source_target_pairs={{0,1},{1,0},{2,3},{3,2},{4,5},{5,4},{6,7},{7,6},{8,9},{9,8},{10,11... | collective-permute-start | bytes 1376264 | tf_op jit(solution)/shard_map/ppermute | solution.py:30
  47.4 25.2 %collective-permute-start.4 = (bf16[8,16,1536]{2,1,0:T(8,128)(2,1)S(1)}, bf16[8,16,1536]{2,1,0:T(8,128)(2,1)S(1)}, u32[]{:S(2)}, u32[]{:S(2)}) collective-permute-start(bf16[8,16,1536]{2,1,0:T(8,128)(2,1)S(1)} %all_to_all.5.row_ref), channel_id=1, source_target_pairs={{0,128},{128,0},{1,129},{129,1},{2,130},{130,2},{3,131},{131,3},{4... | collective-permute-start | bytes 1179656 | tf_op jit(solution)/shard_map/ppermute | solution.py:389
  54.4 1.6 %copy-start.1 = (bf16[8,16,10752]{2,1,0:T(8,128)(2,1)}, bf16[8,16,10752]{2,1,0:T(8,128)(2,1)S(1)}, u32[]{:S(2)}) copy-start(bf16[8,16,10752]{2,1,0:T(8,128)(2,1)S(1)} %fan.3.fan_hbm) | copy-start | bytes 8257540
  73.9 1.5 %copy-start.2 = (bf16[8,16,10752]{2,1,0:T(8,128)(2,1)}, bf16[8,16,10752]{2,1,0:T(8,128)(2,1)S(1)}, u32[]{:S(2)}) copy-start(bf16[8,16,10752]{2,1,0:T(8,128)(2,1)S(1)} %fan.2.fan_hbm) | copy-start | bytes 8257540
  90.6 19.8 %collective-permute-start.5 = (bf16[1,65,16,128]{3,2,1,0:T(8,128)(2,1)S(1)}, bf16[1,65,16,128]{3,2,1,0:T(8,128)(2,1)S(1)}, u32[]{:S(2)}, u32[]{:S(2)}) collective-permute-start(bf16[1,65,16,128]{3,2,1,0:T(8,128)(2,1)S(1)} %lagged.2), channel_id=1, source_target_pairs={{0,128},{128,0},{1,129},{129,1},{2,130},{130,2},{3,131},{131,3},{4... | collective-permute-start | bytes 798728 | tf_op jit(solution)/shard_map/ppermute | solution.py:398
Sparse Core Ops, SparseCore 0:
  30.7 52.5 all-gather.2
